TPU v7x, 128 devices: a whole 4x4x4 slice. The times are simulated.
128 devices in a mesh: lat: 32 (over y, z, core), lev: 4 (over x).
Axes of the slice: x: 4, y: 4, z: 4, core: 2. Of those that a mesh axis runs over, the one named last changes fastest.
Arguments:
- probes: bfloat16 [512, 2, 256, 512], P('lat', None, None, 'lev'), may hold values from -40 to 40
- legendre: bfloat16 [512, 2, 512, 256], P('lat'), may hold values from -0.25 to 0.25
- quad_weight: float32 [512], P('lat'), may hold values from 0.5 to 2
- trunc_counts: int32 [512], P('lat'), may hold values from 128 to 512, as said below
- background: float32 [2, 512, 16, 1024], P(None, 'lat'), may hold values from 0.5 to 1.5
- level_up: float32 [16], replicated, may hold values from 0.2 to 0.5
- level_down: float32 [16], replicated, may hold values from 0.1 to 0.3
- viscosity: float32 [16], replicated, may hold values from 0.5 to 4
Outputs:
- basis_out: bfloat16 [512, 2, 256, 512], P('lat', None, None, 'lev')
- factor: float32 [16, 16], replicated
Inputs may be any that keep to these rules, and one draw needn't show every extreme that they name: `trunc_counts`: wavenumbers kept on a northern latitude and on its mirror; some latitude keeps all 512.
All inputs are finite; a program needn't handle non-finite values.
Results may differ from a plain program's by a relative error of at most 0.017.
Values may be sent and summed in bfloat16 or wider, within the bound.
No kernel may reach another device: no remote copies, remote signals or barrier semaphores. Data moves between devices by JAX's collectives and lax.ppermute only.
A program may use at most 128 MiB of HBM per device.

v0:
```python
import math

import jax
import jax.numpy as jnp
from jax import lax
from jax.sharding import PartitionSpec as P

M = 512
K = 512
PROBES = 16


def make_waves(wave_count, lon_count):
    zonal_ids = lax.broadcasted_iota(jnp.int32, (wave_count, lon_count), 0)
    lon_ids = lax.broadcasted_iota(jnp.int32, (wave_count, lon_count), 1)
    phase = (zonal_ids * lon_ids % lon_count).astype(jnp.float32) * (2.0 * math.pi / lon_count)
    return jnp.stack([jnp.cos(phase), -jnp.sin(phase)], axis=1).astype(jnp.bfloat16)


def damping(wave_first, wave_count, half_degree, visc_cols):
    zonal_ids = wave_first + jnp.arange(wave_count, dtype=jnp.int32)
    degree = (
        zonal_ids[:, None, None]
        + 2 * jnp.arange(half_degree, dtype=jnp.int32)[None, None, :]
        + jnp.arange(2, dtype=jnp.int32)[None, :, None]
    )
    scaled_deg = (degree * (degree + 1)).astype(jnp.float32) / float((M + K) * (M + K + 1))
    damp_one = 1.0 / (1.0 + scaled_deg[..., None] * visc_cols[None, None, None, :])
    return damp_one * damp_one


def unfold(parities):
    even_part = parities[:, 0].astype(jnp.float32)
    odd_part = parities[:, 1].astype(jnp.float32)
    return jnp.stack([even_part + odd_part, even_part - odd_part], axis=1)


def couple(grid_field, outer_coef, inner_coef, level_count, probe_count, reduce_levels):
    wave_count, _, row_count, col_count = grid_field.shape
    shaped = grid_field.reshape(wave_count, 2, row_count, level_count, 2, probe_count)
    level_total = reduce_levels(jnp.sum(shaped * inner_coef[:, None, None], axis=3))
    coupled = shaped + outer_coef[:, None, None] * level_total[:, :, :, None]
    return coupled.reshape(wave_count, 2, row_count, col_count)


def grid_pass(
    grid_field,
    wave_rows,
    gain_grid,
    keep_mask,
    weights,
    outer_coef,
    inner_coef,
    probe_count,
    promote,
    reduce_levels,
    adjoint,
):
    wave_count, _, row_count, col_count = grid_field.shape
    level_count = gain_grid.shape[2]
    if adjoint:
        grid_field = grid_field * weights[None, None, :, None]
    else:
        grid_field = couple(
            grid_field, outer_coef, inner_coef, level_count, probe_count, reduce_levels
        )
        grid_field = grid_field * keep_mask[:, None, :, None]
    operand = promote(grid_field.astype(jnp.bfloat16)).reshape(
        wave_count, 2, row_count, level_count, 2, probe_count
    )
    points = jnp.einsum(
        "mhjlcs,mci->hjlsi", operand, promote(wave_rows), preferred_element_type=jnp.float32
    )
    points = promote((points * gain_grid[:, :, :, None, :]).astype(jnp.bfloat16))
    analysed = jnp.einsum(
        "hjlsi,mci->mhjlcs", points, promote(wave_rows), preferred_element_type=jnp.float32
    )
    analysed = analysed.reshape(wave_count, 2, row_count, col_count)
    if adjoint:
        analysed = analysed * keep_mask[:, None, :, None]
        analysed = couple(analysed, outer_coef, inner_coef, level_count, probe_count, reduce_levels)
    else:
        analysed = analysed * weights[None, None, :, None]
    return jnp.stack(
        [analysed[:, 0] + analysed[:, 1], analysed[:, 0] - analysed[:, 1]], axis=1
    ).astype(jnp.bfloat16)


def to_parities(legendre, spectral):
    return jnp.einsum(
        "mpjq,mpqc->mpjc", legendre, spectral, preferred_element_type=jnp.float32
    ).astype(jnp.bfloat16)


def to_spectral(legendre, folded):
    return jnp.einsum("mpjq,mpjc->mpqc", legendre, folded, preferred_element_type=jnp.float32)


def same_values(values):
    return values


def level_sum(partial_value):
    return lax.psum(partial_value.astype(jnp.bfloat16), "lev").astype(jnp.float32)


def to_rows(parities):
    arrived = lax.all_to_all(parities, "lat", split_axis=2, concat_axis=0, tiled=True)
    return arrived


def to_waves(folded):
    arrived = lax.all_to_all(folded, "lat", split_axis=0, concat_axis=2, tiled=True)
    return arrived


def shards(
    probes, legendre, quad_weight, trunc_counts, background, level_up, level_down, viscosity
):
    lat_count = lax.axis_size("lat")
    lev_count = lax.axis_size("lev")
    lat_index = lax.axis_index("lat")
    lev_index = lax.axis_index("lev")
    wave_local = probes.shape[0]
    level_local = probes.shape[3] // (2 * PROBES)
    wave_count = wave_local * lat_count
    lon_count = 2 * wave_count
    wave_rows = make_waves(wave_count, lon_count)
    weights = quad_weight
    gain_grid = lax.dynamic_slice_in_dim(background, lev_index * level_local, level_local, 2)
    up_coef = lax.dynamic_slice_in_dim(level_up, lev_index * level_local, level_local, 0)
    down_coef = lax.dynamic_slice_in_dim(level_down, lev_index * level_local, level_local, 0)
    zonal_ids = jnp.arange(wave_count, dtype=jnp.int32)
    doubling = jnp.where(zonal_ids == 0, 1.0, 2.0).astype(jnp.float32)
    keep_mask = (zonal_ids[:, None] < trunc_counts[None, :]).astype(jnp.float32) * doubling[:, None]
    weights = weights / float(lon_count)
    grid_field = unfold(to_rows(to_parities(legendre, probes)))
    folded = grid_pass(
        grid_field,
        wave_rows,
        gain_grid,
        keep_mask,
        weights,
        up_coef,
        down_coef,
        PROBES,
        same_values,
        level_sum,
        False,
    )
    tangent = to_spectral(legendre, to_waves(folded))
    visc_cols = jnp.repeat(
        lax.dynamic_slice_in_dim(viscosity, lev_index * level_local, level_local, 0), 2 * PROBES
    )
    damping_sq = damping(lat_index * wave_local, wave_local, probes.shape[2], visc_cols)
    damped = (tangent * damping_sq).astype(jnp.bfloat16)
    grid_field = unfold(to_rows(to_parities(legendre, damped)))
    folded = grid_pass(
        grid_field,
        wave_rows,
        gain_grid,
        keep_mask,
        weights,
        down_coef,
        up_coef,
        PROBES,
        same_values,
        level_sum,
        True,
    )
    images = to_spectral(legendre, to_waves(folded))
    flattened = images.reshape(-1, PROBES)
    gram_local = lax.dot_general(
        flattened, flattened, (((0,), (0,)), ((), ())), precision=lax.Precision.HIGHEST
    )
    gram_matrix = lax.psum(gram_local, ("lat", "lev"))
    lower_factor = jnp.linalg.cholesky(gram_matrix)
    inverse = lax.linalg.triangular_solve(
        lower_factor, jnp.eye(PROBES, dtype=jnp.float32), left_side=True, lower=True
    )
    row_scale = math.sqrt(flattened.shape[0] * lat_count * lev_count)
    basis_out = (row_scale * jnp.dot(flattened, inverse.T, precision=lax.Precision.HIGHEST)).astype(
        jnp.bfloat16
    )
    basis_out = basis_out.reshape(images.shape)
    factor = lower_factor.T / row_scale
    return (basis_out, factor)


def solution(mesh):
    placed = (
        P("lat", None, None, "lev"),
        P("lat", None, None, None),
        P("lat"),
        P("lat"),
        P(None, "lat", None, None),
        P(),
        P(),
        P(),
    )
    return jax.shard_map(
        shards,
        mesh=mesh,
        in_specs=placed,
        out_specs=(P("lat", None, None, "lev"), P()),
        check_vma=False,
    )
```

profile of v0, /device:TPU:1, one launch (start us, length us, event | category | flops | bytes accessed | tf_op | source)
XLA Modules:
  0.0 726.1 jit_solution(6764757870753245017)
XLA Ops:
  7.2 1.6 copy-done
  8.8 5.7 convolution_convert_fusion
  14.5 6.3 copy.88
  20.8 9.8 %all-to-all-start = ((bf16[16,2,512,128]{3,1,0,2:T(2,128)(2,1)}), bf16[16,2,512,128]{3,1,0,2:T(2,128)(2,1)}, u32[]{:S(2)}, u32[]{:S(2)}) async-start(bf16[16,2,512,128]{3,1,0,2:T(2,128)(2,1)} %copy.88), calls=%async_computation | async-start | bytes 8388608 | tf_op jit(solution)/shard_map/all_to_all | solution.py:108
  30.6 0.3 all-reduce.3.cloned.1.call-start
  30.9 0.1 dynamic_slice.13
  31.0 51.7 %all-to-all-done = bf16[16,2,512,128]{3,1,0,2:T(2,128)(2,1)} async-done(((bf16[16,2,512,128]{3,1,0,2:T(2,128)(2,1)}), bf16[16,2,512,128]{3,1,0,2:T(2,128)(2,1)}, u32[]{:S(2)}, u32[]{:S(2)}) %all-to-all-start) | async-done | bytes 4194336 | tf_op jit(solution)/shard_map/all_to_all | solution.py:108
  82.7 3.8 copy.89
  86.5 1.2 copy.90
  87.7 3.8 convert_add_fusion.1
  91.5 5.3 copy.91
  96.8 5.3 copy.92
  102.1 5.5 multiply_reduce_fusion
  107.6 0.1 dynamic_slice.12
  107.7 2.1 constant_dynamic-slice_fusion
  109.9 9.7 %negate_convert_fusion = (bf16[512,1,1024]{2,0,1:T(8,128)(2,1)S(1)}, bf16[512,1,1024]{2,0,1:T(8,128)(2,1)}) fusion(), kind=kLoop, calls=%fused_computation.52 | loop fusion | flops 8912896 | bytes 2097152 | tf_op jit(solution)/shard_map/convert.5
  119.6 33.0 %all-reduce.3.cloned.1.call-done = bf16[512,2,16,2,16]{0,4,2,1,3:T(8,128)(2,1)} async-done(((bf16[512,2,16,2,16]{0,4,2,1,3:T(8,128)(2,1)}), bf16[512,2,16,2,16]{0,4,2,1,3:T(8,128)(2,1)}) %all-reduce.3.cloned.1.call-update) | async-done | bytes 1048592 | tf_op jit(solution)/shard_map/psum | solution.py:104
  152.6 1.5 convert_element_type.94
  154.1 8.5 %fusion.14 = f32[2,16,4,16,1024,1]{4,3,0,2,1,5:T(8,128)S(1)} fusion(bf16[512,1,1024]{2,0,1:T(8,128)(2,1)S(1)} %get-tuple-element.24, bf16[512,1,1024]{2,0,1:T(8,128)(2,1)} %get-tuple-element.25, f32[512,16]{0,1:T(8,128)S(1)} %fusion.34, f32[512,2,16,2,16]{0,4,2,1,3:T(8,128)S(1)} %convert_element_type.94, f32[4]{0:T(128)S(1)} %dynamic_slice.12, ...), kind=kOutput, calls=%fused_computation.28 | convolution fusion | flops 4306501632 | bytes 21004304 | tf_op jit(solution)/shard_map/mhjlcs,mci->hjlsi/dot_general | solution.py:71
  162.6 4.6 fusion.19
  167.2 1.9 copy.95
  169.1 2.4 bitcast_multiply_fusion.2
  171.5 1.5 add_convert_fusion.1
  173.0 2.3 pad_maximum_fusion.1
  175.3 7.9 %copy.96 = bf16[512,2,16,128]{3,2,1,0:T(8,128)(2,1)} copy(bf16[512,2,16,128]{0,3,2,1:T(8,128)(2,1)} %pad_maximum_fusion.1) | data formatting | bytes 8388608 | tf_op jit(solution)/shard_map/stack | solution.py:84
  183.3 9.7 %all-to-all-start.1 = ((bf16[512,2,16,128]{3,2,1,0:T(8,128)(2,1)}), bf16[512,2,16,128]{3,2,1,0:T(8,128)(2,1)}, u32[]{:S(2)}, u32[]{:S(2)}) async-start(bf16[512,2,16,128]{3,2,1,0:T(8,128)(2,1)} %copy.96), calls=%async_computation.1 | async-start | bytes 8388608 | tf_op jit(solution)/shard_map/all_to_all | solution.py:113
  193.0 0.1 dynamic_slice.15
  193.1 0.1 mul.211
  193.2 0.1 broadcast_add_fusion
  193.4 51.7 %all-to-all-done.1 = bf16[512,2,16,128]{3,2,1,0:T(8,128)(2,1)} async-done(((bf16[512,2,16,128]{3,2,1,0:T(8,128)(2,1)}), bf16[512,2,16,128]{3,2,1,0:T(8,128)(2,1)}, u32[]{:S(2)}, u32[]{:S(2)}) %all-to-all-start.1) | async-done | bytes 4194336 | tf_op jit(solution)/shard_map/all_to_all | solution.py:113
  245.1 5.3 copy.97
  250.4 13.1 %convert_bitcast_fusion = bf16[16,2,512,128]{2,3,1,0:T(8,128)(2,1)} fusion(bf16[16,2,512,256]{3,2,1,0:T(8,128)(2,1)} %param.9, bf16[16,2,512,128]{3,2,1,0:T(8,128)(2,1)} %bitcast.131, f32[128]{0:T(128)S(1)} %mul.211, f32[16,2,256]{2,1,0:T(2,128)S(1)} %fusion.33), kind=kOutput, calls=%fused_computation.33 | convolution fusion | flops 2155872256 | bytes 16810496 | tf_op jit(solution)/shard_map/mpjq,mpqc->mpjc/dot_general | solution.py:90
  263.5 11.2 %copy.99 = bf16[16,2,512,128]{3,1,0,2:T(2,128)(2,1)} copy(bf16[16,2,512,128]{2,3,1,0:T(8,128)(2,1)} %convert_bitcast_fusion) | data formatting | bytes 8388608 | tf_op jit(solution)/shard_map/convert_element_type | solution.py:92
  274.7 57.9 %all_to_all.72 = bf16[16,2,512,128]{3,1,0,2:T(2,128)(2,1)S(1)} all-to-all(bf16[16,2,512,128]{3,1,0,2:T(2,128)(2,1)} %copy.99), channel_id=1, replica_groups=mesh['lat'=32,'lev'=4] {'lat'}, dimensions={2} | all-to-all | bytes 8388608 | tf_op jit(solution)/shard_map/all_to_all | solution.py:108
  332.6 1.6 copy.100
  334.3 1.2 copy.101
  335.4 3.8 convert_add_fusion
  339.2 5.2 copy.102
  344.4 5.4 copy.103
  349.8 14.8 %fusion.2 = (bf16[512,2,16,2,16]{0,4,2,1,3:T(8,128)(2,1)}, f32[512,2,2,16,4,16]{0,5,4,3,2,1:T(8,128)}) fusion(f32[512,16]{0,1:T(8,128)S(1)} %fusion.34, f32[4]{0:T(128)S(1)} %dynamic_slice.12, f32[2,16,4,1024]{3,2,1,0:T(4,128)S(1)} %copy-done.5, bf16[512,1,1024]{2,0,1:T(8,128)(2,1)S(1)} %get-tuple-element.24, bf16[512,1,1024]{2,0,1:T(8,128)(2,1)S(1)} %copy-done.3, ...), kind=kOutput, calls=%fused_computation.7 | convolution fusion | flops 8611430400 | bytes 20480080 | tf_op jit(solution)/shard_map/hjlsi,mci->mhjlcs/dot_general | solution.py:75
  364.6 41.5 %all-reduce.5.cloned.1.call-done = bf16[512,2,16,2,16]{0,4,2,1,3:T(8,128)(2,1)} async-done(((bf16[512,2,16,2,16]{0,4,2,1,3:T(8,128)(2,1)}), bf16[512,2,16,2,16]{0,4,2,1,3:T(8,128)(2,1)}) %all-reduce.5.cloned.1.call-update) | async-done | bytes 1048592 | tf_op jit(solution)/shard_map/psum | solution.py:104
  406.1 1.5 convert_element_type.106
  407.6 5.2 bitcast_add_fusion
  412.9 4.2 copy.104
  417.1 4.8 add_convert_fusion
  421.9 2.3 pad_maximum_fusion.2
  424.2 7.9 %copy.105 = bf16[512,2,16,128]{3,2,1,0:T(8,128)(2,1)} copy(bf16[512,2,16,128]{0,3,2,1:T(8,128)(2,1)} %pad_maximum_fusion.2) | data formatting | bytes 8388608 | tf_op jit(solution)/shard_map/stack | solution.py:84
  432.1 60.4 %all_to_all.73 = bf16[512,2,16,128]{3,2,1,0:T(8,128)(2,1)S(1)} all-to-all(bf16[512,2,16,128]{3,2,1,0:T(8,128)(2,1)} %copy.105), channel_id=1, replica_groups=mesh['lat'=32,'lev'=4] {'lat'}, dimensions={0} | all-to-all | bytes 8388608 | tf_op jit(solution)/shard_map/all_to_all | solution.py:113
  492.5 1.2 copy.106
  493.7 1.0 slice-done.1
  494.7 3.5 convolution_bitcast_fusion
  498.2 5.4 copy.108
  503.6 19.6 %reshape.201 = f32[65536,16]{1,0:T(8,128)} reshape(f32[16,2,256,128]{3,2,1,0:T(8,128)} %copy.108) | data formatting | bytes 8388608 | tf_op jit(solution)/shard_map/reshape | solution.py:172
  523.2 64.4 %fusion.53 = f32[16,16]{0,1:T(8,128)S(1)} fusion(f32[65536,16]{1,0:T(8,128)} %reshape.201), kind=kOutput, calls=%fused_computation.82 | convolution fusion | flops 201326592 | bytes 4195328 | tf_op jit(solution)/shard_map/dot_general | solution.py:173
  587.5 63.6 %psum.23 = f32[16,16]{0,1:T(8,128)S(1)} all-reduce(f32[16,16]{0,1:T(8,128)S(1)} %fusion.53), channel_id=1, replica_groups=mesh['lat'=32,'lev'=4] {'lat','lev'}, use_global_device_ids=true, to_apply=%region_4.5 | all-reduce | flops 256 | bytes 2048 | tf_op jit(solution)/shard_map/psum | solution.py:176
  651.3 1.5 cholesky.17
  652.7 0.6 compare_reduce_fusion
  653.4 0.7 multiply_bitcast_fusion
  654.0 0.7 copy.112
  654.7 1.2 custom-call.6
  655.9 0.2 fusion.35
  656.1 32.9 %fusion = bf16[65536,16]{0,1:T(8,128)(2,1)S(1)} fusion(f32[65536,16]{1,0:T(8,128)} %reshape.201, f32[16,16]{1,0:T(8,128)S(1)} %fusion.35), kind=kOutput, calls=%fused_computation.1 | convolution fusion | flops 203423744 | bytes 6292480 | tf_op jit(solution)/shard_map/dot_general | solution.py:182
  689.0 11.1 %copy.111 = bf16[65536,16]{1,0:T(8,128)(2,1)} copy(bf16[65536,16]{0,1:T(8,128)(2,1)S(1)} %fusion) | data formatting | bytes 4194304 | tf_op jit(solution)/shard_map/convert_element_type | solution.py:182
  700.1 18.9 %reshape.202 = bf16[16,2,256,128]{3,2,1,0:T(8,128)(2,1)} reshape(bf16[65536,16]{1,0:T(8,128)(2,1)} %copy.111) | data formatting | bytes 4194304 | tf_op jit(solution)/shard_map/reshape | solution.py:185
  (38 shorter events, 0.4 us)
Async XLA Ops:
  7.2 1.6 copy-start
  20.8 10.1 %copy-start.7 = (f32[16]{0:T(128)S(1)}, f32[16]{0:T(128)}, u32[]{:S(2)}) copy-start(f32[16]{0:T(128)} %param.14) | copy-start | bytes 196
  20.8 61.9 %all-to-all-start = ((bf16[16,2,512,128]{3,1,0,2:T(2,128)(2,1)}), bf16[16,2,512,128]{3,1,0,2:T(2,128)(2,1)}, u32[]{:S(2)}, u32[]{:S(2)}) async-start(bf16[16,2,512,128]{3,1,0,2:T(2,128)(2,1)} %copy.88), calls=%async_computation | async-start | bytes 8388608 | tf_op jit(solution)/shard_map/all_to_all | solution.py:108
  30.6 122.0 %all-reduce.3.cloned.1.call-start = ((), (), s32[]{:S(2)}) async-start(), calls=%async_computation.4 | async-start | bytes 2097152 | tf_op jit(solution)/shard_map/psum | solution.py:104
  102.1 5.5 copy-start.8
  102.1 7.7 %copy-start.9 = (f32[16]{0:T(128)S(1)}, f32[16]{0:T(128)}, u32[]{:S(2)}) copy-start(f32[16]{0:T(128)} %param.10) | copy-start | bytes 196
  102.1 7.8 %copy-start.6 = (s32[16]{0:T(128)S(1)}, s32[16]{0:T(128)}, u32[]{:S(2)}) copy-start(s32[16]{0:T(128)} %param.11) | copy-start | bytes 196
  154.1 8.5 %copy-start.2 = (bf16[512,1,1024]{2,0,1:T(8,128)(2,1)S(1)}, bf16[512,1,1024]{2,0,1:T(8,128)(2,1)}, u32[]{:S(2)}) copy-start(bf16[512,1,1024]{2,0,1:T(8,128)(2,1)} %get-tuple-element.25) | copy-start | bytes 3145732
  154.1 8.5 %copy-start.4 = (f32[2,16,4,1024]{3,2,1,0:T(4,128)S(1)}, f32[2,16,4,1024]{3,2,1,0:T(4,128)}, u32[]{:S(2)}) copy-start(f32[2,16,4,1024]{3,2,1,0:T(4,128)} %constant_dynamic-slice_fusion) | copy-start | bytes 1572868
  183.3 9.7 %copy-start.10 = (f32[16]{0:T(128)S(1)}, f32[16]{0:T(128)}, u32[]{:S(2)}) copy-start(f32[16]{0:T(128)} %param.15) | copy-start | bytes 196
  183.3 61.8 %all-to-all-start.1 = ((bf16[512,2,16,128]{3,2,1,0:T(8,128)(2,1)}), bf16[512,2,16,128]{3,2,1,0:T(8,128)(2,1)}, u32[]{:S(2)}, u32[]{:S(2)}) async-start(bf16[512,2,16,128]{3,2,1,0:T(8,128)(2,1)} %copy.96), calls=%async_computation.1 | async-start | bytes 8388608 | tf_op jit(solution)/shard_map/all_to_all | solution.py:113
  192.9 213.2 %all-reduce.5.cloned.1.call-start = ((), (), s32[]{:S(2)}) async-start(), calls=%async_computation.5 | async-start | bytes 2097152 | tf_op jit(solution)/shard_map/psum | solution.py:104
  344.4 5.4 copy-start.3
  344.4 5.4 copy-start.5
  432.1 61.6 %slice-start = ((s8[8388608]{0:T(1024)(128)(4,1)}), s8[4194304]{0:T(1024)(128)(4,1)S(1)}, s32[]{:S(2)}) async-start(s8[8388608]{0:T(1024)(128)(4,1)} %bitcast.116), calls=%async_computation.6 | async-start | bytes 8388608
  492.5 2.2 slice-start.1
  700.1 18.9 %copy-start.1 = (bf16[16,2,256,128]{3,2,1,0:T(8,128)(2,1)S(1)}, bf16[16,2,256,128]{3,2,1,0:T(8,128)(2,1)}, u32[]{:S(2)}) copy-start(bf16[16,2,256,128]{3,2,1,0:T(8,128)(2,1)} %param.8) | copy-start | bytes 6291460
Sparse Core Ops, SparseCore 0:
  107.7 44.8 all-reduce.2
  364.8 41.2 all-reduce.4
where the time goes:
time: 734 us; the launch traced here: 726 us
  blocking collectives  182 us (25%)
  waiting for transfers between devices  178 us (24%)
  matrix products  148 us (20%)
  local copies, waits for them, and re-layouts  136 us (19%)
  other arithmetic  48.5 us (7%)
  starting transfers between devices  19.8 us (3%)
  between operations  14.5 us (2%)
    psum x2, waiting for transfers between devices, level_sum(): lax.psum(partial_value.astype(jnp.bfloat16), 'lev').astype(jnp.float32)  74.4 us
    dot_general x1, matrix products, shards(): lax.dot_general(flattened, flattened, (((0,), (0,)), ((), ())), precision...  64.4 us
    psum x1, blocking collectives, shards(): gram_matrix = lax.psum(gram_local, ('lat', 'lev'))  63.6 us
    all_to_all x1, blocking collectives, to_waves(): lax.all_to_all(folded, 'lat', split_axis=0, concat_axis=2, tiled=True)  60.4 us
    all_to_all x1, blocking collectives, to_rows(): lax.all_to_all(parities, 'lat', split_axis=2, concat_axis=0, tiled=True)  57.9 us
    all_to_all x1, waiting for transfers between devices, to_waves(): lax.all_to_all(folded, 'lat', split_axis=0, concat_axis=2, tiled=True)  51.7 us
    all_to_all x1, waiting for transfers between devices, to_rows(): lax.all_to_all(parities, 'lat', split_axis=2, concat_axis=0, tiled=True)  51.7 us
    dot_general x1, matrix products, shards(): jnp.dot(flattened, inverse.T, precision=lax.Precision.HIGHEST)  32.9 us
  transfers between devices with their start and end apart: 4, of which 4 were waited for; matrix products, arithmetic and copies ran while one was open for 2% of the time, Pallas kernels for 0%

commit v1 on v0

v1 whole, which is shorter than its diff:
```python
import functools
import math

import jax
import jax.numpy as jnp
import ml_dtypes
import numpy as np
from jax import lax
from jax.experimental import pallas as pl
from jax.experimental.pallas import tpu as pltpu
from jax.sharding import PartitionSpec as P


M = 512
K = 512
PROBES = 16
LANES = 128
F32 = jnp.float32
BF16 = jnp.bfloat16


def params(mib):
    return pltpu.CompilerParams(vmem_limit_bytes=mib << 20)


def in_hbm(values):
    return pltpu.with_memory_space_constraint(values, pltpu.HBM)


def hbm_result(shape, dtype):
    return pltpu.HBM(shape, dtype)


def wave_tables(wave_count):
    lon = np.arange(wave_count)[:, None]
    tables = []
    for parity in range(2):
        zonal = np.arange(parity, wave_count, 2)[None, :]
        phase = (zonal * lon % (2 * wave_count)) * (math.pi / wave_count)
        tables.append(np.concatenate([np.cos(phase), -np.sin(phase)], axis=1))
    return np.stack(tables).astype(np.float32).astype(ml_dtypes.bfloat16)


def spread_table():
    rows = np.arange(8)[:, None]
    lanes = np.arange(LANES)[None, :] // PROBES
    return (rows == lanes).astype(ml_dtypes.bfloat16)


def lane_ids(rows, lanes=LANES):
    return lax.broadcasted_iota(jnp.int32, (rows, lanes), 1)


def row_ids(rows, lanes=LANES):
    return lax.broadcasted_iota(jnp.int32, (rows, lanes), 0)


def halves(values):
    high = values.astype(BF16)
    return high, (values - high.astype(F32)).astype(BF16)


def slot(wave):
    return (wave & 1) * 8 + (wave >> 1)


def own_levels(coef_ref, lev_ref, level):
    first = lev_ref[0] * 4
    coef = jnp.where(level == 0, coef_ref[first], coef_ref[first + 1])
    return jnp.where(
        level < 2, coef, jnp.where(level == 2, coef_ref[first + 2], coef_ref[first + 3])
    )


def sum_matrix(coef_ref, lev_ref):
    rows = row_ids(LANES)
    weights = jnp.where(
        (rows & 31) == (lane_ids(LANES) & 31), own_levels(coef_ref, lev_ref, rows // 32), 0.0
    )
    return jnp.concatenate(halves(weights), axis=0)


def unpack_matrix(coef_ref, lev_ref):
    rows = row_ids(LANES, 4 * LANES)
    lanes = lane_ids(LANES, 4 * LANES)
    level = (lanes & (LANES - 1)) // 32
    hit = (rows // 32 == lanes // LANES) & ((rows & 31) == (lanes & 31))
    weights = jnp.where(hit, own_levels(coef_ref, lev_ref, level), 0.0)
    return jnp.concatenate(halves(weights), axis=0)


def twice(values):
    return jnp.concatenate([values, values], axis=1)


def pack_levels(summed):
    rows = summed.shape[0] // 4
    group = lane_ids(rows) // 32
    low = jnp.where(group == 0, summed[0:rows], summed[rows : 2 * rows])
    high = jnp.where(group == 2, summed[2 * rows : 3 * rows], summed[3 * rows :])
    return jnp.where(group < 2, low, high)


def unpack_levels(packed, matrix):
    wide = jnp.dot(twice(packed), matrix, preferred_element_type=F32)
    return jnp.concatenate([wide[:, g * LANES : (g + 1) * LANES] for g in range(4)], axis=0)


def add_totals(refs, m):
    parts = [ref[m].astype(F32) for ref in refs]
    return ((parts[0] + parts[1]) + (parts[2] + parts[3])).astype(BF16)


def smem_spec():
    return pl.BlockSpec(memory_space=pltpu.SMEM)


def whole_spec(shape):
    return pl.BlockSpec(shape, lambda g: (0,) * len(shape))


def partial_kernel(coef_ref, lev_ref, probes_ref, out_ref):
    matrix = sum_matrix(coef_ref, lev_ref)
    for m in range(probes_ref.shape[0]):
        summed = jnp.dot(twice(probes_ref[m, 0]), matrix, preferred_element_type=F32)
        out_ref[m] = pack_levels(summed).astype(BF16)


def level_partial(probes, coef, lev, parity):
    waves, _, degrees, _ = probes.shape
    steps = 2
    return pl.pallas_call(
        partial_kernel,
        grid=(steps,),
        in_specs=[
            smem_spec(),
            smem_spec(),
            pl.BlockSpec((waves // steps, 1, degrees, LANES), lambda g: (g, parity, 0, 0)),
        ],
        out_specs=pl.BlockSpec((waves // steps, degrees // 4, LANES), lambda g: (g, 0, 0)),
        out_shape=jax.ShapeDtypeStruct((waves, degrees // 4, LANES), BF16),
        compiler_params=params(8),
        name="level_partial",
    )(coef, lev, in_hbm(probes))


def legendre_kernel(coef_ref, lev_ref, probes_ref, *refs):
    totals = refs[:4]
    table_ref, out_ref, mixed, turned = refs[4:]
    waves = probes_ref.shape[0]
    rows = table_ref.shape[2]

    @pl.when(pl.program_id(0) == 0)
    def _():
        matrix = unpack_matrix(coef_ref, lev_ref)

        def mix(m, carry):
            total = add_totals(totals, m)
            mixed[m] = (probes_ref[m, 0].astype(F32) + unpack_levels(total, matrix)).astype(BF16)
            return carry

        lax.fori_loop(0, waves, mix, 0, unroll=4)

    def transform(m, carry):
        turned[pl.ds(slot(m), rows, stride=waves), :] = jnp.dot(
            table_ref[m, 0], mixed[m], preferred_element_type=F32
        )
        return carry

    lax.fori_loop(0, waves, transform, 0, unroll=4)
    out_ref[...] = turned[...].astype(BF16).reshape(out_ref.shape)


def legendre_forward(probes, totals, legendre, coef, lev, parity):
    waves, _, degrees, _ = probes.shape
    lats = legendre.shape[2]
    blocks = lats // waves
    steps = 4
    total_spec = whole_spec(totals[0].shape)
    return pl.pallas_call(
        legendre_kernel,
        grid=(steps,),
        in_specs=[
            smem_spec(),
            smem_spec(),
            pl.BlockSpec((waves, 1, degrees, LANES), lambda g: (0, parity, 0, 0)),
        ]
        + [total_spec] * 4
        + [pl.BlockSpec((waves, 1, lats // steps, degrees), lambda g: (0, parity, g, 0))],
        out_specs=pl.BlockSpec((blocks // steps, waves, waves, LANES), lambda g: (g, 0, 0, 0)),
        out_shape=hbm_result((blocks, waves, waves, LANES), BF16),
        scratch_shapes=[
            pltpu.VMEM((waves, degrees, LANES), BF16),
            pltpu.VMEM((lats // steps * waves, LANES), F32),
        ],
        compiler_params=params(14),
        name="legendre_forward",
    )(coef, lev, in_hbm(probes), *totals, in_hbm(legendre))


HALF = M // 2


def mask_rows(count, parity):
    zonal = 2 * row_ids(HALF) + parity
    factor = jnp.where(zonal == 0, 1.0, 2.0)
    return jnp.where(zonal < count, factor, 0.0).astype(F32)


def load_waves(counts_ref, x_ref, operand, masked):
    step = pl.program_id(0)
    real_lane = (lane_ids(HALF) & PROBES) == 0
    for pair in range(2):
        both = [x_ref[:, 2 * pair + k].astype(F32) for k in range(2)]
        lanes = slice(pair * LANES, (pair + 1) * LANES)
        for parity in range(2):
            first, second = [
                x[:, 8 * parity : 8 * parity + 8].reshape(HALF, LANES) for x in both
            ]
            if masked:
                first = first * mask_rows(counts_ref[4 * step + 2 * pair], parity)
                second = second * mask_rows(counts_ref[4 * step + 2 * pair + 1], parity)
            operand[parity, :HALF, lanes] = jnp.where(
                real_lane, first, pltpu.roll(second, PROBES, 1)
            ).astype(BF16)
            operand[parity, HALF:, lanes] = jnp.where(
                real_lane, pltpu.roll(first, LANES - PROBES, 1), second
            ).astype(BF16)


def store_waves(counts_ref, fields, table_ref, out_ref, masked):
    step = pl.program_id(0)
    real_lane = (lane_ids(HALF) & PROBES) == 0
    results = {}
    for parity in range(2):
        cos_part = jnp.dot(table_ref[parity, :HALF], fields[parity], preferred_element_type=F32)
        sin_part = jnp.dot(table_ref[parity, HALF:], fields[parity], preferred_element_type=F32)
        for pair in range(2):
            cosine = cos_part[:, pair * LANES : (pair + 1) * LANES]
            sine = sin_part[:, pair * LANES : (pair + 1) * LANES]
            first = jnp.where(real_lane, cosine, pltpu.roll(sine, PROBES, 1))
            second = jnp.where(real_lane, pltpu.roll(cosine, LANES - PROBES, 1), sine)
            if masked:
                first = first * mask_rows(counts_ref[4 * step + 2 * pair], parity)
                second = second * mask_rows(counts_ref[4 * step + 2 * pair + 1], parity)
            results[2 * pair, parity] = first.reshape(-1, 8, LANES)
            results[2 * pair + 1, parity] = second.reshape(-1, 8, LANES)
    for k in range(4):
        out_ref[:, k] = jnp.concatenate([results[k, 0], results[k, 1]], axis=1).astype(BF16)


def grid_even_kernel(counts_ref, x_ref, table_ref, out_ref, operand, *, masked):
    load_waves(counts_ref, x_ref, operand, masked)
    even = jnp.dot(table_ref[0], operand[0], preferred_element_type=F32)
    odd = jnp.dot(table_ref[1], operand[1], preferred_element_type=F32)
    out_ref[0, 0] = even + odd
    out_ref[0, 1] = even - odd


def grid_middle_kernel(
    counts_ref, x_ref, even_ref, gain_ref, forward_ref, inverse_ref, out_ref, odd_ref,
    operand, fields, *, masked_in, masked_out,
):
    load_waves(counts_ref, x_ref, operand, masked_in)
    size = 256
    for r in range(0, M, size):
        rows = slice(r, r + size)
        even = jnp.dot(forward_ref[0, rows], operand[0], preferred_element_type=F32)
        odd = jnp.dot(forward_ref[1, rows], operand[1], preferred_element_type=F32)
        for pair in range(2):
            lanes = slice(pair * LANES, (pair + 1) * LANES)
            kept = []
            for half, sent in enumerate((even[:, lanes] + odd[:, lanes], even[:, lanes] - odd[:, lanes])):
                base = even_ref[0, half, rows, lanes]
                longitudes = slice(half * M + r, half * M + r + size)
                north = gain_ref[0, pair, longitudes].astype(F32) * (base + sent)
                south = gain_ref[1, pair, longitudes].astype(F32) * (base - sent)
                kept.append((north + south, north - south))
            fields[0, rows, lanes] = (kept[0][0] + kept[1][0]).astype(BF16)
            fields[1, rows, lanes] = (kept[0][0] - kept[1][0]).astype(BF16)
            odd_ref[0, 0, rows, lanes] = (kept[0][1] + kept[1][1]).astype(BF16)
            odd_ref[0, 1, rows, lanes] = (kept[0][1] - kept[1][1]).astype(BF16)
    store_waves(counts_ref, fields, inverse_ref, out_ref, masked_out)


def grid_odd_kernel(counts_ref, odd_ref, table_ref, out_ref, *, masked):
    store_waves(counts_ref, odd_ref[0], table_ref, out_ref, masked)


def gain_kernel(gain_ref, spread_ref, out_ref):
    for h in range(2):
        out_ref[h, 0] = lax.dot_general(
            gain_ref[h, 0], spread_ref[...], (((0,), (0,)), ((), ())), preferred_element_type=F32
        ).astype(BF16)


def spread_gain(gain):
    pairs = gain.shape[1]
    return pl.pallas_call(
        gain_kernel,
        grid=(pairs,),
        in_specs=[
            pl.BlockSpec((2, 1, 8, 2 * M), lambda g: (0, g, 0, 0)),
            whole_spec((8, LANES)),
        ],
        out_specs=pl.BlockSpec((2, 1, 2 * M, LANES), lambda g: (0, g, 0, 0)),
        out_shape=hbm_result((2, pairs, 2 * M, LANES), BF16),
        compiler_params=params(8),
        name="spread_gain",
    )(gain, jnp.asarray(spread_table()))


def wave_block(x):
    return pl.BlockSpec((x.shape[0], 4, x.shape[2], LANES), lambda g: (0, g, 0, 0))


def grid_pass(arrive, depart, counts, gain, tables, masked_in, masked_out):
    forward, inverse = tables
    x_even = arrive(0)
    steps = x_even.shape[1] // 4
    field_spec = pl.BlockSpec((1, 2, M, 2 * LANES), lambda g: (g, 0, 0, 0))
    field_shape = (steps, 2, M, 2 * LANES)
    operand = pltpu.VMEM((2, M, 2 * LANES), BF16)
    even = pl.pallas_call(
        functools.partial(grid_even_kernel, masked=masked_in),
        grid=(steps,),
        in_specs=[smem_spec(), wave_block(x_even), whole_spec(forward.shape)],
        out_specs=field_spec,
        out_shape=hbm_result(field_shape, F32),
        scratch_shapes=[operand],
        compiler_params=params(16),
        name="grid_even",
    )(counts, in_hbm(x_even), in_hbm(forward))
    x_odd = arrive(1)
    out_shape = hbm_result(x_odd.shape, BF16)
    y_even, odd = pl.pallas_call(
        functools.partial(grid_middle_kernel, masked_in=masked_in, masked_out=masked_out),
        grid=(steps,),
        in_specs=[
            smem_spec(),
            wave_block(x_odd),
            field_spec,
            pl.BlockSpec((2, 2, 2 * M, LANES), lambda g: (0, g, 0, 0)),
            whole_spec(forward.shape),
            whole_spec(inverse.shape),
        ],
        out_specs=(wave_block(x_odd), field_spec),
        out_shape=(out_shape, hbm_result(field_shape, BF16)),
        scratch_shapes=[operand, operand],
        compiler_params=params(24),
        name="grid_middle",
    )(counts, x_odd, in_hbm(even), in_hbm(gain), in_hbm(forward), in_hbm(inverse))
    depart(0, y_even)
    y_odd = odd_stage(counts, odd, inverse, x_odd, masked_out)
    depart(1, y_odd)


def odd_stage(counts, odd, inverse, like, masked_out):
    steps = odd.shape[0]
    field_spec = pl.BlockSpec((1, 2, M, 2 * LANES), lambda g: (g, 0, 0, 0))
    return pl.pallas_call(
        functools.partial(grid_odd_kernel, masked=masked_out),
        grid=(steps,),
        in_specs=[smem_spec(), field_spec, whole_spec(inverse.shape)],
        out_specs=wave_block(like),
        out_shape=hbm_result(like.shape, BF16),
        compiler_params=params(16),
        name="grid_odd",
    )(counts, in_hbm(odd), in_hbm(inverse))


def spread_rows(x_ref, scratch):
    chunk = 4
    per = x_ref.shape[1] * x_ref.shape[2]

    def widen(b, carry):
        scratch[pl.ds(b * chunk * per, chunk * per), :] = (
            x_ref[pl.ds(b * chunk, chunk)].astype(F32).reshape(chunk * per, LANES)
        )
        return carry

    lax.fori_loop(0, x_ref.shape[0] // chunk, widen, 0, unroll=2)


def transform_of(table, fields):
    return lax.dot_general(table, fields, (((0,), (0,)), ((), ())), preferred_element_type=F32)


def middle_kernel(first_ref, visc_ref, lev_ref, x_ref, table_ref, out_ref, taken, turned, *, parity):
    waves = x_ref.shape[2]
    lats = x_ref.shape[0] * x_ref.shape[1]
    degrees = table_ref.shape[3]
    spread_rows(x_ref, taken)
    visc = own_levels(visc_ref, lev_ref, lane_ids(degrees) // 32)

    def one_wave(m, carry):
        fields = taken[pl.ds(slot(m), lats, stride=waves), :].astype(BF16)
        table = table_ref[m, 0]
        tangent = transform_of(table, fields)
        degree = first_ref[0] + m + parity + 2 * row_ids(degrees)
        scaled = (degree * (degree + 1)).astype(F32) / float((M + K) * (M + K + 1))
        damp = 1.0 / (1.0 + scaled * visc)
        damped = (tangent * (damp * damp)).astype(BF16)
        turned[pl.ds(slot(m), lats, stride=waves), :] = jnp.dot(
            table, damped, preferred_element_type=F32
        )
        return carry

    lax.fori_loop(0, waves, one_wave, 0, unroll=2)
    per = x_ref.shape[1] * waves

    def narrow(b, carry):
        out_ref[pl.ds(b * 4, 4)] = (
            turned[pl.ds(b * 4 * per, 4 * per), :]
            .astype(BF16)
            .reshape(4, x_ref.shape[1], waves, LANES)
        )
        return carry

    lax.fori_loop(0, x_ref.shape[0] // 4, narrow, 0, unroll=2)


def middle_stage(x, legendre, viscosity, lev, wave_first, parity):
    waves, _, lats, degrees = legendre.shape
    return pl.pallas_call(
        functools.partial(middle_kernel, parity=parity),
        grid=(1,),
        in_specs=[
            smem_spec(),
            smem_spec(),
            smem_spec(),
            whole_spec(x.shape),
            pl.BlockSpec((waves, 1, lats, degrees), lambda g: (0, parity, 0, 0)),
        ],
        out_specs=whole_spec(x.shape),
        out_shape=hbm_result(x.shape, BF16),
        scratch_shapes=[pltpu.VMEM((lats * waves, LANES), F32)] * 2,
        compiler_params=params(26),
        name="middle_stage",
    )(wave_first, viscosity, lev, x, in_hbm(legendre))


def images_kernel(up_ref, down_ref, lev_ref, x_ref, table_ref, out_ref, part_ref, low_ref, taken):
    waves = x_ref.shape[2]
    lats = x_ref.shape[0] * x_ref.shape[1]
    count = table_ref.shape[0]
    step = pl.program_id(0)

    @pl.when(step == 0)
    def _():
        spread_rows(x_ref, taken)

    up_matrix = sum_matrix(up_ref, lev_ref)
    down_matrix = sum_matrix(down_ref, lev_ref)
    for k in range(count):
        fields = taken[pl.ds(slot(step * count + k), lats, stride=waves), :].astype(BF16)
        image = transform_of(table_ref[k, 0], fields)
        high, low = halves(image)
        out_ref[k] = jnp.concatenate([high, low], axis=1)
        up_sum = jnp.dot(twice(high), up_matrix, preferred_element_type=F32)
        part_ref[k] = pack_levels(up_sum).astype(BF16)
        down_sum = jnp.dot(twice(high), down_matrix, preferred_element_type=F32) + jnp.dot(
            low, down_matrix[:LANES], preferred_element_type=F32
        )
        low_ref[k] = jnp.concatenate(halves(pack_levels(down_sum)), axis=1)


def image_stage(x, legendre, up, down, lev, parity):
    x = in_hbm(x) if parity == 0 else x
    waves, _, lats, degrees = legendre.shape
    steps = 4
    count = waves // steps
    return pl.pallas_call(
        images_kernel,
        grid=(steps,),
        in_specs=[
            smem_spec(),
            smem_spec(),
            smem_spec(),
            whole_spec(x.shape),
            pl.BlockSpec((count, 1, lats, degrees), lambda g: (g, parity, 0, 0)),
        ],
        out_specs=(
            pl.BlockSpec((count, degrees, 2 * LANES), lambda g: (g, 0, 0)),
            pl.BlockSpec((count, degrees // 4, LANES), lambda g: (g, 0, 0)),
            pl.BlockSpec((count, degrees // 4, 2 * LANES), lambda g: (g, 0, 0)),
        ),
        out_shape=(
            hbm_result((waves, degrees, 2 * LANES), BF16),
            jax.ShapeDtypeStruct((waves, degrees // 4, LANES), BF16),
            hbm_result((waves, degrees // 4, 2 * LANES), BF16),
        ),
        scratch_shapes=[pltpu.VMEM((lats * waves, LANES), F32)],
        compiler_params=params(20),
        name="image_stage",
    )(up, down, lev, x, in_hbm(legendre))


def gram_of(high, both):
    return lax.dot_general(high, both, (((0,), (0,)), ((), ())), preferred_element_type=F32)


def gram_kernel(image_ref, out_ref):
    @pl.when(pl.program_id(0) == 0)
    def _():
        out_ref[...] = jnp.zeros_like(out_ref)

    rows = image_ref.shape[0] * image_ref.shape[1]
    both = image_ref[...].reshape(rows, 2 * LANES)
    out_ref[...] += gram_of(both[:, :LANES], both)


def gram_stage(images):
    waves, degrees, _ = images.shape
    steps = 4
    return pl.pallas_call(
        gram_kernel,
        grid=(steps,),
        in_specs=[pl.BlockSpec((waves // steps, degrees, 2 * LANES), lambda g: (g, 0, 0))],
        out_specs=whole_spec((LANES, 2 * LANES)),
        out_shape=jax.ShapeDtypeStruct((LANES, 2 * LANES), F32),
        compiler_params=params(12),
        name="gram_stage",
    )(in_hbm(images))


def finish_kernel(down_ref, lev_ref, *refs):
    first = lev_ref[0] * 4
    square = down_ref[first] * down_ref[first]
    for k in range(1, 4):
        square = square + down_ref[first + k] * down_ref[first + k]
    grams = refs[:2]
    lows = refs[2:4]
    totals = refs[4:12]
    total_ref, gram_ref = refs[12:]
    sums = grams[0][...] + grams[1][...]
    cross = sums[:, LANES:]
    gram = sums[:, :LANES] + (cross + cross.T)
    for p in range(2):
        parts = [ref[...].astype(F32) for ref in totals[4 * p : 4 * p + 4]]
        total = ((parts[0] + parts[1]) + (parts[2] + parts[3])).astype(BF16)
        total_ref[p] = total
        flat = total.reshape(-1, LANES)
        low = lows[p][...].reshape(-1, 2 * LANES)
        operand = jnp.concatenate([flat, low], axis=1)
        result = gram_of(flat, operand)
        mixed = result[:, LANES : 2 * LANES] + result[:, 2 * LANES :]
        gram = gram + square * result[:, :LANES] + (mixed + mixed.T)
    same = (row_ids(LANES) // PROBES) == (lane_ids(LANES) // PROBES)
    gram = jnp.where(same, gram, 0.0)
    summed = gram[0:PROBES]
    for b in range(1, LANES // PROBES):
        summed = summed + gram[b * PROBES : (b + 1) * PROBES]
    for shift in (64, 32, 16):
        summed = summed + pltpu.roll(summed, shift, 1)
    gram_ref[...] = jnp.broadcast_to(summed[None], gram_ref.shape)


def finish_stage(grams, lows, totals, down, lev, copies):
    shape = totals[0].shape
    return pl.pallas_call(
        finish_kernel,
        in_specs=[smem_spec(), smem_spec()] + [pl.BlockSpec(memory_space=pltpu.VMEM)] * 12,
        out_shape=(
            hbm_result((2,) + shape, BF16),
            hbm_result((copies, PROBES, LANES), F32),
        ),
        compiler_params=params(16),
        name="finish_stage",
    )(down, lev, *grams, *lows, *totals)


def factor_of(gram):
    rows = row_ids(PROBES)
    lanes = lane_ids(PROBES) & (PROBES - 1)
    upper = jnp.zeros_like(gram)
    inverse = jnp.where(rows == lanes, 1.0, 0.0).astype(F32)
    for k in range(PROBES):
        scale = lax.rsqrt(gram[k : k + 1, k : k + 1])
        scale = scale * (1.5 - 0.5 * gram[k : k + 1, k : k + 1] * scale * scale)
        line = jnp.where(lanes[0:1] >= k, gram[k : k + 1] * scale, 0.0)
        solved = inverse[k : k + 1] * scale
        column = jnp.where(rows[:, 0:1] > k, gram[:, k : k + 1] * scale, 0.0)
        upper = jnp.where(rows == k, line, upper)
        gram = gram - column * line
        inverse = jnp.where(rows == k, solved, inverse - column * solved)
    return upper, inverse


def basis_kernel(
    down_ref, lev_ref, own_ref, one_ref, two_ref, three_ref, even_ref, odd_ref, total_ref,
    out_ref, factor_ref, mix, *, row_scale,
):
    @pl.when(pl.program_id(0) == 0)
    def _():
        gram = (own_ref[...] + two_ref[...]) + (one_ref[...] + three_ref[...])
        upper, inverse = factor_of(gram)
        factor_ref[...] = upper[:, :PROBES] / row_scale
        pick = ((lane_ids(PROBES) & (PROBES - 1)) == row_ids(PROBES)).astype(BF16)
        same = (row_ids(LANES) // PROBES) == (lane_ids(LANES) // PROBES)
        high, low = halves(inverse * row_scale)
        mix_high = jnp.where(same, gram_of(high, pick), 0.0).astype(BF16)
        mix_low = jnp.where(same, gram_of(low, pick), 0.0).astype(BF16)
        mix[0:LANES] = mix_high
        mix[LANES : 2 * LANES] = mix_high
        mix[2 * LANES :] = mix_low

    matrix = unpack_matrix(down_ref, lev_ref)
    for m in range(even_ref.shape[0]):
        for p, image_ref in enumerate((even_ref, odd_ref)):
            both = image_ref[m]
            full = (both[:, :LANES].astype(F32) + both[:, LANES:].astype(F32)) + unpack_levels(
                total_ref[p, m], matrix
            )
            high, low = halves(full)
            value = jnp.dot(
                jnp.concatenate([high, low, high], axis=1), mix[...], preferred_element_type=F32
            )
            out_ref[m, p] = value.astype(BF16)


def basis_stage(grams, images, total, down, lev, row_scale):
    waves, degrees, _ = images[0].shape
    steps = 4
    count = waves // steps
    image_spec = pl.BlockSpec((count, degrees, 2 * LANES), lambda g: (g, 0, 0))
    return pl.pallas_call(
        functools.partial(basis_kernel, row_scale=row_scale),
        grid=(steps,),
        in_specs=[smem_spec(), smem_spec()]
        + [whole_spec((PROBES, LANES))] * 4
        + [
            image_spec,
            image_spec,
            pl.BlockSpec((2, count, degrees // 4, LANES), lambda g: (0, g, 0, 0)),
        ],
        out_specs=(
            pl.BlockSpec((count, 2, degrees, LANES), lambda g: (g, 0, 0, 0)),
            whole_spec((PROBES, PROBES)),
        ),
        out_shape=(
            hbm_result((waves, 2, degrees, LANES), BF16),
            hbm_result((PROBES, PROBES), F32),
        ),
        scratch_shapes=[pltpu.VMEM((3 * LANES, LANES), BF16)],
        compiler_params=params(14),
        name="basis_stage",
    )(down, lev, *grams, in_hbm(images[0]), in_hbm(images[1]), in_hbm(total))


def exchange(blocks):
    return lax.all_to_all(blocks, "lat", split_axis=0, concat_axis=0, tiled=True)


def from_levels(part):
    count = lax.axis_size("lev")
    return [
        lax.ppermute(part, "lev", [(i, (i + k) % count) for i in range(count)])
        for k in range(1, count)
    ]


def shards(
    probes, legendre, quad_weight, trunc_counts, background, level_up, level_down, viscosity
):
    lat_count = lax.axis_size("lat")
    lev_count = lax.axis_size("lev")
    lat_index = lax.axis_index("lat")
    lev_index = lax.axis_index("lev")
    wave_local = probes.shape[0]
    level_local = probes.shape[3] // (2 * PROBES)
    lon_count = 2 * M

    lev = lev_index.astype(jnp.int32).reshape(1)
    wave_first = (lat_index * wave_local).astype(jnp.int32).reshape(1)
    forward = wave_tables(M)
    tables = (jnp.asarray(forward), jnp.asarray(np.ascontiguousarray(forward.transpose(0, 2, 1))))

    sent = {}
    for p in range(2):
        partial = level_partial(probes, level_down, lev, p)
        totals = [partial] + from_levels(partial)
        blocks = legendre_forward(probes, totals, legendre, level_up, lev, p)
        sent[p] = exchange(blocks)

    own_gain = lax.dynamic_slice_in_dim(background, lev_index * level_local, level_local, 2)
    own_gain = own_gain * (quad_weight / float(lon_count))[None, :, None, None]
    own_gain = own_gain.reshape(2, -1, 2, level_local, lon_count).swapaxes(2, 3)
    own_gain = own_gain.reshape(2, -1, 2 * level_local, lon_count).astype(BF16)
    gain = spread_gain(own_gain)

    folded = {}

    def depart(p, values):
        folded[p] = exchange(values)

    grid_pass(lambda p: sent[p], depart, trunc_counts, gain, tables, True, False)
    second = {
        p: exchange(middle_stage(folded[p], legendre, viscosity, lev, wave_first, p))
        for p in range(2)
    }
    folded2 = {}

    def depart2(p, values):
        folded2[p] = exchange(values)

    grid_pass(lambda p: second[p], depart2, trunc_counts, gain, tables, False, True)
    images, lows, grams, totals = [], [], [], []
    for p in range(2):
        image, part, low = image_stage(folded2[p], legendre, level_up, level_down, lev, p)
        images.append(image)
        lows.append(low)
        grams.append(gram_stage(image))
        totals += [part] + from_levels(part)
    total, gram_copies = finish_stage(grams, lows, totals, level_down, lev, lat_count)
    over_lat = jnp.sum(exchange(gram_copies), axis=0)
    row_scale = math.sqrt(M * K * 2 * level_local * lev_count)
    return basis_stage(
        [over_lat] + from_levels(over_lat), images, total, level_down, lev, row_scale
    )


def solution(mesh):
    placed = (
        P("lat", None, None, "lev"),
        P("lat", None, None, None),
        P("lat"),
        P("lat"),
        P(None, "lat", None, None),
        P(),
        P(),
        P(),
    )
    return jax.shard_map(
        shards,
        mesh=mesh,
        in_specs=placed,
        out_specs=(P("lat", None, None, "lev"), P()),
        check_vma=False,
    )
```

time: 734 us -> 380 us (0.52)
  blocking collectives: 182 us -> 13.1 us
  matrix products: 148 us -> 0 us
  local copies, waits for them, and re-layouts: 136 us -> 5.01 us
  Pallas kernels: 0 us -> 130 us
  other arithmetic: 48.5 us -> 1.43 us
  starting transfers between devices: 19.8 us -> 52.6 us
  between operations: 14.5 us -> 0.88 us
    dot_general x8 -> x0, matrix products: 147 us -> none  [the longest x1 64.4 us: shards(): lax.dot_general(flattened, flattened, (((0,), (0,)), ((), ())), precision...]
    pallas_call x0 -> x19, Pallas kernels: none -> 130 us  [the longest x2 25.3 us: middle_stage(): pl.pallas_call(functools.partial(middle_kernel, parity=parity), grid=(1,)...]
    all_to_all x2 -> x1, blocking collectives: 118 us -> 13.1 us  [exchange(): lax.all_to_all(blocks, 'lat', split_axis=0, concat_axis=0, tiled=True)]
    psum x2 -> x0, waiting for transfers between devices: 74.4 us -> none  [level_sum(): lax.psum(partial_value.astype(jnp.bfloat16), 'lev').astype(jnp.float32)]
    psum x1 -> x0, blocking collectives: 63.6 us -> none  [shards(): gram_matrix = lax.psum(gram_local, ('lat', 'lev'))]
    ppermute x0 -> x15, waiting for transfers between devices: none -> 40.4 us  [from_levels(): lax.ppermute(part, 'lev', [(i, (i + k) % count) for i in range(count)])]
    reshape x2 -> x0, local copies, waits for them, and re-layouts: 38.5 us -> none  [the longest x1 19.6 us: shards(): flattened = images.reshape(-1, PROBES)]
    all_to_all x2 -> x8, waiting for transfers between devices: 103 us -> 135 us  [exchange(): lax.all_to_all(blocks, 'lat', split_axis=0, concat_axis=0, tiled=True)]
  transfers between devices with their start and end apart: 4 -> 23, of which waited for: 4 -> 19; matrix products, arithmetic and copies ran while one was open for 2% -> 0% of each run, Pallas kernels for 0% -> 23%
where the time goes in v1:
time: 380 us; the launch traced here: 379 us
  waiting for transfers between devices  176 us (46%)
  Pallas kernels  130 us (34%)
  starting transfers between devices  52.6 us (14%)
  blocking collectives  13.1 us (3%)
  local copies, waits for them, and re-layouts  5.01 us (1%)
    all_to_all x8, waiting for transfers between devices, exchange(): lax.all_to_all(blocks, 'lat', split_axis=0, concat_axis=0, tiled=True)  135 us
    all_to_all x8, starting transfers between devices, exchange(): lax.all_to_all(blocks, 'lat', split_axis=0, concat_axis=0, tiled=True)  42.1 us
    ppermute x15, waiting for transfers between devices, from_levels(): lax.ppermute(part, 'lev', [(i, (i + k) % count) for i in range(count)])  40.4 us
    pallas_call x2, Pallas kernels, middle_stage(): pl.pallas_call(functools.partial(middle_kernel, parity=parity), grid=(1,)...  25.3 us
    pallas_call x2, Pallas kernels, grid_pass(): pl.pallas_call(functools.partial(grid_middle_kernel, masked_in=masked_in,...  19.3 us
    pallas_call x2, Pallas kernels, image_stage(): pl.pallas_call(images_kernel, grid=(steps,), in_specs=[smem_spec(), smem_...  17.9 us
    pallas_call x2, Pallas kernels, legendre_forward(): pl.pallas_call(legendre_kernel, grid=(steps,), in_specs=[smem_spec(), sme...  17.5 us
    all_to_all x1, blocking collectives, exchange(): lax.all_to_all(blocks, 'lat', split_axis=0, concat_axis=0, tiled=True)  13.1 us
  transfers between devices with their start and end apart: 23, of which 19 were waited for; matrix products, arithmetic and copies ran while one was open for 0% of the time, Pallas kernels for 23%

profile of v1, /device:TPU:1, one launch (start us, length us, event | category | flops | bytes accessed | tf_op | source)
XLA Modules:
  0.0 378.6 jit_solution(3655411661696310919)
XLA Ops:
  0.7 0.6 copy-done.2
  1.3 2.0 level_partial.3.refs_0_
  3.3 3.4 collective-permute-start.5
  6.6 0.5 collective-permute-start.4
  7.2 0.6 collective-permute-start.3
  7.8 5.0 %collective-permute-done.5.refs_3_ = bf16[16,64,128]{2,1,0:T(8,128)(2,1)S(1)} collective-permute-done((bf16[16,64,128]{2,1,0:T(8,128)(2,1)S(1)}, bf16[16,64,128]{2,1,0:T(8,128)(2,1)S(1)}, u32[]{:S(2)}, u32[]{:S(2)}) %collective-permute-start.5) | collective-permute-done | bytes 262176 | tf_op jit(solution)/shard_map/ppermute | solution.py:658
  12.8 2.3 collective-permute-done.4.refs_2_
  15.1 6.9 %collective-permute-done.3.refs_1_ = bf16[16,64,128]{2,1,0:T(8,128)(2,1)S(1)} collective-permute-done((bf16[16,64,128]{2,1,0:T(8,128)(2,1)S(1)}, bf16[16,64,128]{2,1,0:T(8,128)(2,1)S(1)}, u32[]{:S(2)}, u32[]{:S(2)}) %collective-permute-start.3) | collective-permute-done | bytes 262176 | tf_op jit(solution)/shard_map/ppermute | solution.py:658
  22.0 8.8 %legendre_forward.3 = bf16[32,16,16,128]{3,2,1,0:T(8,128)(2,1)} custom-call(f32[16]{0:T(128)S(1)} %copy-done.5, s32[1]{0:T(128)} %bitcast.lev_ref, bf16[16,2,256,128]{3,2,1,0:T(8,128)(2,1)} %probes_ref.7, bf16[16,64,128]{2,1,0:T(8,128)(2,1)S(1)} %level_partial.3.refs_0_, bf16[16,64,128]{2,1,0:T(8,128)(2,1)S(1)} %collective-permute-done.3.refs_1_, ...), custom_call_target="tpu_custom_call" | custom-call | tf_op jit(solution)/shard_map/legendre_forward/pallas_call | solution.py:180
  30.7 8.7 %all-to-all-start.1 = ((bf16[32,16,16,128]{3,2,1,0:T(8,128)(2,1)}), bf16[32,16,16,128]{3,2,1,0:T(8,128)(2,1)S(1)}, u32[]{:S(2)}, u32[]{:S(2)}) async-start(bf16[32,16,16,128]{3,2,1,0:T(8,128)(2,1)} %legendre_forward.3), calls=%async_computation.1 | async-start | bytes 4194304 | tf_op jit(solution)/shard_map/all_to_all | solution.py:652
  39.5 2.0 level_partial.2.refs_0_
  41.5 0.4 collective-permute-start.2
  41.9 0.5 collective-permute-start.1
  42.4 0.6 collective-permute-start
  43.0 6.2 %collective-permute-done.2.refs_3_ = bf16[16,64,128]{2,1,0:T(8,128)(2,1)S(1)} collective-permute-done((bf16[16,64,128]{2,1,0:T(8,128)(2,1)S(1)}, bf16[16,64,128]{2,1,0:T(8,128)(2,1)S(1)}, u32[]{:S(2)}, u32[]{:S(2)}) %collective-permute-start.2) | collective-permute-done | bytes 262176 | tf_op jit(solution)/shard_map/ppermute | solution.py:658
  49.2 1.6 collective-permute-done.1.refs_2_
  50.8 6.5 %collective-permute-done.refs_1_ = bf16[16,64,128]{2,1,0:T(8,128)(2,1)S(1)} collective-permute-done((bf16[16,64,128]{2,1,0:T(8,128)(2,1)S(1)}, bf16[16,64,128]{2,1,0:T(8,128)(2,1)S(1)}, u32[]{:S(2)}, u32[]{:S(2)}) %collective-permute-start) | collective-permute-done | bytes 262176 | tf_op jit(solution)/shard_map/ppermute | solution.py:658
  57.2 8.7 %legendre_forward.2 = bf16[32,16,16,128]{3,2,1,0:T(8,128)(2,1)} custom-call(f32[16]{0:T(128)S(1)} %copy-done.5, s32[1]{0:T(128)} %bitcast.lev_ref, bf16[16,2,256,128]{3,2,1,0:T(8,128)(2,1)} %probes_ref.7, bf16[16,64,128]{2,1,0:T(8,128)(2,1)S(1)} %level_partial.2.refs_0_, bf16[16,64,128]{2,1,0:T(8,128)(2,1)S(1)} %collective-permute-done.refs_1_, ...), custom_call_target="tpu_custom_call" | custom-call | tf_op jit(solution)/shard_map/legendre_forward/pallas_call | solution.py:180
  66.0 1.8 all-to-all-done.1.x_ref
  67.8 1.3 copy-done.8
  69.2 5.6 %all-to-all-start = ((bf16[32,16,16,128]{3,2,1,0:T(8,128)(2,1)}), bf16[32,16,16,128]{3,2,1,0:T(8,128)(2,1)S(1)}, u32[]{:S(2)}, u32[]{:S(2)}) async-start(bf16[32,16,16,128]{3,2,1,0:T(8,128)(2,1)} %legendre_forward.2), calls=%async_computation | async-start | bytes 4194304 | tf_op jit(solution)/shard_map/all_to_all | solution.py:652
  74.8 1.4 multiply_convert_fusion
  76.6 5.0 %spread_gain.1.gain_ref = bf16[2,8,1024,128]{3,2,1,0:T(8,128)(2,1)} custom-call(bf16[2,8,8,1024]{3,2,1,0:T(8,128)(2,1)S(1)} %convert_element_type.12.gain_ref, bf16[8,128]{1,0:T(8,128)(2,1)S(1)} %copy-done.6), custom_call_target="tpu_custom_call" | custom-call | tf_op jit(solution)/shard_map/spread_gain/pallas_call | solution.py:299
  81.6 6.1 %grid_even.2.even_ref = f32[4,2,512,256]{3,2,1,0:T(8,128)} custom-call(s32[16]{0:T(128)S(1)} %copy-done.4, bf16[32,16,16,128]{3,2,1,0:T(8,128)(2,1)} %copy-done.8, bf16[2,512,512]{2,1,0:T(8,128)(2,1)} %constant.26.clone.table_ref.forward_ref), custom_call_target="tpu_custom_call" | custom-call | tf_op jit(solution)/shard_map/grid_even/pallas_call | solution.py:324
  87.6 15.5 %all-to-all-done.x_ref = bf16[32,16,16,128]{3,2,1,0:T(8,128)(2,1)S(1)} async-done(((bf16[32,16,16,128]{3,2,1,0:T(8,128)(2,1)}), bf16[32,16,16,128]{3,2,1,0:T(8,128)(2,1)S(1)}, u32[]{:S(2)}, u32[]{:S(2)}) %all-to-all-start) | async-done | bytes 2097184 | tf_op jit(solution)/shard_map/all_to_all | solution.py:652
  103.2 9.7 %grid_middle.2 = (bf16[32,16,16,128]{3,2,1,0:T(8,128)(2,1)}, bf16[4,2,512,256]{3,2,1,0:T(8,128)(2,1)}) custom-call(s32[16]{0:T(128)S(1)} %copy-done.4, bf16[32,16,16,128]{3,2,1,0:T(8,128)(2,1)S(1)} %all-to-all-done.x_ref, f32[4,2,512,256]{3,2,1,0:T(8,128)} %grid_even.2.even_ref, bf16[2,8,1024,128]{3,2,1,0:T(8,128)(2,1)} %spread_gain.1.gain_ref, ...), custom_call_target="tpu_custom_call" | custom-call | tf_op jit(solution)/shard_map/grid_middle/pallas_call | solution.py:336
  112.8 4.5 %all-to-all-start.4 = ((bf16[32,16,16,128]{3,2,1,0:T(8,128)(2,1)}), bf16[32,16,16,128]{3,2,1,0:T(8,128)(2,1)S(1)}, u32[]{:S(2)}, u32[]{:S(2)}) async-start(bf16[32,16,16,128]{3,2,1,0:T(8,128)(2,1)} %get-tuple-element.15), calls=%async_computation.4 | async-start | bytes 4194304 | tf_op jit(solution)/shard_map/all_to_all | solution.py:652
  117.3 5.2 %grid_odd.2 = bf16[32,16,16,128]{3,2,1,0:T(8,128)(2,1)} custom-call(s32[16]{0:T(128)S(1)} %copy-done.4, bf16[4,2,512,256]{3,2,1,0:T(8,128)(2,1)} %get-tuple-element.14.odd_ref, bf16[2,512,512]{2,1,0:T(8,128)(2,1)} %constant.27.clone.inverse_ref.table_ref), custom_call_target="tpu_custom_call" | custom-call | tf_op jit(solution)/shard_map/grid_odd/pallas_call | solution.py:361
  122.5 23.2 %all-to-all-done.4.x_ref = bf16[32,16,16,128]{3,2,1,0:T(8,128)(2,1)S(1)} async-done(((bf16[32,16,16,128]{3,2,1,0:T(8,128)(2,1)}), bf16[32,16,16,128]{3,2,1,0:T(8,128)(2,1)S(1)}, u32[]{:S(2)}, u32[]{:S(2)}) %all-to-all-start.4) | async-done | bytes 2097184 | tf_op jit(solution)/shard_map/all_to_all | solution.py:652
  145.7 5.2 %all-to-all-start.2 = ((bf16[32,16,16,128]{3,2,1,0:T(8,128)(2,1)}), bf16[32,16,16,128]{3,2,1,0:T(8,128)(2,1)}, u32[]{:S(2)}, u32[]{:S(2)}) async-start(bf16[32,16,16,128]{3,2,1,0:T(8,128)(2,1)} %grid_odd.2), calls=%async_computation.2 | async-start | bytes 4194304 | tf_op jit(solution)/shard_map/all_to_all | solution.py:652
  150.9 12.3 %middle_stage.3 = bf16[32,16,16,128]{3,2,1,0:T(8,128)(2,1)} custom-call(s32[1]{0:T(128)} %bitcast.1.first_ref, f32[16]{0:T(128)S(1)} %copy-done.7, s32[1]{0:T(128)} %bitcast.lev_ref, bf16[32,16,16,128]{3,2,1,0:T(8,128)(2,1)S(1)} %all-to-all-done.4.x_ref, bf16[16,2,512,256]{3,2,1,0:T(8,128)(2,1)} %table_ref.11), custom_call_target="tpu_custom_call" | custom-call | tf_op jit(solution)/shard_map/middle_stage/pallas_call | solution.py:425
  163.3 16.1 %all-to-all-done.2.x_ref = bf16[32,16,16,128]{3,2,1,0:T(8,128)(2,1)} async-done(((bf16[32,16,16,128]{3,2,1,0:T(8,128)(2,1)}), bf16[32,16,16,128]{3,2,1,0:T(8,128)(2,1)}, u32[]{:S(2)}, u32[]{:S(2)}) %all-to-all-start.2) | async-done | bytes 2097184 | tf_op jit(solution)/shard_map/all_to_all | solution.py:652
  179.4 4.5 %all-to-all-start.5 = ((bf16[32,16,16,128]{3,2,1,0:T(8,128)(2,1)}), bf16[32,16,16,128]{3,2,1,0:T(8,128)(2,1)S(1)}, u32[]{:S(2)}, u32[]{:S(2)}) async-start(bf16[32,16,16,128]{3,2,1,0:T(8,128)(2,1)} %middle_stage.3), calls=%async_computation.5 | async-start | bytes 4194304 | tf_op jit(solution)/shard_map/all_to_all | solution.py:652
  183.9 13.0 %middle_stage.2 = bf16[32,16,16,128]{3,2,1,0:T(8,128)(2,1)} custom-call(s32[1]{0:T(128)} %bitcast.1.first_ref, f32[16]{0:T(128)S(1)} %copy-done.7, s32[1]{0:T(128)} %bitcast.lev_ref, bf16[32,16,16,128]{3,2,1,0:T(8,128)(2,1)} %all-to-all-done.2.x_ref, bf16[16,2,512,256]{3,2,1,0:T(8,128)(2,1)} %table_ref.11), custom_call_target="tpu_custom_call" | custom-call | tf_op jit(solution)/shard_map/middle_stage/pallas_call | solution.py:425
  196.9 15.5 %all-to-all-done.5.x_ref = bf16[32,16,16,128]{3,2,1,0:T(8,128)(2,1)S(1)} async-done(((bf16[32,16,16,128]{3,2,1,0:T(8,128)(2,1)}), bf16[32,16,16,128]{3,2,1,0:T(8,128)(2,1)S(1)}, u32[]{:S(2)}, u32[]{:S(2)}) %all-to-all-start.5) | async-done | bytes 2097184 | tf_op jit(solution)/shard_map/all_to_all | solution.py:652
  212.3 1.3 copy-done.10
  213.7 4.7 %all-to-all-start.3 = ((bf16[32,16,16,128]{3,2,1,0:T(8,128)(2,1)}), bf16[32,16,16,128]{3,2,1,0:T(8,128)(2,1)S(1)}, u32[]{:S(2)}, u32[]{:S(2)}) async-start(bf16[32,16,16,128]{3,2,1,0:T(8,128)(2,1)} %middle_stage.2), calls=%async_computation.3 | async-start | bytes 4194304 | tf_op jit(solution)/shard_map/all_to_all | solution.py:652
  218.3 5.8 %grid_even.3.even_ref = f32[4,2,512,256]{3,2,1,0:T(8,128)} custom-call(s32[16]{0:T(128)S(1)} %copy-done.4, bf16[32,16,16,128]{3,2,1,0:T(8,128)(2,1)} %copy-done.10, bf16[2,512,512]{2,1,0:T(8,128)(2,1)} %constant.26.clone.table_ref.forward_ref), custom_call_target="tpu_custom_call" | custom-call | tf_op jit(solution)/shard_map/grid_even/pallas_call | solution.py:324
  224.1 22.6 %all-to-all-done.3.x_ref = bf16[32,16,16,128]{3,2,1,0:T(8,128)(2,1)S(1)} async-done(((bf16[32,16,16,128]{3,2,1,0:T(8,128)(2,1)}), bf16[32,16,16,128]{3,2,1,0:T(8,128)(2,1)S(1)}, u32[]{:S(2)}, u32[]{:S(2)}) %all-to-all-start.3) | async-done | bytes 2097184 | tf_op jit(solution)/shard_map/all_to_all | solution.py:652
  246.8 9.6 %grid_middle.3 = (bf16[32,16,16,128]{3,2,1,0:T(8,128)(2,1)}, bf16[4,2,512,256]{3,2,1,0:T(8,128)(2,1)}) custom-call(s32[16]{0:T(128)S(1)} %copy-done.4, bf16[32,16,16,128]{3,2,1,0:T(8,128)(2,1)S(1)} %all-to-all-done.3.x_ref, f32[4,2,512,256]{3,2,1,0:T(8,128)} %grid_even.3.even_ref, bf16[2,8,1024,128]{3,2,1,0:T(8,128)(2,1)} %spread_gain.1.gain_ref, ...), custom_call_target="tpu_custom_call" | custom-call | tf_op jit(solution)/shard_map/grid_middle/pallas_call | solution.py:336
  256.4 4.5 %all-to-all-start.6 = ((bf16[32,16,16,128]{3,2,1,0:T(8,128)(2,1)}), bf16[32,16,16,128]{3,2,1,0:T(8,128)(2,1)S(1)}, u32[]{:S(2)}, u32[]{:S(2)}) async-start(bf16[32,16,16,128]{3,2,1,0:T(8,128)(2,1)} %get-tuple-element.16), calls=%async_computation.6 | async-start | bytes 4194304 | tf_op jit(solution)/shard_map/all_to_all | solution.py:652
  260.9 5.4 %grid_odd.3 = bf16[32,16,16,128]{3,2,1,0:T(8,128)(2,1)} custom-call(s32[16]{0:T(128)S(1)} %copy-done.4, bf16[4,2,512,256]{3,2,1,0:T(8,128)(2,1)} %get-tuple-element.18.odd_ref, bf16[2,512,512]{2,1,0:T(8,128)(2,1)} %constant.27.clone.inverse_ref.table_ref), custom_call_target="tpu_custom_call" | custom-call | tf_op jit(solution)/shard_map/grid_odd/pallas_call | solution.py:361
  266.2 23.0 %all-to-all-done.6.x_ref = bf16[32,16,16,128]{3,2,1,0:T(8,128)(2,1)S(1)} async-done(((bf16[32,16,16,128]{3,2,1,0:T(8,128)(2,1)}), bf16[32,16,16,128]{3,2,1,0:T(8,128)(2,1)S(1)}, u32[]{:S(2)}, u32[]{:S(2)}) %all-to-all-start.6) | async-done | bytes 2097184 | tf_op jit(solution)/shard_map/all_to_all | solution.py:652
  289.3 1.3 copy-done.9
  290.6 4.5 %all-to-all-start.7 = ((bf16[32,16,16,128]{3,2,1,0:T(8,128)(2,1)}), bf16[32,16,16,128]{3,2,1,0:T(8,128)(2,1)S(1)}, u32[]{:S(2)}, u32[]{:S(2)}) async-start(bf16[32,16,16,128]{3,2,1,0:T(8,128)(2,1)} %grid_odd.3), calls=%async_computation.7 | async-start | bytes 4194304 | tf_op jit(solution)/shard_map/all_to_all | solution.py:652
  295.1 9.3 %image_stage.2 = (bf16[16,256,256]{2,1,0:T(8,128)(2,1)}, bf16[16,64,128]{2,1,0:T(8,128)(2,1)S(1)}, bf16[16,64,256]{2,1,0:T(8,128)(2,1)}) custom-call(f32[16]{0:T(128)S(1)} %copy-done.5, f32[16]{0:T(128)S(1)} %copy-done.3, s32[1]{0:T(128)} %bitcast.lev_ref, bf16[32,16,16,128]{3,2,1,0:T(8,128)(2,1)} %copy-done.9, bf16[16,2,512,256]{3,2,1,0:T(8,128)(2,1)} %table_ref.11), custom_call_target="tpu_custom_call" | custom-call | tf_op jit(solution)/shard_map/image_stage/pallas_call | solution.py:473
  304.4 0.6 collective-permute-start.8
  305.3 0.6 collective-permute-start.6
  305.9 17.6 %all-to-all-done.7.x_ref = bf16[32,16,16,128]{3,2,1,0:T(8,128)(2,1)S(1)} async-done(((bf16[32,16,16,128]{3,2,1,0:T(8,128)(2,1)}), bf16[32,16,16,128]{3,2,1,0:T(8,128)(2,1)S(1)}, u32[]{:S(2)}, u32[]{:S(2)}) %all-to-all-start.7) | async-done | bytes 2097184 | tf_op jit(solution)/shard_map/all_to_all | solution.py:652
  323.5 8.6 %image_stage.3 = (bf16[16,256,256]{2,1,0:T(8,128)(2,1)}, bf16[16,64,128]{2,1,0:T(8,128)(2,1)S(1)}, bf16[16,64,256]{2,1,0:T(8,128)(2,1)}) custom-call(f32[16]{0:T(128)S(1)} %copy-done.5, f32[16]{0:T(128)S(1)} %copy-done.3, s32[1]{0:T(128)} %bitcast.lev_ref, bf16[32,16,16,128]{3,2,1,0:T(8,128)(2,1)S(1)} %all-to-all-done.7.x_ref, ...), custom_call_target="tpu_custom_call" | custom-call | tf_op jit(solution)/shard_map/image_stage/pallas_call | solution.py:473
  332.1 0.6 collective-permute-start.11
  333.0 0.6 collective-permute-start.9
  333.6 3.1 gram_stage.2.refs_0_
  336.7 3.0 gram_stage.3.refs_1_
  339.8 1.2 collective-permute-done.10.refs_10_
  341.0 7.0 %collective-permute-done.9.refs_9_ = bf16[16,64,128]{2,1,0:T(8,128)(2,1)S(1)} collective-permute-done((bf16[16,64,128]{2,1,0:T(8,128)(2,1)S(1)}, bf16[16,64,128]{2,1,0:T(8,128)(2,1)S(1)}, u32[]{:S(2)}, u32[]{:S(2)}) %collective-permute-start.9) | collective-permute-done | bytes 262176 | tf_op jit(solution)/shard_map/ppermute | solution.py:658
  348.1 2.1 finish_stage.1
  350.1 13.1 %all_to_all.45 = f32[32,16,128]{2,1,0:T(8,128)S(1)} all-to-all(f32[32,16,128]{2,1,0:T(8,128)} %get-tuple-element.24), channel_id=1, replica_groups=mesh['lat'=32,'lev'=4] {'lat'}, dimensions={0} | all-to-all | bytes 524288 | tf_op jit(solution)/shard_map/all_to_all | solution.py:652
  363.2 0.4 collective-permute-start.14
  363.9 0.9 collective-permute-start.12
  364.8 1.0 collective-permute-done.14.three_ref
  365.8 1.8 collective-permute-done.13.two_ref
  367.7 0.8 collective-permute-done.12.one_ref
  368.5 10.1 %basis_stage.1 = (bf16[16,2,256,128]{3,2,1,0:T(8,128)(2,1)}, f32[16,16]{1,0:T(8,128)}) custom-call(f32[16]{0:T(128)S(1)} %copy-done.3, s32[1]{0:T(128)} %bitcast.lev_ref, f32[16,128]{1,0:T(8,128)S(1)} %reduce_sum.9.own_ref, f32[16,128]{1,0:T(8,128)S(1)} %collective-permute-done.12.one_ref, f32[16,128]{1,0:T(8,128)S(1)} %collective-permute-done.13.two_ref, ...), custom_call_target="tpu_custom_call" | custom-call | tf_op jit(solution)/shard_map/basis_stage/pallas_call | solution.py:627
  (31 shorter events, 1.3 us)
Async XLA Ops:
  0.6 21.4 %copy-start.5 = (f32[16]{0:T(128)S(1)}, f32[16]{0:T(128)}, u32[]{:S(2)}) copy-start(f32[16]{0:T(128)} %up_ref.3) | copy-start | bytes 196
  0.6 0.7 copy-start.2
  3.3 9.5 %collective-permute-start.5 = (bf16[16,64,128]{2,1,0:T(8,128)(2,1)S(1)}, bf16[16,64,128]{2,1,0:T(8,128)(2,1)S(1)}, u32[]{:S(2)}, u32[]{:S(2)}) collective-permute-start(bf16[16,64,128]{2,1,0:T(8,128)(2,1)S(1)} %level_partial.3.refs_0_), channel_id=1, source_target_pairs={{0,3},{1,0},{2,1},{3,2},{4,7},{5,4},{6,5},{7,6},{8,11},{9,8},{10,9... | collective-permute-start | bytes 786440 | tf_op jit(solution)/shard_map/ppermute | solution.py:658
  6.6 8.5 %collective-permute-start.4 = (bf16[16,64,128]{2,1,0:T(8,128)(2,1)S(1)}, bf16[16,64,128]{2,1,0:T(8,128)(2,1)S(1)}, u32[]{:S(2)}, u32[]{:S(2)}) collective-permute-start(bf16[16,64,128]{2,1,0:T(8,128)(2,1)S(1)} %level_partial.3.refs_0_), channel_id=1, source_target_pairs={{0,2},{1,3},{2,0},{3,1},{4,6},{5,7},{6,4},{7,5},{8,10},{9,11},{10,... | collective-permute-start | bytes 786440 | tf_op jit(solution)/shard_map/ppermute | solution.py:658
  7.2 14.8 %collective-permute-start.3 = (bf16[16,64,128]{2,1,0:T(8,128)(2,1)S(1)}, bf16[16,64,128]{2,1,0:T(8,128)(2,1)S(1)}, u32[]{:S(2)}, u32[]{:S(2)}) collective-permute-start(bf16[16,64,128]{2,1,0:T(8,128)(2,1)S(1)} %level_partial.3.refs_0_), channel_id=1, source_target_pairs={{0,1},{1,2},{2,3},{3,0},{4,5},{5,6},{6,7},{7,4},{8,9},{9,10},{10,1... | collective-permute-start | bytes 786440 | tf_op jit(solution)/shard_map/ppermute | solution.py:658
  30.7 8.7 %copy-start.3 = (f32[16]{0:T(128)S(1)}, f32[16]{0:T(128)}, u32[]{:S(2)}) copy-start(f32[16]{0:T(128)} %down_ref.7) | copy-start | bytes 196
  30.7 37.1 %all-to-all-start.1 = ((bf16[32,16,16,128]{3,2,1,0:T(8,128)(2,1)}), bf16[32,16,16,128]{3,2,1,0:T(8,128)(2,1)S(1)}, u32[]{:S(2)}, u32[]{:S(2)}) async-start(bf16[32,16,16,128]{3,2,1,0:T(8,128)(2,1)} %legendre_forward.3), calls=%async_computation.1 | async-start | bytes 4194304 | tf_op jit(solution)/shard_map/all_to_all | solution.py:652
  41.5 7.7 %collective-permute-start.2 = (bf16[16,64,128]{2,1,0:T(8,128)(2,1)S(1)}, bf16[16,64,128]{2,1,0:T(8,128)(2,1)S(1)}, u32[]{:S(2)}, u32[]{:S(2)}) collective-permute-start(bf16[16,64,128]{2,1,0:T(8,128)(2,1)S(1)} %level_partial.2.refs_0_), channel_id=1, source_target_pairs={{0,3},{1,0},{2,1},{3,2},{4,7},{5,4},{6,5},{7,6},{8,11},{9,8},{10,9... | collective-permute-start | bytes 786440 | tf_op jit(solution)/shard_map/ppermute | solution.py:658
  41.9 8.9 %collective-permute-start.1 = (bf16[16,64,128]{2,1,0:T(8,128)(2,1)S(1)}, bf16[16,64,128]{2,1,0:T(8,128)(2,1)S(1)}, u32[]{:S(2)}, u32[]{:S(2)}) collective-permute-start(bf16[16,64,128]{2,1,0:T(8,128)(2,1)S(1)} %level_partial.2.refs_0_), channel_id=1, source_target_pairs={{0,2},{1,3},{2,0},{3,1},{4,6},{5,7},{6,4},{7,5},{8,10},{9,11},{10,... | collective-permute-start | bytes 786440 | tf_op jit(solution)/shard_map/ppermute | solution.py:658
  42.4 14.8 %collective-permute-start = (bf16[16,64,128]{2,1,0:T(8,128)(2,1)S(1)}, bf16[16,64,128]{2,1,0:T(8,128)(2,1)S(1)}, u32[]{:S(2)}, u32[]{:S(2)}) collective-permute-start(bf16[16,64,128]{2,1,0:T(8,128)(2,1)S(1)} %level_partial.2.refs_0_), channel_id=1, source_target_pairs={{0,1},{1,2},{2,3},{3,0},{4,5},{5,6},{6,7},{7,4},{8,9},{9,10},{10,1... | collective-permute-start | bytes 786440 | tf_op jit(solution)/shard_map/ppermute | solution.py:658
  66.0 8.8 %copy-start.11 = (f32[16]{0:T(128)S(1)}, f32[16]{0:T(128)}, u32[]{:S(2)}) copy-start(f32[16]{0:T(128)} %param.13) | copy-start | bytes 196
  66.0 10.6 %copy-start.6 = (bf16[8,128]{1,0:T(8,128)(2,1)S(1)}, bf16[8,128]{1,0:T(8,128)(2,1)}, u32[]{:S(2)}) copy-start(bf16[8,128]{1,0:T(8,128)(2,1)} %constant.28.clone.spread_ref) | copy-start | bytes 6148
  67.8 1.3 copy-start.8
  69.2 34.0 %all-to-all-start = ((bf16[32,16,16,128]{3,2,1,0:T(8,128)(2,1)}), bf16[32,16,16,128]{3,2,1,0:T(8,128)(2,1)S(1)}, u32[]{:S(2)}, u32[]{:S(2)}) async-start(bf16[32,16,16,128]{3,2,1,0:T(8,128)(2,1)} %legendre_forward.2), calls=%async_computation | async-start | bytes 4194304 | tf_op jit(solution)/shard_map/all_to_all | solution.py:652
  76.6 5.0 %copy-start.4 = (s32[16]{0:T(128)S(1)}, s32[16]{0:T(128)}, u32[]{:S(2)}) copy-start(s32[16]{0:T(128)} %counts_ref.11) | copy-start | bytes 196
  112.8 32.9 %all-to-all-start.4 = ((bf16[32,16,16,128]{3,2,1,0:T(8,128)(2,1)}), bf16[32,16,16,128]{3,2,1,0:T(8,128)(2,1)S(1)}, u32[]{:S(2)}, u32[]{:S(2)}) async-start(bf16[32,16,16,128]{3,2,1,0:T(8,128)(2,1)} %get-tuple-element.15), calls=%async_computation.4 | async-start | bytes 4194304 | tf_op jit(solution)/shard_map/all_to_all | solution.py:652
  122.5 28.4 %copy-start.7 = (f32[16]{0:T(128)S(1)}, f32[16]{0:T(128)}, u32[]{:S(2)}) copy-start(f32[16]{0:T(128)} %visc_ref.3) | copy-start | bytes 196
  145.7 33.6 %all-to-all-start.2 = ((bf16[32,16,16,128]{3,2,1,0:T(8,128)(2,1)}), bf16[32,16,16,128]{3,2,1,0:T(8,128)(2,1)}, u32[]{:S(2)}, u32[]{:S(2)}) async-start(bf16[32,16,16,128]{3,2,1,0:T(8,128)(2,1)} %grid_odd.2), calls=%async_computation.2 | async-start | bytes 4194304 | tf_op jit(solution)/shard_map/all_to_all | solution.py:652
  179.4 32.9 %all-to-all-start.5 = ((bf16[32,16,16,128]{3,2,1,0:T(8,128)(2,1)}), bf16[32,16,16,128]{3,2,1,0:T(8,128)(2,1)S(1)}, u32[]{:S(2)}, u32[]{:S(2)}) async-start(bf16[32,16,16,128]{3,2,1,0:T(8,128)(2,1)} %middle_stage.3), calls=%async_computation.5 | async-start | bytes 4194304 | tf_op jit(solution)/shard_map/all_to_all | solution.py:652
  212.3 1.3 copy-start.10
  213.7 33.1 %all-to-all-start.3 = ((bf16[32,16,16,128]{3,2,1,0:T(8,128)(2,1)}), bf16[32,16,16,128]{3,2,1,0:T(8,128)(2,1)S(1)}, u32[]{:S(2)}, u32[]{:S(2)}) async-start(bf16[32,16,16,128]{3,2,1,0:T(8,128)(2,1)} %middle_stage.2), calls=%async_computation.3 | async-start | bytes 4194304 | tf_op jit(solution)/shard_map/all_to_all | solution.py:652
  256.4 32.9 %all-to-all-start.6 = ((bf16[32,16,16,128]{3,2,1,0:T(8,128)(2,1)}), bf16[32,16,16,128]{3,2,1,0:T(8,128)(2,1)S(1)}, u32[]{:S(2)}, u32[]{:S(2)}) async-start(bf16[32,16,16,128]{3,2,1,0:T(8,128)(2,1)} %get-tuple-element.16), calls=%async_computation.6 | async-start | bytes 4194304 | tf_op jit(solution)/shard_map/all_to_all | solution.py:652
  289.3 1.3 copy-start.9
  290.6 32.9 %all-to-all-start.7 = ((bf16[32,16,16,128]{3,2,1,0:T(8,128)(2,1)}), bf16[32,16,16,128]{3,2,1,0:T(8,128)(2,1)S(1)}, u32[]{:S(2)}, u32[]{:S(2)}) async-start(bf16[32,16,16,128]{3,2,1,0:T(8,128)(2,1)} %grid_odd.3), calls=%async_computation.7 | async-start | bytes 4194304 | tf_op jit(solution)/shard_map/all_to_all | solution.py:652
  304.4 28.6 %collective-permute-start.8 = (bf16[16,64,128]{2,1,0:T(8,128)(2,1)S(1)}, bf16[16,64,128]{2,1,0:T(8,128)(2,1)S(1)}, u32[]{:S(2)}, u32[]{:S(2)}) collective-permute-start(bf16[16,64,128]{2,1,0:T(8,128)(2,1)S(1)} %get-tuple-element.22.refs_4_), channel_id=1, source_target_pairs={{0,3},{1,0},{2,1},{3,2},{4,7},{5,4},{6,5},{7,6},{8,11},{9,8},{10,9... | collective-permute-start | bytes 786440 | tf_op jit(solution)/shard_map/ppermute | solution.py:658
  305.0 34.8 %collective-permute-start.7 = (bf16[16,64,128]{2,1,0:T(8,128)(2,1)S(1)}, bf16[16,64,128]{2,1,0:T(8,128)(2,1)S(1)}, u32[]{:S(2)}, u32[]{:S(2)}) collective-permute-start(bf16[16,64,128]{2,1,0:T(8,128)(2,1)S(1)} %get-tuple-element.22.refs_4_), channel_id=1, source_target_pairs={{0,2},{1,3},{2,0},{3,1},{4,6},{5,7},{6,4},{7,5},{8,10},{9,11},{10,... | collective-permute-start | bytes 786440 | tf_op jit(solution)/shard_map/ppermute | solution.py:658
  305.3 34.5 %collective-permute-start.6 = (bf16[16,64,128]{2,1,0:T(8,128)(2,1)S(1)}, bf16[16,64,128]{2,1,0:T(8,128)(2,1)S(1)}, u32[]{:S(2)}, u32[]{:S(2)}) collective-permute-start(bf16[16,64,128]{2,1,0:T(8,128)(2,1)S(1)} %get-tuple-element.22.refs_4_), channel_id=1, source_target_pairs={{0,1},{1,2},{2,3},{3,0},{4,5},{5,6},{6,7},{7,4},{8,9},{9,10},{10,1... | collective-permute-start | bytes 786440 | tf_op jit(solution)/shard_map/ppermute | solution.py:658
  332.1 7.6 %collective-permute-start.11 = (bf16[16,64,128]{2,1,0:T(8,128)(2,1)S(1)}, bf16[16,64,128]{2,1,0:T(8,128)(2,1)S(1)}, u32[]{:S(2)}, u32[]{:S(2)}) collective-permute-start(bf16[16,64,128]{2,1,0:T(8,128)(2,1)S(1)} %get-tuple-element.23.refs_8_), channel_id=1, source_target_pairs={{0,3},{1,0},{2,1},{3,2},{4,7},{5,4},{6,5},{7,6},{8,11},{9,8},{10,9... | collective-permute-start | bytes 786440 | tf_op jit(solution)/shard_map/ppermute | solution.py:658
  332.7 8.3 %collective-permute-start.10 = (bf16[16,64,128]{2,1,0:T(8,128)(2,1)S(1)}, bf16[16,64,128]{2,1,0:T(8,128)(2,1)S(1)}, u32[]{:S(2)}, u32[]{:S(2)}) collective-permute-start(bf16[16,64,128]{2,1,0:T(8,128)(2,1)S(1)} %get-tuple-element.23.refs_8_), channel_id=1, source_target_pairs={{0,2},{1,3},{2,0},{3,1},{4,6},{5,7},{6,4},{7,5},{8,10},{9,11},{10,... | collective-permute-start | bytes 786440 | tf_op jit(solution)/shard_map/ppermute | solution.py:658
  333.0 15.1 %collective-permute-start.9 = (bf16[16,64,128]{2,1,0:T(8,128)(2,1)S(1)}, bf16[16,64,128]{2,1,0:T(8,128)(2,1)S(1)}, u32[]{:S(2)}, u32[]{:S(2)}) collective-permute-start(bf16[16,64,128]{2,1,0:T(8,128)(2,1)S(1)} %get-tuple-element.23.refs_8_), channel_id=1, source_target_pairs={{0,1},{1,2},{2,3},{3,0},{4,5},{5,6},{6,7},{7,4},{8,9},{9,10},{10,1... | collective-permute-start | bytes 786440 | tf_op jit(solution)/shard_map/ppermute | solution.py:658
  333.6 14.4 %copy-start = (bf16[16,64,256]{2,1,0:T(8,128)(2,1)S(1)}, bf16[16,64,256]{2,1,0:T(8,128)(2,1)}, u32[]{:S(2)}) copy-start(bf16[16,64,256]{2,1,0:T(8,128)(2,1)} %get-tuple-element.20.refs_2_) | copy-start | bytes 1572868
  333.6 14.4 %copy-start.1 = (bf16[16,64,256]{2,1,0:T(8,128)(2,1)S(1)}, bf16[16,64,256]{2,1,0:T(8,128)(2,1)}, u32[]{:S(2)}) copy-start(bf16[16,64,256]{2,1,0:T(8,128)(2,1)} %get-tuple-element.21.refs_3_) | copy-start | bytes 1572868
  363.2 2.6 collective-permute-start.14
  363.7 4.0 %collective-permute-start.13 = (f32[16,128]{1,0:T(8,128)S(1)}, f32[16,128]{1,0:T(8,128)S(1)}, u32[]{:S(2)}, u32[]{:S(2)}) collective-permute-start(f32[16,128]{1,0:T(8,128)S(1)} %reduce_sum.9.own_ref), channel_id=1, source_target_pairs={{0,2},{1,3},{2,0},{3,1},{4,6},{5,7},{6,4},{7,5},{8,10},{9,11},{10,... | collective-permute-start | bytes 24584 | tf_op jit(solution)/shard_map/ppermute | solution.py:658
  363.9 4.6 %collective-permute-start.12 = (f32[16,128]{1,0:T(8,128)S(1)}, f32[16,128]{1,0:T(8,128)S(1)}, u32[]{:S(2)}, u32[]{:S(2)}) collective-permute-start(f32[16,128]{1,0:T(8,128)S(1)} %reduce_sum.9.own_ref), channel_id=1, source_target_pairs={{0,1},{1,2},{2,3},{3,0},{4,5},{5,6},{6,7},{7,4},{8,9},{9,10},{10,1... | collective-permute-start | bytes 24584 | tf_op jit(solution)/shard_map/ppermute | solution.py:658

commit v2 on v1

--- a/solution.py
+++ b/solution.py
@@ -142,6 +142,125 @@
         compiler_params=params(8),
         name="level_partial",
     )(coef, lev, in_hbm(probes))
+
+
+def legendre_raw_kernel(probes_ref, table_ref, out_ref, turned):
+    waves = probes_ref.shape[0]
+    rows = table_ref.shape[2]
+    for m in range(waves):
+        turned[pl.ds(slot(m), rows, stride=waves), :] = jnp.dot(
+            table_ref[m, 0], probes_ref[m, 0], preferred_element_type=F32
+        )
+    out_ref[...] = turned[...].astype(BF16).reshape(out_ref.shape)
+
+
+def legendre_raw(probes, legendre, parity):
+    waves, _, degrees, _ = probes.shape
+    lats = legendre.shape[2]
+    blocks = lats // waves
+    steps = 4
+    return pl.pallas_call(
+        legendre_raw_kernel,
+        grid=(steps,),
+        in_specs=[
+            pl.BlockSpec((waves, 1, degrees, LANES), lambda g: (0, parity, 0, 0)),
+            pl.BlockSpec((waves, 1, lats // steps, degrees), lambda g: (0, parity, g, 0)),
+        ],
+        out_specs=pl.BlockSpec((blocks // steps, waves, waves, LANES), lambda g: (g, 0, 0, 0)),
+        out_shape=hbm_result((blocks, waves, waves, LANES), BF16),
+        scratch_shapes=[pltpu.VMEM((lats // steps * waves, LANES), F32)],
+        compiler_params=params(14),
+        name="legendre_raw",
+    )(in_hbm(probes), in_hbm(legendre))
+
+
+def grid_sum_kernel(coef_ref, lev_ref, x_ref, out_ref):
+    matrix = sum_matrix(coef_ref, lev_ref)
+    blocks, _, waves, _ = x_ref.shape
+    group = lane_ids(blocks * waves) // 32
+    for k in range(4):
+        packed = None
+        for g in range(4):
+            x = x_ref[:, 4 * g + k].reshape(blocks * waves, LANES)
+            summed = jnp.dot(twice(x), matrix, preferred_element_type=F32)
+            packed = summed if g == 0 else jnp.where(group == g, summed, packed)
+        out_ref[:, k] = packed.astype(BF16).reshape(blocks, waves, LANES)
+
+
+def grid_sum(x, coef, lev):
+    blocks, lats, waves, _ = x.shape
+    steps = 4
+    return pl.pallas_call(
+        grid_sum_kernel,
+        grid=(steps,),
+        in_specs=[
+            smem_spec(),
+            smem_spec(),
+            pl.BlockSpec((blocks // steps, lats, waves, LANES), lambda g: (g, 0, 0, 0)),
+        ],
+        out_specs=pl.BlockSpec((blocks // steps, 4, waves, LANES), lambda g: (g, 0, 0, 0)),
+        out_shape=jax.ShapeDtypeStruct((blocks, 4, waves, LANES), BF16),
+        compiler_params=params(12),
+        name="grid_sum",
+    )(coef, lev, in_hbm(x))
+
+
+def grid_total_kernel(counts_ref, *refs):
+    totals = refs[:4]
+    table_ref, out_ref, operand = refs[4:]
+    real_lane = (lane_ids(HALF) & PROBES) == 0
+    group = lane_ids(HALF) // 32
+    zonal = 2 * row_ids(HALF)
+    for pair in range(2):
+        both = []
+        for k in range(2):
+            parts = [ref[:, 2 * pair + k].astype(F32) for ref in totals]
+            both.append((parts[0] + parts[1]) + (parts[2] + parts[3]))
+        lanes = slice(pair * LANES, (pair + 1) * LANES)
+        for parity in range(2):
+            masked = []
+            for k in range(2):
+                x = both[k][:, 8 * parity : 8 * parity + 8].reshape(HALF, LANES)
+                lat = 2 * pair + k
+                count = jnp.where(
+                    group < 2,
+                    jnp.where(group == 0, counts_ref[lat], counts_ref[4 + lat]),
+                    jnp.where(group == 2, counts_ref[8 + lat], counts_ref[12 + lat]),
+                )
+                factor = jnp.where(zonal + parity == 0, 1.0, 2.0)
+                masked.append(x * jnp.where(zonal + parity < count, factor, 0.0))
+            first, second = masked
+            operand[parity, :HALF, lanes] = jnp.where(
+                real_lane, first, pltpu.roll(second, PROBES, 1)
+            ).astype(BF16)
+            operand[parity, HALF:, lanes] = jnp.where(
+                real_lane, pltpu.roll(first, LANES - PROBES, 1), second
+            ).astype(BF16)
+    even = jnp.dot(table_ref[0], operand[0], preferred_element_type=F32)
+    odd = jnp.dot(table_ref[1], operand[1], preferred_element_type=F32)
+    out_ref[0] = (even + odd).astype(BF16)
+    out_ref[1] = (even - odd).astype(BF16)
+
+
+def grid_total(counts, totals, forward):
+    shape = (2, M, 2 * LANES)
+    vmem = pl.BlockSpec(memory_space=pltpu.VMEM)
+    return pl.pallas_call(
+        grid_total_kernel,
+        in_specs=[smem_spec()] + [vmem] * 5,
+        out_shape=hbm_result(shape, BF16),
+        scratch_shapes=[pltpu.VMEM(shape, BF16)],
+        compiler_params=params(12),
+        name="grid_total",
+    )(counts, *totals, forward)
+
+
+def place_matrix(coef_ref, lev_ref, taken_group):
+    rows = row_ids(LANES)
+    lanes = lane_ids(LANES)
+    hit = (rows // 32 == taken_group) & ((rows & 31) == (lanes & 31))
+    weights = jnp.where(hit, own_levels(coef_ref, lev_ref, lanes // 32), 0.0)
+    return jnp.concatenate(halves(weights), axis=0)
 
 
 def legendre_kernel(coef_ref, lev_ref, probes_ref, *refs):
@@ -258,9 +377,11 @@
 
 
 def grid_middle_kernel(
-    counts_ref, x_ref, even_ref, gain_ref, forward_ref, inverse_ref, out_ref, odd_ref,
-    operand, fields, *, masked_in, masked_out,
+    counts_ref, coef_ref, lev_ref, x_ref, even_ref, total_ref, gain_ref, forward_ref, inverse_ref,
+    out_ref, odd_ref, operand, fields, *, coupled, masked_in, masked_out,
 ):
+    if coupled:
+        place = place_matrix(coef_ref, lev_ref, pl.program_id(0))
     load_waves(counts_ref, x_ref, operand, masked_in)
     size = 256
     for r in range(0, M, size):
@@ -272,6 +393,10 @@
             kept = []
             for half, sent in enumerate((even[:, lanes] + odd[:, lanes], even[:, lanes] - odd[:, lanes])):
                 base = even_ref[0, half, rows, lanes]
+                if coupled:
+                    base = base + jnp.dot(
+                        twice(total_ref[half, rows, lanes]), place, preferred_element_type=F32
+                    )
                 longitudes = slice(half * M + r, half * M + r + size)
                 north = gain_ref[0, pair, longitudes].astype(F32) * (base + sent)
                 south = gain_ref[1, pair, longitudes].astype(F32) * (base - sent)
@@ -314,7 +439,7 @@
     return pl.BlockSpec((x.shape[0], 4, x.shape[2], LANES), lambda g: (0, g, 0, 0))
 
 
-def grid_pass(arrive, depart, counts, gain, tables, masked_in, masked_out):
+def grid_pass(arrive, depart, counts, gain, tables, coupling, masked_in, masked_out):
     forward, inverse = tables
     x_even = arrive(0)
     steps = x_even.shape[1] // 4
@@ -333,13 +458,19 @@
     )(counts, in_hbm(x_even), in_hbm(forward))
     x_odd = arrive(1)
     out_shape = hbm_result(x_odd.shape, BF16)
+    coupled, coef, lev, total = coupling(x_even)
     y_even, odd = pl.pallas_call(
-        functools.partial(grid_middle_kernel, masked_in=masked_in, masked_out=masked_out),
+        functools.partial(
+            grid_middle_kernel, coupled=coupled, masked_in=masked_in, masked_out=masked_out
+        ),
         grid=(steps,),
         in_specs=[
+            smem_spec(),
+            smem_spec(),
             smem_spec(),
             wave_block(x_odd),
             field_spec,
+            whole_spec(total.shape),
             pl.BlockSpec((2, 2, 2 * M, LANES), lambda g: (0, g, 0, 0)),
             whole_spec(forward.shape),
             whole_spec(inverse.shape),
@@ -349,7 +480,7 @@
         scratch_shapes=[operand, operand],
         compiler_params=params(24),
         name="grid_middle",
-    )(counts, x_odd, in_hbm(even), in_hbm(gain), in_hbm(forward), in_hbm(inverse))
+    )(counts, coef, lev, x_odd, in_hbm(even), in_hbm(total), in_hbm(gain), in_hbm(forward), in_hbm(inverse))
     depart(0, y_even)
     y_odd = odd_stage(counts, odd, inverse, x_odd, masked_out)
     depart(1, y_odd)
@@ -676,12 +807,10 @@
     forward = wave_tables(M)
     tables = (jnp.asarray(forward), jnp.asarray(np.ascontiguousarray(forward.transpose(0, 2, 1))))
 
-    sent = {}
-    for p in range(2):
-        partial = level_partial(probes, level_down, lev, p)
-        totals = [partial] + from_levels(partial)
-        blocks = legendre_forward(probes, totals, legendre, level_up, lev, p)
-        sent[p] = exchange(blocks)
+    sent = {0: exchange(legendre_raw(probes, legendre, 0))}
+    partial = level_partial(probes, level_down, lev, 1)
+    totals = [partial] + from_levels(partial)
+    sent[1] = exchange(legendre_forward(probes, totals, legendre, level_up, lev, 1))
 
     own_gain = lax.dynamic_slice_in_dim(background, lev_index * level_local, level_local, 2)
     own_gain = own_gain * (quad_weight / float(lon_count))[None, :, None, None]
@@ -694,7 +823,15 @@
     def depart(p, values):
         folded[p] = exchange(values)
 
-    grid_pass(lambda p: sent[p], depart, trunc_counts, gain, tables, True, False)
+    def couple_first(x):
+        partial = grid_sum(x, level_down, lev)
+        total = grid_total(trunc_counts, [partial] + from_levels(partial), tables[0])
+        return True, level_up, lev, total
+
+    def couple_none(x):
+        return False, level_up, lev, jnp.zeros((8, LANES), BF16)
+
+    grid_pass(lambda p: sent[p], depart, trunc_counts, gain, tables, couple_first, True, False)
     second = {
         p: exchange(middle_stage(folded[p], legendre, viscosity, lev, wave_first, p))
         for p in range(2)
@@ -704,7 +841,7 @@
     def depart2(p, values):
         folded2[p] = exchange(values)
 
-    grid_pass(lambda p: second[p], depart2, trunc_counts, gain, tables, False, True)
+    grid_pass(lambda p: second[p], depart2, trunc_counts, gain, tables, couple_none, False, True)
     images, lows, grams, totals = [], [], [], []
     for p in range(2):
         image, part, low = image_stage(folded2[p], legendre, level_up, level_down, lev, p)

time: 380 us -> 374 us (0.984)
  waiting for transfers between devices: 176 us -> 121 us
  blocking collectives: 13.1 us -> 47 us
  starting transfers between devices: 52.6 us -> 64.5 us
    all_to_all x8 -> x7, waiting for transfers between devices: 135 us -> 95.3 us  [exchange(): lax.all_to_all(blocks, 'lat', split_axis=0, concat_axis=0, tiled=True)]
    all_to_all x1 -> x2, blocking collectives: 13.1 us -> 47 us  [exchange(): lax.all_to_all(blocks, 'lat', split_axis=0, concat_axis=0, tiled=True)]
    ppermute x15, waiting for transfers between devices: 40.4 us -> 25.8 us  [from_levels(): lax.ppermute(part, 'lev', [(i, (i + k) % count) for i in range(count)])]
    pallas_call x2 -> x5, Pallas kernels: 19.3 us -> 33.2 us  [the longest x2 19.9 us: grid_pass(): pl.pallas_call(functools.partial(grid_middle_kernel, coupled=coupled, mas...]
    ppermute x15, starting transfers between devices: 10.5 us -> 21.8 us  [from_levels(): lax.ppermute(part, 'lev', [(i, (i + k) % count) for i in range(count)])]
    pallas_call x2 -> x1, Pallas kernels: 17.5 us -> 8.77 us  [legendre_forward(): pl.pallas_call(legendre_kernel, grid=(steps,), in_specs=[smem_spec(), sme...]
    all_to_all x8 -> x7, starting transfers between devices: 42.1 us -> 42.7 us  [exchange(): lax.all_to_all(blocks, 'lat', split_axis=0, concat_axis=0, tiled=True)]
  transfers between devices with their start and end apart: 23 -> 22, of which waited for: 19 -> 12; matrix products, arithmetic and copies ran while one was open for 0% -> 0% of each run, Pallas kernels for 23% -> 24%
where the time goes in v2:
time: 374 us; the launch traced here: 372 us
  Pallas kernels  133 us (36%)
  waiting for transfers between devices  121 us (32%)
  starting transfers between devices  64.5 us (17%)
  blocking collectives  47 us (13%)
    all_to_all x7, waiting for transfers between devices, exchange(): lax.all_to_all(blocks, 'lat', split_axis=0, concat_axis=0, tiled=True)  95.3 us
    all_to_all x2, blocking collectives, exchange(): lax.all_to_all(blocks, 'lat', split_axis=0, concat_axis=0, tiled=True)  47 us
    all_to_all x7, starting transfers between devices, exchange(): lax.all_to_all(blocks, 'lat', split_axis=0, concat_axis=0, tiled=True)  42.7 us
    ppermute x15, waiting for transfers between devices, from_levels(): lax.ppermute(part, 'lev', [(i, (i + k) % count) for i in range(count)])  25.8 us
    pallas_call x2, Pallas kernels, middle_stage(): pl.pallas_call(functools.partial(middle_kernel, parity=parity), grid=(1,)...  25.3 us
    ppermute x15, starting transfers between devices, from_levels(): lax.ppermute(part, 'lev', [(i, (i + k) % count) for i in range(count)])  21.8 us
    pallas_call x2, Pallas kernels, grid_pass(): pl.pallas_call(functools.partial(grid_middle_kernel, coupled=coupled, mas...  19.9 us
    pallas_call x2, Pallas kernels, image_stage(): pl.pallas_call(images_kernel, grid=(steps,), in_specs=[smem_spec(), smem_...  18 us
  transfers between devices with their start and end apart: 22, of which 12 were waited for; matrix products, arithmetic and copies ran while one was open for 0% of the time, Pallas kernels for 24%

profile of v2, /device:TPU:1, one launch (start us, length us, event | category | flops | bytes accessed | tf_op | source)
XLA Modules:
  0.0 371.6 jit_solution(11909558143128262623)
XLA Ops:
  0.6 5.7 %legendre_raw.1 = bf16[32,16,16,128]{3,2,1,0:T(8,128)(2,1)} custom-call(bf16[16,2,256,128]{3,2,1,0:T(8,128)(2,1)} %probes_ref.5, bf16[16,2,512,256]{3,2,1,0:T(8,128)(2,1)} %table_ref.13), custom_call_target="tpu_custom_call" | custom-call | tf_op jit(solution)/shard_map/legendre_raw/pallas_call | solution.py:162
  6.4 9.7 %all-to-all-start.1 = ((bf16[32,16,16,128]{3,2,1,0:T(8,128)(2,1)}), bf16[32,16,16,128]{3,2,1,0:T(8,128)(2,1)S(1)}, u32[]{:S(2)}, u32[]{:S(2)}) async-start(bf16[32,16,16,128]{3,2,1,0:T(8,128)(2,1)} %legendre_raw.1), calls=%async_computation.1 | async-start | bytes 4194304 | tf_op jit(solution)/shard_map/all_to_all | solution.py:783
  16.1 0.0 copy-start.5
  16.1 2.0 level_partial.1.refs_0_
  18.1 1.3 collective-permute-start
  19.4 2.4 collective-permute-start.1
  21.8 1.2 collective-permute-start.2
  23.0 4.0 %collective-permute-done.refs_1_ = bf16[16,64,128]{2,1,0:T(8,128)(2,1)S(1)} collective-permute-done((bf16[16,64,128]{2,1,0:T(8,128)(2,1)S(1)}, bf16[16,64,128]{2,1,0:T(8,128)(2,1)S(1)}, u32[]{:S(2)}, u32[]{:S(2)}) %collective-permute-start) | collective-permute-done | bytes 262176 | tf_op jit(solution)/shard_map/ppermute | solution.py:789
  27.0 6.6 %collective-permute-done.1.refs_2_ = bf16[16,64,128]{2,1,0:T(8,128)(2,1)S(1)} collective-permute-done((bf16[16,64,128]{2,1,0:T(8,128)(2,1)S(1)}, bf16[16,64,128]{2,1,0:T(8,128)(2,1)S(1)}, u32[]{:S(2)}, u32[]{:S(2)}) %collective-permute-start.1) | collective-permute-done | bytes 262176 | tf_op jit(solution)/shard_map/ppermute | solution.py:789
  33.6 8.8 %legendre_forward.1 = bf16[32,16,16,128]{3,2,1,0:T(8,128)(2,1)} custom-call(f32[16]{0:T(128)S(1)} %copy-done.5, s32[1]{0:T(128)} %bitcast.lev_ref, bf16[16,2,256,128]{3,2,1,0:T(8,128)(2,1)} %probes_ref.5, bf16[16,64,128]{2,1,0:T(8,128)(2,1)S(1)} %level_partial.1.refs_0_, bf16[16,64,128]{2,1,0:T(8,128)(2,1)S(1)} %collective-permute-done.refs_1_, ...), custom_call_target="tpu_custom_call" | custom-call | tf_op jit(solution)/shard_map/legendre_forward/pallas_call | solution.py:299
  42.4 2.0 all-to-all-done.1.x_ref
  44.4 1.4 copy-done.8
  45.8 6.0 %all-to-all-start = ((bf16[32,16,16,128]{3,2,1,0:T(8,128)(2,1)}), bf16[32,16,16,128]{3,2,1,0:T(8,128)(2,1)S(1)}, u32[]{:S(2)}, u32[]{:S(2)}) async-start(bf16[32,16,16,128]{3,2,1,0:T(8,128)(2,1)} %legendre_forward.1), calls=%async_computation | async-start | bytes 4194304 | tf_op jit(solution)/shard_map/all_to_all | solution.py:783
  51.9 0.0 copy-start.6
  51.9 4.3 %grid_sum.1.refs_0_ = bf16[32,4,16,128]{3,2,1,0:T(8,128)(2,1)} custom-call(f32[16]{0:T(128)S(1)} %copy-done.4, s32[1]{0:T(128)} %bitcast.lev_ref, bf16[32,16,16,128]{3,2,1,0:T(8,128)(2,1)} %copy-done.8), custom_call_target="tpu_custom_call" | custom-call | tf_op jit(solution)/shard_map/grid_sum/pallas_call | solution.py:193
  56.2 1.0 collective-permute-start.3
  57.3 2.1 collective-permute-start.4
  59.4 1.3 collective-permute-start.5
  60.7 1.4 multiply_convert_fusion
  62.0 0.2 copy.15
  62.3 0.1 convert_element_type.12.gain_ref
  62.4 0.0 copy-start.3
  62.4 5.0 %spread_gain.1.gain_ref = bf16[2,8,1024,128]{3,2,1,0:T(8,128)(2,1)} custom-call(bf16[2,8,8,1024]{3,2,1,0:T(8,128)(2,1)S(1)} %convert_element_type.12.gain_ref, bf16[8,128]{1,0:T(8,128)(2,1)S(1)} %copy-done.6), custom_call_target="tpu_custom_call" | custom-call | tf_op jit(solution)/shard_map/spread_gain/pallas_call | solution.py:424
  67.4 6.2 %grid_even.2.even_ref = f32[4,2,512,256]{3,2,1,0:T(8,128)} custom-call(s32[16]{0:T(128)S(1)} %copy-done.3, bf16[32,16,16,128]{3,2,1,0:T(8,128)(2,1)} %copy-done.8, bf16[2,512,512]{2,1,0:T(8,128)(2,1)} %constant.28.clone.table_ref.refs_4_.forward_ref), custom_call_target="tpu_custom_call" | custom-call | tf_op jit(solution)/shard_map/grid_even/pallas_call | solution.py:449
  73.6 9.1 %collective-permute-done.4.refs_2_ = bf16[32,4,16,128]{3,2,1,0:T(8,128)(2,1)} collective-permute-done((bf16[32,4,16,128]{3,2,1,0:T(8,128)(2,1)}, bf16[32,4,16,128]{3,2,1,0:T(8,128)(2,1)}, u32[]{:S(2)}, u32[]{:S(2)}) %collective-permute-start.4) | collective-permute-done | bytes 524320 | tf_op jit(solution)/shard_map/ppermute | solution.py:789
  82.7 3.2 grid_total.1.total_ref
  85.9 10.3 %grid_middle.2 = (bf16[32,16,16,128]{3,2,1,0:T(8,128)(2,1)}, bf16[4,2,512,256]{3,2,1,0:T(8,128)(2,1)}) custom-call(s32[16]{0:T(128)S(1)} %copy-done.3, f32[16]{0:T(128)S(1)} %copy-done.5, s32[1]{0:T(128)} %bitcast.lev_ref, bf16[32,16,16,128]{3,2,1,0:T(8,128)(2,1)S(1)} %all-to-all-done.x_ref, f32[4,2,512,256]{3,2,1,0:T(8,128)} %grid_even.2.even_ref, ...), custom_call_target="tpu_custom_call" | custom-call | tf_op jit(solution)/shard_map/grid_middle/pallas_call | solution.py:462
  96.2 8.2 %all-to-all-start.4 = ((bf16[32,16,16,128]{3,2,1,0:T(8,128)(2,1)}), bf16[32,16,16,128]{3,2,1,0:T(8,128)(2,1)S(1)}, u32[]{:S(2)}, u32[]{:S(2)}) async-start(bf16[32,16,16,128]{3,2,1,0:T(8,128)(2,1)} %get-tuple-element.15), calls=%async_computation.4 | async-start | bytes 4194304 | tf_op jit(solution)/shard_map/all_to_all | solution.py:783
  104.5 5.2 %grid_odd.2 = bf16[32,16,16,128]{3,2,1,0:T(8,128)(2,1)} custom-call(s32[16]{0:T(128)S(1)} %copy-done.3, bf16[4,2,512,256]{3,2,1,0:T(8,128)(2,1)} %get-tuple-element.14.odd_ref, bf16[2,512,512]{2,1,0:T(8,128)(2,1)} %constant.29.clone.inverse_ref.table_ref), custom_call_target="tpu_custom_call" | custom-call | tf_op jit(solution)/shard_map/grid_odd/pallas_call | solution.py:492
  109.7 23.1 %all-to-all-done.4.x_ref = bf16[32,16,16,128]{3,2,1,0:T(8,128)(2,1)S(1)} async-done(((bf16[32,16,16,128]{3,2,1,0:T(8,128)(2,1)}), bf16[32,16,16,128]{3,2,1,0:T(8,128)(2,1)S(1)}, u32[]{:S(2)}, u32[]{:S(2)}) %all-to-all-start.4) | async-done | bytes 2097184 | tf_op jit(solution)/shard_map/all_to_all | solution.py:783
  132.8 5.2 %all-to-all-start.2 = ((bf16[32,16,16,128]{3,2,1,0:T(8,128)(2,1)}), bf16[32,16,16,128]{3,2,1,0:T(8,128)(2,1)}, u32[]{:S(2)}, u32[]{:S(2)}) async-start(bf16[32,16,16,128]{3,2,1,0:T(8,128)(2,1)} %grid_odd.2), calls=%async_computation.2 | async-start | bytes 4194304 | tf_op jit(solution)/shard_map/all_to_all | solution.py:783
  138.0 12.4 %middle_stage.3 = bf16[32,16,16,128]{3,2,1,0:T(8,128)(2,1)} custom-call(s32[1]{0:T(128)} %bitcast.1.first_ref, f32[16]{0:T(128)S(1)} %copy-done.7, s32[1]{0:T(128)} %bitcast.lev_ref, bf16[32,16,16,128]{3,2,1,0:T(8,128)(2,1)S(1)} %all-to-all-done.4.x_ref, bf16[16,2,512,256]{3,2,1,0:T(8,128)(2,1)} %table_ref.13), custom_call_target="tpu_custom_call" | custom-call | tf_op jit(solution)/shard_map/middle_stage/pallas_call | solution.py:556
  150.3 16.1 %all-to-all-done.2.x_ref = bf16[32,16,16,128]{3,2,1,0:T(8,128)(2,1)} async-done(((bf16[32,16,16,128]{3,2,1,0:T(8,128)(2,1)}), bf16[32,16,16,128]{3,2,1,0:T(8,128)(2,1)}, u32[]{:S(2)}, u32[]{:S(2)}) %all-to-all-start.2) | async-done | bytes 2097184 | tf_op jit(solution)/shard_map/all_to_all | solution.py:783
  166.4 4.5 %all-to-all-start.5 = ((bf16[32,16,16,128]{3,2,1,0:T(8,128)(2,1)}), bf16[32,16,16,128]{3,2,1,0:T(8,128)(2,1)S(1)}, u32[]{:S(2)}, u32[]{:S(2)}) async-start(bf16[32,16,16,128]{3,2,1,0:T(8,128)(2,1)} %middle_stage.3), calls=%async_computation.5 | async-start | bytes 4194304 | tf_op jit(solution)/shard_map/all_to_all | solution.py:783
  170.9 13.0 %middle_stage.2 = bf16[32,16,16,128]{3,2,1,0:T(8,128)(2,1)} custom-call(s32[1]{0:T(128)} %bitcast.1.first_ref, f32[16]{0:T(128)S(1)} %copy-done.7, s32[1]{0:T(128)} %bitcast.lev_ref, bf16[32,16,16,128]{3,2,1,0:T(8,128)(2,1)} %all-to-all-done.2.x_ref, bf16[16,2,512,256]{3,2,1,0:T(8,128)(2,1)} %table_ref.13), custom_call_target="tpu_custom_call" | custom-call | tf_op jit(solution)/shard_map/middle_stage/pallas_call | solution.py:556
  183.9 15.5 %all-to-all-done.5.x_ref = bf16[32,16,16,128]{3,2,1,0:T(8,128)(2,1)S(1)} async-done(((bf16[32,16,16,128]{3,2,1,0:T(8,128)(2,1)}), bf16[32,16,16,128]{3,2,1,0:T(8,128)(2,1)S(1)}, u32[]{:S(2)}, u32[]{:S(2)}) %all-to-all-start.5) | async-done | bytes 2097184 | tf_op jit(solution)/shard_map/all_to_all | solution.py:783
  199.4 1.4 copy-done.9
  200.7 4.5 %all-to-all-start.3 = ((bf16[32,16,16,128]{3,2,1,0:T(8,128)(2,1)}), bf16[32,16,16,128]{3,2,1,0:T(8,128)(2,1)S(1)}, u32[]{:S(2)}, u32[]{:S(2)}) async-start(bf16[32,16,16,128]{3,2,1,0:T(8,128)(2,1)} %middle_stage.2), calls=%async_computation.3 | async-start | bytes 4194304 | tf_op jit(solution)/shard_map/all_to_all | solution.py:783
  205.2 5.8 %grid_even.3.even_ref = f32[4,2,512,256]{3,2,1,0:T(8,128)} custom-call(s32[16]{0:T(128)S(1)} %copy-done.3, bf16[32,16,16,128]{3,2,1,0:T(8,128)(2,1)} %copy-done.9, bf16[2,512,512]{2,1,0:T(8,128)(2,1)} %constant.28.clone.table_ref.refs_4_.forward_ref), custom_call_target="tpu_custom_call" | custom-call | tf_op jit(solution)/shard_map/grid_even/pallas_call | solution.py:449
  211.0 22.6 %all-to-all-done.3.x_ref = bf16[32,16,16,128]{3,2,1,0:T(8,128)(2,1)S(1)} async-done(((bf16[32,16,16,128]{3,2,1,0:T(8,128)(2,1)}), bf16[32,16,16,128]{3,2,1,0:T(8,128)(2,1)S(1)}, u32[]{:S(2)}, u32[]{:S(2)}) %all-to-all-start.3) | async-done | bytes 2097184 | tf_op jit(solution)/shard_map/all_to_all | solution.py:783
  233.6 0.6 broadcast_in_dim.4.total_ref
  234.2 9.6 %grid_middle.3 = (bf16[32,16,16,128]{3,2,1,0:T(8,128)(2,1)}, bf16[4,2,512,256]{3,2,1,0:T(8,128)(2,1)}) custom-call(s32[16]{0:T(128)S(1)} %copy-done.3, f32[16]{0:T(128)S(1)} %copy-done.5, s32[1]{0:T(128)} %bitcast.lev_ref, bf16[32,16,16,128]{3,2,1,0:T(8,128)(2,1)S(1)} %all-to-all-done.3.x_ref, f32[4,2,512,256]{3,2,1,0:T(8,128)} %grid_even.3.even_ref, ...), custom_call_target="tpu_custom_call" | custom-call | tf_op jit(solution)/shard_map/grid_middle/pallas_call | solution.py:462
  243.9 5.4 %grid_odd.3 = bf16[32,16,16,128]{3,2,1,0:T(8,128)(2,1)} custom-call(s32[16]{0:T(128)S(1)} %copy-done.3, bf16[4,2,512,256]{3,2,1,0:T(8,128)(2,1)} %get-tuple-element.18.odd_ref, bf16[2,512,512]{2,1,0:T(8,128)(2,1)} %constant.29.clone.inverse_ref.table_ref), custom_call_target="tpu_custom_call" | custom-call | tf_op jit(solution)/shard_map/grid_odd/pallas_call | solution.py:492
  249.2 32.7 %all_to_all.45.x_ref = bf16[32,16,16,128]{3,2,1,0:T(8,128)(2,1)S(1)} all-to-all(bf16[32,16,16,128]{3,2,1,0:T(8,128)(2,1)} %grid_odd.3), channel_id=1, replica_groups=mesh['lat'=32,'lev'=4] {'lat'}, dimensions={0} | all-to-all | bytes 4194304 | tf_op jit(solution)/shard_map/all_to_all | solution.py:783
  281.9 4.6 %all-to-all-start.6 = ((bf16[32,16,16,128]{3,2,1,0:T(8,128)(2,1)}), bf16[32,16,16,128]{3,2,1,0:T(8,128)(2,1)}, u32[]{:S(2)}, u32[]{:S(2)}) async-start(bf16[32,16,16,128]{3,2,1,0:T(8,128)(2,1)} %get-tuple-element.16), calls=%async_computation.6 | async-start | bytes 4194304 | tf_op jit(solution)/shard_map/all_to_all | solution.py:783
  286.5 8.7 %image_stage.3 = (bf16[16,256,256]{2,1,0:T(8,128)(2,1)}, bf16[16,64,128]{2,1,0:T(8,128)(2,1)S(1)}, bf16[16,64,256]{2,1,0:T(8,128)(2,1)}) custom-call(f32[16]{0:T(128)S(1)} %copy-done.5, f32[16]{0:T(128)S(1)} %copy-done.4, s32[1]{0:T(128)} %bitcast.lev_ref, bf16[32,16,16,128]{3,2,1,0:T(8,128)(2,1)S(1)} %all_to_all.45.x_ref, bf16[16,2,512,256]{3,2,1,0:T(8,128)(2,1)} %table_ref.13), custom_call_target="tpu_custom_call" | custom-call | tf_op jit(solution)/shard_map/image_stage/pallas_call | solution.py:604
  295.2 2.4 collective-permute-start.10
  297.5 1.5 collective-permute-start.11
  299.0 15.9 %all-to-all-done.6.x_ref = bf16[32,16,16,128]{3,2,1,0:T(8,128)(2,1)} async-done(((bf16[32,16,16,128]{3,2,1,0:T(8,128)(2,1)}), bf16[32,16,16,128]{3,2,1,0:T(8,128)(2,1)}, u32[]{:S(2)}, u32[]{:S(2)}) %all-to-all-start.6) | async-done | bytes 2097184 | tf_op jit(solution)/shard_map/all_to_all | solution.py:783
  314.9 9.3 %image_stage.2 = (bf16[16,256,256]{2,1,0:T(8,128)(2,1)}, bf16[16,64,128]{2,1,0:T(8,128)(2,1)S(1)}, bf16[16,64,256]{2,1,0:T(8,128)(2,1)}) custom-call(f32[16]{0:T(128)S(1)} %copy-done.5, f32[16]{0:T(128)S(1)} %copy-done.4, s32[1]{0:T(128)} %bitcast.lev_ref, bf16[32,16,16,128]{3,2,1,0:T(8,128)(2,1)} %all-to-all-done.6.x_ref, bf16[16,2,512,256]{3,2,1,0:T(8,128)(2,1)} %table_ref.13), custom_call_target="tpu_custom_call" | custom-call | tf_op jit(solution)/shard_map/image_stage/pallas_call | solution.py:604
  324.2 1.4 collective-permute-start.6
  325.6 2.1 collective-permute-start.7
  327.7 0.9 collective-permute-start.8
  328.6 3.1 gram_stage.3.refs_1_
  331.7 3.0 gram_stage.2.refs_0_
  334.8 4.2 %collective-permute-done.7.refs_6_ = bf16[16,64,128]{2,1,0:T(8,128)(2,1)S(1)} collective-permute-done((bf16[16,64,128]{2,1,0:T(8,128)(2,1)S(1)}, bf16[16,64,128]{2,1,0:T(8,128)(2,1)S(1)}, u32[]{:S(2)}, u32[]{:S(2)}) %collective-permute-start.7) | collective-permute-done | bytes 262176 | tf_op jit(solution)/shard_map/ppermute | solution.py:789
  339.0 2.1 finish_stage.1
  341.0 14.2 %all_to_all.46 = f32[32,16,128]{2,1,0:T(8,128)S(1)} all-to-all(f32[32,16,128]{2,1,0:T(8,128)} %get-tuple-element.24), channel_id=1, replica_groups=mesh['lat'=32,'lev'=4] {'lat'}, dimensions={0} | all-to-all | bytes 524288 | tf_op jit(solution)/shard_map/all_to_all | solution.py:783
  355.3 1.3 collective-permute-start.12
  356.6 2.1 collective-permute-start.13
  358.7 0.9 collective-permute-start.14
  359.6 1.0 collective-permute-done.13.two_ref
  360.6 0.9 collective-permute-done.14.three_ref
  361.5 10.1 %basis_stage.1 = (bf16[16,2,256,128]{3,2,1,0:T(8,128)(2,1)}, f32[16,16]{1,0:T(8,128)}) custom-call(f32[16]{0:T(128)S(1)} %copy-done.4, s32[1]{0:T(128)} %bitcast.lev_ref, f32[16,128]{1,0:T(8,128)S(1)} %reduce_sum.9.own_ref, f32[16,128]{1,0:T(8,128)S(1)} %collective-permute-done.12.one_ref, f32[16,128]{1,0:T(8,128)S(1)} %collective-permute-done.13.two_ref, ...), custom_call_target="tpu_custom_call" | custom-call | tf_op jit(solution)/shard_map/basis_stage/pallas_call | solution.py:758
  (30 shorter events, 0.1 us)
Async XLA Ops:
  6.4 9.8 %copy-start.4 = (f32[16]{0:T(128)S(1)}, f32[16]{0:T(128)}, u32[]{:S(2)}) copy-start(f32[16]{0:T(128)} %down_ref.7) | copy-start | bytes 196
  6.4 38.1 %all-to-all-start.1 = ((bf16[32,16,16,128]{3,2,1,0:T(8,128)(2,1)}), bf16[32,16,16,128]{3,2,1,0:T(8,128)(2,1)S(1)}, u32[]{:S(2)}, u32[]{:S(2)}) async-start(bf16[32,16,16,128]{3,2,1,0:T(8,128)(2,1)} %legendre_raw.1), calls=%async_computation.1 | async-start | bytes 4194304 | tf_op jit(solution)/shard_map/all_to_all | solution.py:783
  16.1 17.5 %copy-start.5 = (f32[16]{0:T(128)S(1)}, f32[16]{0:T(128)}, u32[]{:S(2)}) copy-start(f32[16]{0:T(128)} %up_ref.3) | copy-start | bytes 196
  18.1 8.9 %collective-permute-start = (bf16[16,64,128]{2,1,0:T(8,128)(2,1)S(1)}, bf16[16,64,128]{2,1,0:T(8,128)(2,1)S(1)}, u32[]{:S(2)}, u32[]{:S(2)}) collective-permute-start(bf16[16,64,128]{2,1,0:T(8,128)(2,1)S(1)} %level_partial.1.refs_0_), channel_id=1, source_target_pairs={{0,1},{1,2},{2,3},{3,0},{4,5},{5,6},{6,7},{7,4},{8,9},{9,10},{10,1... | collective-permute-start | bytes 786440 | tf_op jit(solution)/shard_map/ppermute | solution.py:789
  19.4 14.2 %collective-permute-start.1 = (bf16[16,64,128]{2,1,0:T(8,128)(2,1)S(1)}, bf16[16,64,128]{2,1,0:T(8,128)(2,1)S(1)}, u32[]{:S(2)}, u32[]{:S(2)}) collective-permute-start(bf16[16,64,128]{2,1,0:T(8,128)(2,1)S(1)} %level_partial.1.refs_0_), channel_id=1, source_target_pairs={{0,2},{1,3},{2,0},{3,1},{4,6},{5,7},{6,4},{7,5},{8,10},{9,11},{10,... | collective-permute-start | bytes 786440 | tf_op jit(solution)/shard_map/ppermute | solution.py:789
  21.8 11.8 %collective-permute-start.2 = (bf16[16,64,128]{2,1,0:T(8,128)(2,1)S(1)}, bf16[16,64,128]{2,1,0:T(8,128)(2,1)S(1)}, u32[]{:S(2)}, u32[]{:S(2)}) collective-permute-start(bf16[16,64,128]{2,1,0:T(8,128)(2,1)S(1)} %level_partial.1.refs_0_), channel_id=1, source_target_pairs={{0,3},{1,0},{2,1},{3,2},{4,7},{5,4},{6,5},{7,6},{8,11},{9,8},{10,9... | collective-permute-start | bytes 786440 | tf_op jit(solution)/shard_map/ppermute | solution.py:789
  44.4 1.4 copy-start.8
  45.8 40.1 %all-to-all-start = ((bf16[32,16,16,128]{3,2,1,0:T(8,128)(2,1)}), bf16[32,16,16,128]{3,2,1,0:T(8,128)(2,1)S(1)}, u32[]{:S(2)}, u32[]{:S(2)}) async-start(bf16[32,16,16,128]{3,2,1,0:T(8,128)(2,1)} %legendre_forward.1), calls=%async_computation | async-start | bytes 4194304 | tf_op jit(solution)/shard_map/all_to_all | solution.py:783
  51.9 8.8 %copy-start.10 = (f32[16]{0:T(128)S(1)}, f32[16]{0:T(128)}, u32[]{:S(2)}) copy-start(f32[16]{0:T(128)} %param.13) | copy-start | bytes 196
  51.9 10.5 %copy-start.6 = (bf16[8,128]{1,0:T(8,128)(2,1)S(1)}, bf16[8,128]{1,0:T(8,128)(2,1)}, u32[]{:S(2)}) copy-start(bf16[8,128]{1,0:T(8,128)(2,1)} %constant.30.clone.spread_ref) | copy-start | bytes 6148
  56.2 17.4 %collective-permute-start.3 = (bf16[32,4,16,128]{3,2,1,0:T(8,128)(2,1)}, bf16[32,4,16,128]{3,2,1,0:T(8,128)(2,1)}, u32[]{:S(2)}, u32[]{:S(2)}) collective-permute-start(bf16[32,4,16,128]{3,2,1,0:T(8,128)(2,1)} %grid_sum.1.refs_0_), channel_id=1, source_target_pairs={{0,1},{1,2},{2,3},{3,0},{4,5},{5,6},{6,7},{7,4},{8,9},{9,10},{10,1... | collective-permute-start | bytes 1572872 | tf_op jit(solution)/shard_map/ppermute | solution.py:789
  57.3 25.4 %collective-permute-start.4 = (bf16[32,4,16,128]{3,2,1,0:T(8,128)(2,1)}, bf16[32,4,16,128]{3,2,1,0:T(8,128)(2,1)}, u32[]{:S(2)}, u32[]{:S(2)}) collective-permute-start(bf16[32,4,16,128]{3,2,1,0:T(8,128)(2,1)} %grid_sum.1.refs_0_), channel_id=1, source_target_pairs={{0,2},{1,3},{2,0},{3,1},{4,6},{5,7},{6,4},{7,5},{8,10},{9,11},{10,... | collective-permute-start | bytes 1572872 | tf_op jit(solution)/shard_map/ppermute | solution.py:789
  59.4 23.3 %collective-permute-start.5 = (bf16[32,4,16,128]{3,2,1,0:T(8,128)(2,1)}, bf16[32,4,16,128]{3,2,1,0:T(8,128)(2,1)}, u32[]{:S(2)}, u32[]{:S(2)}) collective-permute-start(bf16[32,4,16,128]{3,2,1,0:T(8,128)(2,1)} %grid_sum.1.refs_0_), channel_id=1, source_target_pairs={{0,3},{1,0},{2,1},{3,2},{4,7},{5,4},{6,5},{7,6},{8,11},{9,8},{10,9... | collective-permute-start | bytes 1572872 | tf_op jit(solution)/shard_map/ppermute | solution.py:789
  62.4 5.0 %copy-start.3 = (s32[16]{0:T(128)S(1)}, s32[16]{0:T(128)}, u32[]{:S(2)}) copy-start(s32[16]{0:T(128)} %counts_ref.13) | copy-start | bytes 196
  67.4 15.3 %copy-start = (bf16[2,512,512]{2,1,0:T(8,128)(2,1)S(1)}, bf16[2,512,512]{2,1,0:T(8,128)(2,1)}, u32[]{:S(2)}) copy-start(bf16[2,512,512]{2,1,0:T(8,128)(2,1)} %constant.28.clone.table_ref.refs_4_.forward_ref) | copy-start | bytes 3145732
  96.2 36.6 %all-to-all-start.4 = ((bf16[32,16,16,128]{3,2,1,0:T(8,128)(2,1)}), bf16[32,16,16,128]{3,2,1,0:T(8,128)(2,1)S(1)}, u32[]{:S(2)}, u32[]{:S(2)}) async-start(bf16[32,16,16,128]{3,2,1,0:T(8,128)(2,1)} %get-tuple-element.15), calls=%async_computation.4 | async-start | bytes 4194304 | tf_op jit(solution)/shard_map/all_to_all | solution.py:783
  109.6 28.3 %copy-start.7 = (f32[16]{0:T(128)S(1)}, f32[16]{0:T(128)}, u32[]{:S(2)}) copy-start(f32[16]{0:T(128)} %visc_ref.3) | copy-start | bytes 196
  132.8 33.6 %all-to-all-start.2 = ((bf16[32,16,16,128]{3,2,1,0:T(8,128)(2,1)}), bf16[32,16,16,128]{3,2,1,0:T(8,128)(2,1)}, u32[]{:S(2)}, u32[]{:S(2)}) async-start(bf16[32,16,16,128]{3,2,1,0:T(8,128)(2,1)} %grid_odd.2), calls=%async_computation.2 | async-start | bytes 4194304 | tf_op jit(solution)/shard_map/all_to_all | solution.py:783
  166.4 32.9 %all-to-all-start.5 = ((bf16[32,16,16,128]{3,2,1,0:T(8,128)(2,1)}), bf16[32,16,16,128]{3,2,1,0:T(8,128)(2,1)S(1)}, u32[]{:S(2)}, u32[]{:S(2)}) async-start(bf16[32,16,16,128]{3,2,1,0:T(8,128)(2,1)} %middle_stage.3), calls=%async_computation.5 | async-start | bytes 4194304 | tf_op jit(solution)/shard_map/all_to_all | solution.py:783
  199.4 1.4 copy-start.9
  200.7 32.9 %all-to-all-start.3 = ((bf16[32,16,16,128]{3,2,1,0:T(8,128)(2,1)}), bf16[32,16,16,128]{3,2,1,0:T(8,128)(2,1)S(1)}, u32[]{:S(2)}, u32[]{:S(2)}) async-start(bf16[32,16,16,128]{3,2,1,0:T(8,128)(2,1)} %middle_stage.2), calls=%async_computation.3 | async-start | bytes 4194304 | tf_op jit(solution)/shard_map/all_to_all | solution.py:783
  281.9 32.9 %all-to-all-start.6 = ((bf16[32,16,16,128]{3,2,1,0:T(8,128)(2,1)}), bf16[32,16,16,128]{3,2,1,0:T(8,128)(2,1)}, u32[]{:S(2)}, u32[]{:S(2)}) async-start(bf16[32,16,16,128]{3,2,1,0:T(8,128)(2,1)} %get-tuple-element.16), calls=%async_computation.6 | async-start | bytes 4194304 | tf_op jit(solution)/shard_map/all_to_all | solution.py:783
  295.2 32.6 %collective-permute-start.10 = (bf16[16,64,128]{2,1,0:T(8,128)(2,1)S(1)}, bf16[16,64,128]{2,1,0:T(8,128)(2,1)S(1)}, u32[]{:S(2)}, u32[]{:S(2)}) collective-permute-start(bf16[16,64,128]{2,1,0:T(8,128)(2,1)S(1)} %get-tuple-element.23.refs_8_), channel_id=1, source_target_pairs={{0,2},{1,3},{2,0},{3,1},{4,6},{5,7},{6,4},{7,5},{8,10},{9,11},{10,... | collective-permute-start | bytes 786440 | tf_op jit(solution)/shard_map/ppermute | solution.py:789
  297.5 37.2 %collective-permute-start.11 = (bf16[16,64,128]{2,1,0:T(8,128)(2,1)S(1)}, bf16[16,64,128]{2,1,0:T(8,128)(2,1)S(1)}, u32[]{:S(2)}, u32[]{:S(2)}) collective-permute-start(bf16[16,64,128]{2,1,0:T(8,128)(2,1)S(1)} %get-tuple-element.23.refs_8_), channel_id=1, source_target_pairs={{0,3},{1,0},{2,1},{3,2},{4,7},{5,4},{6,5},{7,6},{8,11},{9,8},{10,9... | collective-permute-start | bytes 786440 | tf_op jit(solution)/shard_map/ppermute | solution.py:789
  299.0 35.8 %collective-permute-start.9 = (bf16[16,64,128]{2,1,0:T(8,128)(2,1)S(1)}, bf16[16,64,128]{2,1,0:T(8,128)(2,1)S(1)}, u32[]{:S(2)}, u32[]{:S(2)}) collective-permute-start(bf16[16,64,128]{2,1,0:T(8,128)(2,1)S(1)} %get-tuple-element.23.refs_8_), channel_id=1, source_target_pairs={{0,1},{1,2},{2,3},{3,0},{4,5},{5,6},{6,7},{7,4},{8,9},{9,10},{10,1... | collective-permute-start | bytes 786440 | tf_op jit(solution)/shard_map/ppermute | solution.py:789
  324.2 10.6 %collective-permute-start.6 = (bf16[16,64,128]{2,1,0:T(8,128)(2,1)S(1)}, bf16[16,64,128]{2,1,0:T(8,128)(2,1)S(1)}, u32[]{:S(2)}, u32[]{:S(2)}) collective-permute-start(bf16[16,64,128]{2,1,0:T(8,128)(2,1)S(1)} %get-tuple-element.22.refs_4_), channel_id=1, source_target_pairs={{0,1},{1,2},{2,3},{3,0},{4,5},{5,6},{6,7},{7,4},{8,9},{9,10},{10,1... | collective-permute-start | bytes 786440 | tf_op jit(solution)/shard_map/ppermute | solution.py:789
  325.6 13.3 %collective-permute-start.7 = (bf16[16,64,128]{2,1,0:T(8,128)(2,1)S(1)}, bf16[16,64,128]{2,1,0:T(8,128)(2,1)S(1)}, u32[]{:S(2)}, u32[]{:S(2)}) collective-permute-start(bf16[16,64,128]{2,1,0:T(8,128)(2,1)S(1)} %get-tuple-element.22.refs_4_), channel_id=1, source_target_pairs={{0,2},{1,3},{2,0},{3,1},{4,6},{5,7},{6,4},{7,5},{8,10},{9,11},{10,... | collective-permute-start | bytes 786440 | tf_op jit(solution)/shard_map/ppermute | solution.py:789
  327.7 11.2 %collective-permute-start.8 = (bf16[16,64,128]{2,1,0:T(8,128)(2,1)S(1)}, bf16[16,64,128]{2,1,0:T(8,128)(2,1)S(1)}, u32[]{:S(2)}, u32[]{:S(2)}) collective-permute-start(bf16[16,64,128]{2,1,0:T(8,128)(2,1)S(1)} %get-tuple-element.22.refs_4_), channel_id=1, source_target_pairs={{0,3},{1,0},{2,1},{3,2},{4,7},{5,4},{6,5},{7,6},{8,11},{9,8},{10,9... | collective-permute-start | bytes 786440 | tf_op jit(solution)/shard_map/ppermute | solution.py:789
  328.6 10.3 %copy-start.1 = (bf16[16,64,256]{2,1,0:T(8,128)(2,1)S(1)}, bf16[16,64,256]{2,1,0:T(8,128)(2,1)}, u32[]{:S(2)}) copy-start(bf16[16,64,256]{2,1,0:T(8,128)(2,1)} %get-tuple-element.21.refs_3_) | copy-start | bytes 1572868
  328.6 10.3 %copy-start.2 = (bf16[16,64,256]{2,1,0:T(8,128)(2,1)S(1)}, bf16[16,64,256]{2,1,0:T(8,128)(2,1)}, u32[]{:S(2)}) copy-start(bf16[16,64,256]{2,1,0:T(8,128)(2,1)} %get-tuple-element.20.refs_2_) | copy-start | bytes 1572868
  355.3 4.3 %collective-permute-start.12 = (f32[16,128]{1,0:T(8,128)S(1)}, f32[16,128]{1,0:T(8,128)S(1)}, u32[]{:S(2)}, u32[]{:S(2)}) collective-permute-start(f32[16,128]{1,0:T(8,128)S(1)} %reduce_sum.9.own_ref), channel_id=1, source_target_pairs={{0,1},{1,2},{2,3},{3,0},{4,5},{5,6},{6,7},{7,4},{8,9},{9,10},{10,1... | collective-permute-start | bytes 24584 | tf_op jit(solution)/shard_map/ppermute | solution.py:789
  356.6 4.0 %collective-permute-start.13 = (f32[16,128]{1,0:T(8,128)S(1)}, f32[16,128]{1,0:T(8,128)S(1)}, u32[]{:S(2)}, u32[]{:S(2)}) collective-permute-start(f32[16,128]{1,0:T(8,128)S(1)} %reduce_sum.9.own_ref), channel_id=1, source_target_pairs={{0,2},{1,3},{2,0},{3,1},{4,6},{5,7},{6,4},{7,5},{8,10},{9,11},{10,... | collective-permute-start | bytes 24584 | tf_op jit(solution)/shard_map/ppermute | solution.py:789
  358.7 2.8 collective-permute-start.14

commit v3 on v2

--- a/solution.py
+++ b/solution.py
@@ -101,16 +101,6 @@
     return jnp.where(group < 2, low, high)
 
 
-def unpack_levels(packed, matrix):
-    wide = jnp.dot(twice(packed), matrix, preferred_element_type=F32)
-    return jnp.concatenate([wide[:, g * LANES : (g + 1) * LANES] for g in range(4)], axis=0)
-
-
-def add_totals(refs, m):
-    parts = [ref[m].astype(F32) for ref in refs]
-    return ((parts[0] + parts[1]) + (parts[2] + parts[3])).astype(BF16)
-
-
 def smem_spec():
     return pl.BlockSpec(memory_space=pltpu.SMEM)
 
@@ -120,10 +110,11 @@
 
 
 def partial_kernel(coef_ref, lev_ref, probes_ref, out_ref):
-    matrix = sum_matrix(coef_ref, lev_ref)
-    for m in range(probes_ref.shape[0]):
-        summed = jnp.dot(twice(probes_ref[m, 0]), matrix, preferred_element_type=F32)
-        out_ref[m] = pack_levels(summed).astype(BF16)
+    waves, _, degrees, _ = probes_ref.shape
+    flat = probes_ref[:, 0].reshape(waves * degrees, LANES)
+    summed = jnp.dot(twice(flat), sum_matrix(coef_ref, lev_ref), preferred_element_type=F32)
+    for m in range(waves):
+        out_ref[m] = pack_levels(summed[m * degrees : (m + 1) * degrees]).astype(BF16)
 
 
 def level_partial(probes, coef, lev, parity):
@@ -158,7 +149,7 @@
     waves, _, degrees, _ = probes.shape
     lats = legendre.shape[2]
     blocks = lats // waves
-    steps = 4
+    steps = 2
     return pl.pallas_call(
         legendre_raw_kernel,
         grid=(steps,),
@@ -169,22 +160,20 @@
         out_specs=pl.BlockSpec((blocks // steps, waves, waves, LANES), lambda g: (g, 0, 0, 0)),
         out_shape=hbm_result((blocks, waves, waves, LANES), BF16),
         scratch_shapes=[pltpu.VMEM((lats // steps * waves, LANES), F32)],
-        compiler_params=params(14),
+        compiler_params=params(20),
         name="legendre_raw",
     )(in_hbm(probes), in_hbm(legendre))
 
 
 def grid_sum_kernel(coef_ref, lev_ref, x_ref, out_ref):
-    matrix = sum_matrix(coef_ref, lev_ref)
-    blocks, _, waves, _ = x_ref.shape
-    group = lane_ids(blocks * waves) // 32
-    for k in range(4):
-        packed = None
-        for g in range(4):
-            x = x_ref[:, 4 * g + k].reshape(blocks * waves, LANES)
-            summed = jnp.dot(twice(x), matrix, preferred_element_type=F32)
-            packed = summed if g == 0 else jnp.where(group == g, summed, packed)
-        out_ref[:, k] = packed.astype(BF16).reshape(blocks, waves, LANES)
+    blocks, lats, waves, _ = x_ref.shape
+    flat = x_ref[...].reshape(blocks * lats * waves, LANES)
+    summed = jnp.dot(twice(flat), sum_matrix(coef_ref, lev_ref), preferred_element_type=F32)
+    summed = summed.reshape(blocks, lats, waves, LANES)
+    group = lax.broadcasted_iota(jnp.int32, (blocks, 4, waves, LANES), 3) // 32
+    low = jnp.where(group == 0, summed[:, 0:4], summed[:, 4:8])
+    high = jnp.where(group == 2, summed[:, 8:12], summed[:, 12:16])
+    out_ref[...] = jnp.where(group < 2, low, high).astype(BF16)
 
 
 def grid_sum(x, coef, lev):
@@ -271,22 +260,26 @@
 
     @pl.when(pl.program_id(0) == 0)
     def _():
-        matrix = unpack_matrix(coef_ref, lev_ref)
-
-        def mix(m, carry):
-            total = add_totals(totals, m)
-            mixed[m] = (probes_ref[m, 0].astype(F32) + unpack_levels(total, matrix)).astype(BF16)
-            return carry
-
-        lax.fori_loop(0, waves, mix, 0, unroll=4)
-
-    def transform(m, carry):
+        parts = [ref[...].astype(F32) for ref in totals]
+        total = ((parts[0] + parts[1]) + (parts[2] + parts[3])).astype(BF16)
+        quarter = total.shape[1]
+        wide = jnp.dot(
+            twice(total.reshape(waves * quarter, LANES)),
+            unpack_matrix(coef_ref, lev_ref),
+            preferred_element_type=F32,
+        )
+        for m in range(waves):
+            for g in range(4):
+                piece = slice(g * quarter, (g + 1) * quarter)
+                mixed[m, piece] = (
+                    probes_ref[m, 0, piece].astype(F32)
+                    + wide[m * quarter : (m + 1) * quarter, g * LANES : (g + 1) * LANES]
+                ).astype(BF16)
+
+    for m in range(waves):
         turned[pl.ds(slot(m), rows, stride=waves), :] = jnp.dot(
             table_ref[m, 0], mixed[m], preferred_element_type=F32
         )
-        return carry
-
-    lax.fori_loop(0, waves, transform, 0, unroll=4)
     out_ref[...] = turned[...].astype(BF16).reshape(out_ref.shape)
 
 
@@ -294,7 +287,7 @@
     waves, _, degrees, _ = probes.shape
     lats = legendre.shape[2]
     blocks = lats // waves
-    steps = 4
+    steps = 2
     total_spec = whole_spec(totals[0].shape)
     return pl.pallas_call(
         legendre_kernel,
@@ -312,7 +305,7 @@
             pltpu.VMEM((waves, degrees, LANES), BF16),
             pltpu.VMEM((lats // steps * waves, LANES), F32),
         ],
-        compiler_params=params(14),
+        compiler_params=params(24),
         name="legendre_forward",
     )(coef, lev, in_hbm(probes), *totals, in_hbm(legendre))
 
@@ -372,14 +365,16 @@
     load_waves(counts_ref, x_ref, operand, masked)
     even = jnp.dot(table_ref[0], operand[0], preferred_element_type=F32)
     odd = jnp.dot(table_ref[1], operand[1], preferred_element_type=F32)
-    out_ref[0, 0] = even + odd
-    out_ref[0, 1] = even - odd
+    out_ref[0, 0] = (even + odd).astype(BF16)
+    out_ref[0, 1] = (even - odd).astype(BF16)
 
 
 def grid_middle_kernel(
-    counts_ref, coef_ref, lev_ref, x_ref, even_ref, total_ref, gain_ref, forward_ref, inverse_ref,
-    out_ref, odd_ref, operand, fields, *, coupled, masked_in, masked_out,
+    counts_ref, coef_ref, lev_ref, x_ref, even_ref, *refs, coupled, masked_in, masked_out
 ):
+    if coupled:
+        total_ref, refs = refs[0], refs[1:]
+    gain_ref, forward_ref, inverse_ref, out_ref, odd_ref, operand, fields = refs
     if coupled:
         place = place_matrix(coef_ref, lev_ref, pl.program_id(0))
     load_waves(counts_ref, x_ref, operand, masked_in)
@@ -392,7 +387,7 @@
             lanes = slice(pair * LANES, (pair + 1) * LANES)
             kept = []
             for half, sent in enumerate((even[:, lanes] + odd[:, lanes], even[:, lanes] - odd[:, lanes])):
-                base = even_ref[0, half, rows, lanes]
+                base = even_ref[0, half, rows, lanes].astype(F32)
                 if coupled:
                     base = base + jnp.dot(
                         twice(total_ref[half, rows, lanes]), place, preferred_element_type=F32
@@ -451,7 +446,7 @@
         grid=(steps,),
         in_specs=[smem_spec(), wave_block(x_even), whole_spec(forward.shape)],
         out_specs=field_spec,
-        out_shape=hbm_result(field_shape, F32),
+        out_shape=hbm_result(field_shape, BF16),
         scratch_shapes=[operand],
         compiler_params=params(16),
         name="grid_even",
@@ -470,7 +465,9 @@
             smem_spec(),
             wave_block(x_odd),
             field_spec,
-            whole_spec(total.shape),
+        ]
+        + [whole_spec(x.shape) for x in total]
+        + [
             pl.BlockSpec((2, 2, 2 * M, LANES), lambda g: (0, g, 0, 0)),
             whole_spec(forward.shape),
             whole_spec(inverse.shape),
@@ -480,7 +477,7 @@
         scratch_shapes=[operand, operand],
         compiler_params=params(24),
         name="grid_middle",
-    )(counts, coef, lev, x_odd, in_hbm(even), in_hbm(total), in_hbm(gain), in_hbm(forward), in_hbm(inverse))
+    )(counts, coef, lev, x_odd, in_hbm(even), *[in_hbm(x) for x in total], in_hbm(gain), in_hbm(forward), in_hbm(inverse))
     depart(0, y_even)
     y_odd = odd_stage(counts, odd, inverse, x_odd, masked_out)
     depart(1, y_odd)
@@ -684,7 +681,9 @@
         summed = summed + gram[b * PROBES : (b + 1) * PROBES]
     for shift in (64, 32, 16):
         summed = summed + pltpu.roll(summed, shift, 1)
-    gram_ref[...] = jnp.broadcast_to(summed[None], gram_ref.shape)
+    top_lane = (lane_ids(8) & PROBES) == 0
+    packed = jnp.where(top_lane, summed[:8], summed[8:])
+    gram_ref[...] = jnp.broadcast_to(packed[None], gram_ref.shape)
 
 
 def finish_stage(grams, lows, totals, down, lev, copies):
@@ -694,7 +693,7 @@
         in_specs=[smem_spec(), smem_spec()] + [pl.BlockSpec(memory_space=pltpu.VMEM)] * 12,
         out_shape=(
             hbm_result((2,) + shape, BF16),
-            hbm_result((copies, PROBES, LANES), F32),
+            hbm_result((copies, 8, LANES), F32),
         ),
         compiler_params=params(16),
         name="finish_stage",
@@ -719,12 +718,19 @@
 
 
 def basis_kernel(
-    down_ref, lev_ref, own_ref, one_ref, two_ref, three_ref, even_ref, odd_ref, total_ref,
-    out_ref, factor_ref, mix, *, row_scale,
+    own_ref, one_ref, two_ref, three_ref, full_ref, out_ref, factor_ref, mix, *, row_scale
 ):
     @pl.when(pl.program_id(0) == 0)
     def _():
-        gram = (own_ref[...] + two_ref[...]) + (one_ref[...] + three_ref[...])
+        packed = (own_ref[...] + two_ref[...]) + (one_ref[...] + three_ref[...])
+        top_lane = (lane_ids(8) & PROBES) == 0
+        gram = jnp.concatenate(
+            [
+                jnp.where(top_lane, packed, pltpu.roll(packed, PROBES, 1)),
+                jnp.where(top_lane, pltpu.roll(packed, LANES - PROBES, 1), packed),
+            ],
+            axis=0,
+        )
         upper, inverse = factor_of(gram)
         factor_ref[...] = upper[:, :PROBES] / row_scale
         pick = ((lane_ids(PROBES) & (PROBES - 1)) == row_ids(PROBES)).astype(BF16)
@@ -736,35 +742,65 @@
         mix[LANES : 2 * LANES] = mix_high
         mix[2 * LANES :] = mix_low
 
-    matrix = unpack_matrix(down_ref, lev_ref)
-    for m in range(even_ref.shape[0]):
-        for p, image_ref in enumerate((even_ref, odd_ref)):
-            both = image_ref[m]
-            full = (both[:, :LANES].astype(F32) + both[:, LANES:].astype(F32)) + unpack_levels(
-                total_ref[p, m], matrix
-            )
-            high, low = halves(full)
-            value = jnp.dot(
-                jnp.concatenate([high, low, high], axis=1), mix[...], preferred_element_type=F32
+    for m in range(full_ref.shape[0]):
+        for p in range(2):
+            both = full_ref[m, p]
+            value = jnp.dot(both, mix[: 2 * LANES], preferred_element_type=F32) + jnp.dot(
+                both[:, :LANES], mix[2 * LANES :], preferred_element_type=F32
             )
             out_ref[m, p] = value.astype(BF16)
 
 
-def basis_stage(grams, images, total, down, lev, row_scale):
+def full_kernel(down_ref, lev_ref, even_ref, odd_ref, total_ref, out_ref):
+    _, waves, quarter, _ = total_ref.shape
+    wide = jnp.dot(
+        twice(total_ref[...].reshape(2 * waves * quarter, LANES)),
+        unpack_matrix(down_ref, lev_ref),
+        preferred_element_type=F32,
+    )
+    for p, image_ref in enumerate((even_ref, odd_ref)):
+        for m in range(waves):
+            first = (p * waves + m) * quarter
+            for g in range(4):
+                piece = slice(g * quarter, (g + 1) * quarter)
+                both = image_ref[m, piece]
+                full = (both[:, :LANES].astype(F32) + both[:, LANES:].astype(F32)) + wide[
+                    first : first + quarter, g * LANES : (g + 1) * LANES
+                ]
+                out_ref[m, p, piece] = jnp.concatenate(halves(full), axis=1)
+
+
+def full_stage(images, total, down, lev):
     waves, degrees, _ = images[0].shape
     steps = 4
     count = waves // steps
     image_spec = pl.BlockSpec((count, degrees, 2 * LANES), lambda g: (g, 0, 0))
     return pl.pallas_call(
-        functools.partial(basis_kernel, row_scale=row_scale),
-        grid=(steps,),
-        in_specs=[smem_spec(), smem_spec()]
-        + [whole_spec((PROBES, LANES))] * 4
-        + [
+        full_kernel,
+        grid=(steps,),
+        in_specs=[
+            smem_spec(),
+            smem_spec(),
             image_spec,
             image_spec,
             pl.BlockSpec((2, count, degrees // 4, LANES), lambda g: (0, g, 0, 0)),
         ],
+        out_specs=pl.BlockSpec((count, 2, degrees, 2 * LANES), lambda g: (g, 0, 0, 0)),
+        out_shape=hbm_result((waves, 2, degrees, 2 * LANES), BF16),
+        compiler_params=params(14),
+        name="full_stage",
+    )(down, lev, in_hbm(images[0]), in_hbm(images[1]), in_hbm(total))
+
+
+def basis_stage(grams, full, row_scale):
+    waves, _, degrees, _ = full.shape
+    steps = 4
+    count = waves // steps
+    return pl.pallas_call(
+        functools.partial(basis_kernel, row_scale=row_scale),
+        grid=(steps,),
+        in_specs=[whole_spec((8, LANES))] * 4
+        + [pl.BlockSpec((count, 2, degrees, 2 * LANES), lambda g: (g, 0, 0, 0))],
         out_specs=(
             pl.BlockSpec((count, 2, degrees, LANES), lambda g: (g, 0, 0, 0)),
             whole_spec((PROBES, PROBES)),
@@ -776,7 +812,7 @@
         scratch_shapes=[pltpu.VMEM((3 * LANES, LANES), BF16)],
         compiler_params=params(14),
         name="basis_stage",
-    )(down, lev, *grams, in_hbm(images[0]), in_hbm(images[1]), in_hbm(total))
+    )(*grams, in_hbm(full))
 
 
 def exchange(blocks):
@@ -826,10 +862,10 @@
     def couple_first(x):
         partial = grid_sum(x, level_down, lev)
         total = grid_total(trunc_counts, [partial] + from_levels(partial), tables[0])
-        return True, level_up, lev, total
+        return True, level_up, lev, [total]
 
     def couple_none(x):
-        return False, level_up, lev, jnp.zeros((8, LANES), BF16)
+        return False, level_up, lev, []
 
     grid_pass(lambda p: sent[p], depart, trunc_counts, gain, tables, couple_first, True, False)
     second = {
@@ -850,11 +886,11 @@
         grams.append(gram_stage(image))
         totals += [part] + from_levels(part)
     total, gram_copies = finish_stage(grams, lows, totals, level_down, lev, lat_count)
-    over_lat = jnp.sum(exchange(gram_copies), axis=0)
+    received = exchange(gram_copies)
+    full = full_stage(images, total, level_down, lev)
+    over_lat = jnp.sum(received, axis=0)
     row_scale = math.sqrt(M * K * 2 * level_local * lev_count)
-    return basis_stage(
-        [over_lat] + from_levels(over_lat), images, total, level_down, lev, row_scale
-    )
+    return basis_stage([over_lat] + from_levels(over_lat), full, row_scale)
 
 
 def solution(mesh):

time: 374 us -> 364 us (0.973)
  waiting for transfers between devices: 121 us -> 157 us
  blocking collectives: 47 us -> 11.8 us
  starting transfers between devices: 64.5 us -> 56.7 us
    all_to_all x2 -> x1, blocking collectives: 47 us -> 11.8 us  [exchange(): lax.all_to_all(blocks, 'lat', split_axis=0, concat_axis=0, tiled=True)]
    all_to_all x7 -> x8, waiting for transfers between devices: 95.3 us -> 121 us  [exchange(): lax.all_to_all(blocks, 'lat', split_axis=0, concat_axis=0, tiled=True)]
    ppermute x15, starting transfers between devices: 21.8 us -> 11.6 us  [from_levels(): lax.ppermute(part, 'lev', [(i, (i + k) % count) for i in range(count)])]
    ppermute x15, waiting for transfers between devices: 25.8 us -> 35.6 us  [from_levels(): lax.ppermute(part, 'lev', [(i, (i + k) % count) for i in range(count)])]
    pallas_call x0 -> x1, Pallas kernels: none -> 5.46 us  [full_stage(): pl.pallas_call(full_kernel, grid=(steps,), in_specs=[smem_spec(), smem_sp...]
    all_to_all x7 -> x8, starting transfers between devices: 42.7 us -> 45.1 us  [exchange(): lax.all_to_all(blocks, 'lat', split_axis=0, concat_axis=0, tiled=True)]
  transfers between devices with their start and end apart: 22 -> 23, of which waited for: 12 -> 13; matrix products, arithmetic and copies ran while one was open for 0% -> 0% of each run, Pallas kernels for 24% -> 27%
where the time goes in v3:
time: 364 us; the launch traced here: 362 us
  waiting for transfers between devices  157 us (43%)
  Pallas kernels  130 us (36%)
  starting transfers between devices  56.7 us (16%)
  blocking collectives  11.8 us (3%)
  local copies, waits for them, and re-layouts  4.43 us (1%)
    all_to_all x8, waiting for transfers between devices, exchange(): lax.all_to_all(blocks, 'lat', split_axis=0, concat_axis=0, tiled=True)  121 us
    all_to_all x8, starting transfers between devices, exchange(): lax.all_to_all(blocks, 'lat', split_axis=0, concat_axis=0, tiled=True)  45.1 us
    ppermute x15, waiting for transfers between devices, from_levels(): lax.ppermute(part, 'lev', [(i, (i + k) % count) for i in range(count)])  35.6 us
    pallas_call x2, Pallas kernels, middle_stage(): pl.pallas_call(functools.partial(middle_kernel, parity=parity), grid=(1,)...  25.3 us
    pallas_call x2, Pallas kernels, grid_pass(): pl.pallas_call(functools.partial(grid_middle_kernel, coupled=coupled, mas...  19.5 us
    pallas_call x2, Pallas kernels, image_stage(): pl.pallas_call(images_kernel, grid=(steps,), in_specs=[smem_spec(), smem_...  18 us
    all_to_all x1, blocking collectives, exchange(): lax.all_to_all(blocks, 'lat', split_axis=0, concat_axis=0, tiled=True)  11.8 us
    ppermute x15, starting transfers between devices, from_levels(): lax.ppermute(part, 'lev', [(i, (i + k) % count) for i in range(count)])  11.6 us
  transfers between devices with their start and end apart: 23, of which 13 were waited for; matrix products, arithmetic and copies ran while one was open for 0% of the time, Pallas kernels for 27%

profile of v3, /device:TPU:1, one launch (start us, length us, event | category | flops | bytes accessed | tf_op | source)
XLA Modules:
  0.0 362.0 jit_solution(11997030974511033847)
XLA Ops:
  0.6 5.1 %legendre_raw.1 = bf16[32,16,16,128]{3,2,1,0:T(8,128)(2,1)} custom-call(bf16[16,2,256,128]{3,2,1,0:T(8,128)(2,1)} %probes_ref.5, bf16[16,2,512,256]{3,2,1,0:T(8,128)(2,1)} %table_ref.13), custom_call_target="tpu_custom_call" | custom-call | tf_op jit(solution)/shard_map/legendre_raw/pallas_call | solution.py:153
  5.7 9.7 %all-to-all-start.1 = ((bf16[32,16,16,128]{3,2,1,0:T(8,128)(2,1)}), bf16[32,16,16,128]{3,2,1,0:T(8,128)(2,1)S(1)}, u32[]{:S(2)}, u32[]{:S(2)}) async-start(bf16[32,16,16,128]{3,2,1,0:T(8,128)(2,1)} %legendre_raw.1), calls=%async_computation.1 | async-start | bytes 4194304 | tf_op jit(solution)/shard_map/all_to_all | solution.py:819
  15.5 2.0 level_partial.1.refs_0_
  17.5 2.5 collective-permute-start.2
  20.0 0.5 collective-permute-start.1
  20.5 0.6 collective-permute-start
  21.1 9.8 %collective-permute-done.2.refs_3_ = bf16[16,64,128]{2,1,0:T(8,128)(2,1)S(1)} collective-permute-done((bf16[16,64,128]{2,1,0:T(8,128)(2,1)S(1)}, bf16[16,64,128]{2,1,0:T(8,128)(2,1)S(1)}, u32[]{:S(2)}, u32[]{:S(2)}) %collective-permute-start.2) | collective-permute-done | bytes 262176 | tf_op jit(solution)/shard_map/ppermute | solution.py:825
  30.9 4.4 %collective-permute-done.refs_1_ = bf16[16,64,128]{2,1,0:T(8,128)(2,1)S(1)} collective-permute-done((bf16[16,64,128]{2,1,0:T(8,128)(2,1)S(1)}, bf16[16,64,128]{2,1,0:T(8,128)(2,1)S(1)}, u32[]{:S(2)}, u32[]{:S(2)}) %collective-permute-start) | collective-permute-done | bytes 262176 | tf_op jit(solution)/shard_map/ppermute | solution.py:825
  35.4 5.5 %legendre_forward.1 = bf16[32,16,16,128]{3,2,1,0:T(8,128)(2,1)} custom-call(f32[16]{0:T(128)S(1)} %copy-done.5, s32[1]{0:T(128)} %bitcast.lev_ref, bf16[16,2,256,128]{3,2,1,0:T(8,128)(2,1)} %probes_ref.5, bf16[16,64,128]{2,1,0:T(8,128)(2,1)S(1)} %level_partial.1.refs_0_, bf16[16,64,128]{2,1,0:T(8,128)(2,1)S(1)} %collective-permute-done.refs_1_, ...), custom_call_target="tpu_custom_call" | custom-call | tf_op jit(solution)/shard_map/legendre_forward/pallas_call | solution.py:292
  40.9 2.9 all-to-all-done.1.x_ref
  43.8 1.3 copy-done.8
  45.1 4.6 %all-to-all-start = ((bf16[32,16,16,128]{3,2,1,0:T(8,128)(2,1)}), bf16[32,16,16,128]{3,2,1,0:T(8,128)(2,1)S(1)}, u32[]{:S(2)}, u32[]{:S(2)}) async-start(bf16[32,16,16,128]{3,2,1,0:T(8,128)(2,1)} %legendre_forward.1), calls=%async_computation | async-start | bytes 4194304 | tf_op jit(solution)/shard_map/all_to_all | solution.py:819
  49.8 4.3 %grid_sum.1.refs_0_ = bf16[32,4,16,128]{3,2,1,0:T(8,128)(2,1)} custom-call(f32[16]{0:T(128)S(1)} %copy-done.4, s32[1]{0:T(128)} %bitcast.lev_ref, bf16[32,16,16,128]{3,2,1,0:T(8,128)(2,1)} %copy-done.8), custom_call_target="tpu_custom_call" | custom-call | tf_op jit(solution)/shard_map/grid_sum/pallas_call | solution.py:182
  54.1 2.3 collective-permute-start.5
  56.4 0.5 collective-permute-start.4
  56.9 0.6 collective-permute-start.3
  57.5 1.4 multiply_convert_fusion
  58.9 0.2 copy.15
  59.2 0.1 convert_element_type.12.gain_ref
  59.3 5.0 %spread_gain.1.refs_1_.refs_0_ = bf16[2,8,1024,128]{3,2,1,0:T(8,128)(2,1)} custom-call(bf16[2,8,8,1024]{3,2,1,0:T(8,128)(2,1)S(1)} %convert_element_type.12.gain_ref, bf16[8,128]{1,0:T(8,128)(2,1)S(1)} %copy-done.6), custom_call_target="tpu_custom_call" | custom-call | tf_op jit(solution)/shard_map/spread_gain/pallas_call | solution.py:419
  64.3 5.7 %grid_even.2.even_ref = bf16[4,2,512,256]{3,2,1,0:T(8,128)(2,1)} custom-call(s32[16]{0:T(128)S(1)} %copy-done.3, bf16[32,16,16,128]{3,2,1,0:T(8,128)(2,1)} %copy-done.8, bf16[2,512,512]{2,1,0:T(8,128)(2,1)} %constant.26.clone.table_ref.refs_4_.refs_2_.refs_1_), custom_call_target="tpu_custom_call" | custom-call | tf_op jit(solution)/shard_map/grid_even/pallas_call | solution.py:444
  70.0 1.1 collective-permute-done.4.refs_2_
  71.1 12.2 %collective-permute-done.3.refs_1_ = bf16[32,4,16,128]{3,2,1,0:T(8,128)(2,1)} collective-permute-done((bf16[32,4,16,128]{3,2,1,0:T(8,128)(2,1)}, bf16[32,4,16,128]{3,2,1,0:T(8,128)(2,1)}, u32[]{:S(2)}, u32[]{:S(2)}) %collective-permute-start.3) | collective-permute-done | bytes 524320 | tf_op jit(solution)/shard_map/ppermute | solution.py:825
  83.3 3.3 grid_total.1.refs_0_
  86.6 10.1 %grid_middle.2 = (bf16[32,16,16,128]{3,2,1,0:T(8,128)(2,1)}, bf16[4,2,512,256]{3,2,1,0:T(8,128)(2,1)}) custom-call(s32[16]{0:T(128)S(1)} %copy-done.3, f32[16]{0:T(128)S(1)} %copy-done.5, s32[1]{0:T(128)} %bitcast.lev_ref, bf16[32,16,16,128]{3,2,1,0:T(8,128)(2,1)S(1)} %all-to-all-done.x_ref, bf16[4,2,512,256]{3,2,1,0:T(8,128)(2,1)} %grid_even.2.even_ref, ...), custom_call_target="tpu_custom_call" | custom-call | tf_op jit(solution)/shard_map/grid_middle/pallas_call | solution.py:457
  96.7 7.6 %all-to-all-start.4 = ((bf16[32,16,16,128]{3,2,1,0:T(8,128)(2,1)}), bf16[32,16,16,128]{3,2,1,0:T(8,128)(2,1)S(1)}, u32[]{:S(2)}, u32[]{:S(2)}) async-start(bf16[32,16,16,128]{3,2,1,0:T(8,128)(2,1)} %get-tuple-element.15), calls=%async_computation.4 | async-start | bytes 4194304 | tf_op jit(solution)/shard_map/all_to_all | solution.py:819
  104.3 5.2 %grid_odd.2 = bf16[32,16,16,128]{3,2,1,0:T(8,128)(2,1)} custom-call(s32[16]{0:T(128)S(1)} %copy-done.3, bf16[4,2,512,256]{3,2,1,0:T(8,128)(2,1)} %get-tuple-element.14.odd_ref, bf16[2,512,512]{2,1,0:T(8,128)(2,1)} %constant.27.clone.refs_3_.table_ref.refs_2_), custom_call_target="tpu_custom_call" | custom-call | tf_op jit(solution)/shard_map/grid_odd/pallas_call | solution.py:489
  109.5 23.1 %all-to-all-done.4.x_ref = bf16[32,16,16,128]{3,2,1,0:T(8,128)(2,1)S(1)} async-done(((bf16[32,16,16,128]{3,2,1,0:T(8,128)(2,1)}), bf16[32,16,16,128]{3,2,1,0:T(8,128)(2,1)S(1)}, u32[]{:S(2)}, u32[]{:S(2)}) %all-to-all-start.4) | async-done | bytes 2097184 | tf_op jit(solution)/shard_map/all_to_all | solution.py:819
  132.6 5.2 %all-to-all-start.2 = ((bf16[32,16,16,128]{3,2,1,0:T(8,128)(2,1)}), bf16[32,16,16,128]{3,2,1,0:T(8,128)(2,1)}, u32[]{:S(2)}, u32[]{:S(2)}) async-start(bf16[32,16,16,128]{3,2,1,0:T(8,128)(2,1)} %grid_odd.2), calls=%async_computation.2 | async-start | bytes 4194304 | tf_op jit(solution)/shard_map/all_to_all | solution.py:819
  137.8 12.3 %middle_stage.3 = bf16[32,16,16,128]{3,2,1,0:T(8,128)(2,1)} custom-call(s32[1]{0:T(128)} %bitcast.1.first_ref, f32[16]{0:T(128)S(1)} %copy-done.7, s32[1]{0:T(128)} %bitcast.lev_ref, bf16[32,16,16,128]{3,2,1,0:T(8,128)(2,1)S(1)} %all-to-all-done.4.x_ref, bf16[16,2,512,256]{3,2,1,0:T(8,128)(2,1)} %table_ref.13), custom_call_target="tpu_custom_call" | custom-call | tf_op jit(solution)/shard_map/middle_stage/pallas_call | solution.py:553
  150.2 16.1 %all-to-all-done.2.x_ref = bf16[32,16,16,128]{3,2,1,0:T(8,128)(2,1)} async-done(((bf16[32,16,16,128]{3,2,1,0:T(8,128)(2,1)}), bf16[32,16,16,128]{3,2,1,0:T(8,128)(2,1)}, u32[]{:S(2)}, u32[]{:S(2)}) %all-to-all-start.2) | async-done | bytes 2097184 | tf_op jit(solution)/shard_map/all_to_all | solution.py:819
  166.3 4.5 %all-to-all-start.5 = ((bf16[32,16,16,128]{3,2,1,0:T(8,128)(2,1)}), bf16[32,16,16,128]{3,2,1,0:T(8,128)(2,1)S(1)}, u32[]{:S(2)}, u32[]{:S(2)}) async-start(bf16[32,16,16,128]{3,2,1,0:T(8,128)(2,1)} %middle_stage.3), calls=%async_computation.5 | async-start | bytes 4194304 | tf_op jit(solution)/shard_map/all_to_all | solution.py:819
  170.8 13.0 %middle_stage.2 = bf16[32,16,16,128]{3,2,1,0:T(8,128)(2,1)} custom-call(s32[1]{0:T(128)} %bitcast.1.first_ref, f32[16]{0:T(128)S(1)} %copy-done.7, s32[1]{0:T(128)} %bitcast.lev_ref, bf16[32,16,16,128]{3,2,1,0:T(8,128)(2,1)} %all-to-all-done.2.x_ref, bf16[16,2,512,256]{3,2,1,0:T(8,128)(2,1)} %table_ref.13), custom_call_target="tpu_custom_call" | custom-call | tf_op jit(solution)/shard_map/middle_stage/pallas_call | solution.py:553
  183.7 15.5 %all-to-all-done.5.x_ref = bf16[32,16,16,128]{3,2,1,0:T(8,128)(2,1)S(1)} async-done(((bf16[32,16,16,128]{3,2,1,0:T(8,128)(2,1)}), bf16[32,16,16,128]{3,2,1,0:T(8,128)(2,1)S(1)}, u32[]{:S(2)}, u32[]{:S(2)}) %all-to-all-start.5) | async-done | bytes 2097184 | tf_op jit(solution)/shard_map/all_to_all | solution.py:819
  199.2 1.4 copy-done.9
  200.6 4.5 %all-to-all-start.3 = ((bf16[32,16,16,128]{3,2,1,0:T(8,128)(2,1)}), bf16[32,16,16,128]{3,2,1,0:T(8,128)(2,1)S(1)}, u32[]{:S(2)}, u32[]{:S(2)}) async-start(bf16[32,16,16,128]{3,2,1,0:T(8,128)(2,1)} %middle_stage.2), calls=%async_computation.3 | async-start | bytes 4194304 | tf_op jit(solution)/shard_map/all_to_all | solution.py:819
  205.1 5.4 %grid_even.3.even_ref = bf16[4,2,512,256]{3,2,1,0:T(8,128)(2,1)} custom-call(s32[16]{0:T(128)S(1)} %copy-done.3, bf16[32,16,16,128]{3,2,1,0:T(8,128)(2,1)} %copy-done.9, bf16[2,512,512]{2,1,0:T(8,128)(2,1)} %constant.26.clone.table_ref.refs_4_.refs_2_.refs_1_), custom_call_target="tpu_custom_call" | custom-call | tf_op jit(solution)/shard_map/grid_even/pallas_call | solution.py:444
  210.5 23.0 %all-to-all-done.3.x_ref = bf16[32,16,16,128]{3,2,1,0:T(8,128)(2,1)S(1)} async-done(((bf16[32,16,16,128]{3,2,1,0:T(8,128)(2,1)}), bf16[32,16,16,128]{3,2,1,0:T(8,128)(2,1)S(1)}, u32[]{:S(2)}, u32[]{:S(2)}) %all-to-all-start.3) | async-done | bytes 2097184 | tf_op jit(solution)/shard_map/all_to_all | solution.py:819
  233.5 9.4 %grid_middle.3 = (bf16[32,16,16,128]{3,2,1,0:T(8,128)(2,1)}, bf16[4,2,512,256]{3,2,1,0:T(8,128)(2,1)}) custom-call(s32[16]{0:T(128)S(1)} %copy-done.3, f32[16]{0:T(128)S(1)} %copy-done.5, s32[1]{0:T(128)} %bitcast.lev_ref, bf16[32,16,16,128]{3,2,1,0:T(8,128)(2,1)S(1)} %all-to-all-done.3.x_ref, bf16[4,2,512,256]{3,2,1,0:T(8,128)(2,1)} %grid_even.3.even_ref, ...), custom_call_target="tpu_custom_call" | custom-call | tf_op jit(solution)/shard_map/grid_middle/pallas_call | solution.py:457
  242.9 4.5 %all-to-all-start.6 = ((bf16[32,16,16,128]{3,2,1,0:T(8,128)(2,1)}), bf16[32,16,16,128]{3,2,1,0:T(8,128)(2,1)S(1)}, u32[]{:S(2)}, u32[]{:S(2)}) async-start(bf16[32,16,16,128]{3,2,1,0:T(8,128)(2,1)} %get-tuple-element.16), calls=%async_computation.6 | async-start | bytes 4194304 | tf_op jit(solution)/shard_map/all_to_all | solution.py:819
  247.4 5.4 %grid_odd.3 = bf16[32,16,16,128]{3,2,1,0:T(8,128)(2,1)} custom-call(s32[16]{0:T(128)S(1)} %copy-done.3, bf16[4,2,512,256]{3,2,1,0:T(8,128)(2,1)} %get-tuple-element.18.odd_ref, bf16[2,512,512]{2,1,0:T(8,128)(2,1)} %constant.27.clone.refs_3_.table_ref.refs_2_), custom_call_target="tpu_custom_call" | custom-call | tf_op jit(solution)/shard_map/grid_odd/pallas_call | solution.py:489
  252.8 23.0 %all-to-all-done.6.x_ref = bf16[32,16,16,128]{3,2,1,0:T(8,128)(2,1)S(1)} async-done(((bf16[32,16,16,128]{3,2,1,0:T(8,128)(2,1)}), bf16[32,16,16,128]{3,2,1,0:T(8,128)(2,1)S(1)}, u32[]{:S(2)}, u32[]{:S(2)}) %all-to-all-start.6) | async-done | bytes 2097184 | tf_op jit(solution)/shard_map/all_to_all | solution.py:819
  275.8 1.3 copy-done.10
  277.1 4.5 %all-to-all-start.7 = ((bf16[32,16,16,128]{3,2,1,0:T(8,128)(2,1)}), bf16[32,16,16,128]{3,2,1,0:T(8,128)(2,1)S(1)}, u32[]{:S(2)}, u32[]{:S(2)}) async-start(bf16[32,16,16,128]{3,2,1,0:T(8,128)(2,1)} %grid_odd.3), calls=%async_computation.7 | async-start | bytes 4194304 | tf_op jit(solution)/shard_map/all_to_all | solution.py:819
  281.6 9.3 %image_stage.2 = (bf16[16,256,256]{2,1,0:T(8,128)(2,1)}, bf16[16,64,128]{2,1,0:T(8,128)(2,1)S(1)}, bf16[16,64,256]{2,1,0:T(8,128)(2,1)}) custom-call(f32[16]{0:T(128)S(1)} %copy-done.5, f32[16]{0:T(128)S(1)} %copy-done.4, s32[1]{0:T(128)} %bitcast.lev_ref, bf16[32,16,16,128]{3,2,1,0:T(8,128)(2,1)} %copy-done.10, bf16[16,2,512,256]{3,2,1,0:T(8,128)(2,1)} %table_ref.13), custom_call_target="tpu_custom_call" | custom-call | tf_op jit(solution)/shard_map/image_stage/pallas_call | solution.py:601
  291.0 0.3 collective-permute-start.8
  291.3 0.5 collective-permute-start.7
  291.8 0.6 collective-permute-start.6
  292.5 17.6 %all-to-all-done.7.x_ref = bf16[32,16,16,128]{3,2,1,0:T(8,128)(2,1)S(1)} async-done(((bf16[32,16,16,128]{3,2,1,0:T(8,128)(2,1)}), bf16[32,16,16,128]{3,2,1,0:T(8,128)(2,1)S(1)}, u32[]{:S(2)}, u32[]{:S(2)}) %all-to-all-start.7) | async-done | bytes 2097184 | tf_op jit(solution)/shard_map/all_to_all | solution.py:819
  310.1 8.6 %image_stage.3 = (bf16[16,256,256]{2,1,0:T(8,128)(2,1)}, bf16[16,64,128]{2,1,0:T(8,128)(2,1)S(1)}, bf16[16,64,256]{2,1,0:T(8,128)(2,1)}) custom-call(f32[16]{0:T(128)S(1)} %copy-done.5, f32[16]{0:T(128)S(1)} %copy-done.4, s32[1]{0:T(128)} %bitcast.lev_ref, bf16[32,16,16,128]{3,2,1,0:T(8,128)(2,1)S(1)} %all-to-all-done.7.x_ref, ...), custom_call_target="tpu_custom_call" | custom-call | tf_op jit(solution)/shard_map/image_stage/pallas_call | solution.py:601
  318.7 0.3 collective-permute-start.11
  319.0 0.5 collective-permute-start.10
  319.5 0.6 collective-permute-start.9
  320.2 3.1 gram_stage.2.refs_0_
  323.3 3.0 gram_stage.3.refs_1_
  326.3 1.0 collective-permute-done.10.refs_10_
  327.3 7.0 %collective-permute-done.9.refs_9_ = bf16[16,64,128]{2,1,0:T(8,128)(2,1)S(1)} collective-permute-done((bf16[16,64,128]{2,1,0:T(8,128)(2,1)S(1)}, bf16[16,64,128]{2,1,0:T(8,128)(2,1)S(1)}, u32[]{:S(2)}, u32[]{:S(2)}) %collective-permute-start.9) | collective-permute-done | bytes 262176 | tf_op jit(solution)/shard_map/ppermute | solution.py:825
  334.4 2.0 finish_stage.1
  336.4 11.8 %all_to_all.45 = f32[32,8,128]{2,1,0:T(8,128)S(1)} all-to-all(f32[32,8,128]{2,1,0:T(8,128)} %get-tuple-element.24), channel_id=1, replica_groups=mesh['lat'=32,'lev'=4] {'lat'}, dimensions={0} | all-to-all | bytes 262144 | tf_op jit(solution)/shard_map/all_to_all | solution.py:819
  348.2 0.6 collective-permute-start.14
  348.8 0.3 collective-permute-start.13
  349.1 0.6 collective-permute-start.12
  349.7 5.5 %full_stage.1.full_ref = bf16[16,2,256,256]{3,2,1,0:T(8,128)(2,1)} custom-call(f32[16]{0:T(128)S(1)} %copy-done.4, s32[1]{0:T(128)} %bitcast.lev_ref, bf16[16,256,256]{2,1,0:T(8,128)(2,1)} %get-tuple-element.17.image_ref.even_ref, bf16[16,256,256]{2,1,0:T(8,128)(2,1)} %get-tuple-element.19.image_ref.odd_ref, bf16[2,16,64,128]{3,2,1,0:T(8,128)(2,1)} %get-tuple-element.25.total_ref), custom_call_target="tpu_custom_call" | custom-call | tf_op jit(solution)/shard_map/full_stage/pallas_call | solution.py:778
  355.2 6.9 %basis_stage.1 = (bf16[16,2,256,128]{3,2,1,0:T(8,128)(2,1)}, f32[16,16]{1,0:T(8,128)}) custom-call(f32[8,128]{1,0:T(8,128)S(1)} %reduce_sum.9.own_ref, f32[8,128]{1,0:T(8,128)S(1)} %collective-permute-done.12.one_ref, f32[8,128]{1,0:T(8,128)S(1)} %collective-permute-done.13.two_ref, f32[8,128]{1,0:T(8,128)S(1)} %collective-permute-done.14.three_ref, ...), custom_call_target="tpu_custom_call" | custom-call | tf_op jit(solution)/shard_map/basis_stage/pallas_call | solution.py:799
  (33 shorter events, 0.1 us)
Async XLA Ops:
  5.7 9.8 %copy-start.4 = (f32[16]{0:T(128)S(1)}, f32[16]{0:T(128)}, u32[]{:S(2)}) copy-start(f32[16]{0:T(128)} %down_ref.7) | copy-start | bytes 196
  5.7 38.1 %all-to-all-start.1 = ((bf16[32,16,16,128]{3,2,1,0:T(8,128)(2,1)}), bf16[32,16,16,128]{3,2,1,0:T(8,128)(2,1)S(1)}, u32[]{:S(2)}, u32[]{:S(2)}) async-start(bf16[32,16,16,128]{3,2,1,0:T(8,128)(2,1)} %legendre_raw.1), calls=%async_computation.1 | async-start | bytes 4194304 | tf_op jit(solution)/shard_map/all_to_all | solution.py:819
  15.4 19.9 %copy-start.5 = (f32[16]{0:T(128)S(1)}, f32[16]{0:T(128)}, u32[]{:S(2)}) copy-start(f32[16]{0:T(128)} %up_ref.3) | copy-start | bytes 196
  17.5 13.4 %collective-permute-start.2 = (bf16[16,64,128]{2,1,0:T(8,128)(2,1)S(1)}, bf16[16,64,128]{2,1,0:T(8,128)(2,1)S(1)}, u32[]{:S(2)}, u32[]{:S(2)}) collective-permute-start(bf16[16,64,128]{2,1,0:T(8,128)(2,1)S(1)} %level_partial.1.refs_0_), channel_id=1, source_target_pairs={{0,3},{1,0},{2,1},{3,2},{4,7},{5,4},{6,5},{7,6},{8,11},{9,8},{10,9... | collective-permute-start | bytes 786440 | tf_op jit(solution)/shard_map/ppermute | solution.py:825
  20.0 10.9 %collective-permute-start.1 = (bf16[16,64,128]{2,1,0:T(8,128)(2,1)S(1)}, bf16[16,64,128]{2,1,0:T(8,128)(2,1)S(1)}, u32[]{:S(2)}, u32[]{:S(2)}) collective-permute-start(bf16[16,64,128]{2,1,0:T(8,128)(2,1)S(1)} %level_partial.1.refs_0_), channel_id=1, source_target_pairs={{0,2},{1,3},{2,0},{3,1},{4,6},{5,7},{6,4},{7,5},{8,10},{9,11},{10,... | collective-permute-start | bytes 786440 | tf_op jit(solution)/shard_map/ppermute | solution.py:825
  20.5 14.8 %collective-permute-start = (bf16[16,64,128]{2,1,0:T(8,128)(2,1)S(1)}, bf16[16,64,128]{2,1,0:T(8,128)(2,1)S(1)}, u32[]{:S(2)}, u32[]{:S(2)}) collective-permute-start(bf16[16,64,128]{2,1,0:T(8,128)(2,1)S(1)} %level_partial.1.refs_0_), channel_id=1, source_target_pairs={{0,1},{1,2},{2,3},{3,0},{4,5},{5,6},{6,7},{7,4},{8,9},{9,10},{10,1... | collective-permute-start | bytes 786440 | tf_op jit(solution)/shard_map/ppermute | solution.py:825
  43.8 1.3 copy-start.8
  45.1 41.5 %all-to-all-start = ((bf16[32,16,16,128]{3,2,1,0:T(8,128)(2,1)}), bf16[32,16,16,128]{3,2,1,0:T(8,128)(2,1)S(1)}, u32[]{:S(2)}, u32[]{:S(2)}) async-start(bf16[32,16,16,128]{3,2,1,0:T(8,128)(2,1)} %legendre_forward.1), calls=%async_computation | async-start | bytes 4194304 | tf_op jit(solution)/shard_map/all_to_all | solution.py:819
  49.7 7.8 %copy-start.11 = (f32[16]{0:T(128)S(1)}, f32[16]{0:T(128)}, u32[]{:S(2)}) copy-start(f32[16]{0:T(128)} %param.13) | copy-start | bytes 196
  49.7 9.5 %copy-start.6 = (bf16[8,128]{1,0:T(8,128)(2,1)S(1)}, bf16[8,128]{1,0:T(8,128)(2,1)}, u32[]{:S(2)}) copy-start(bf16[8,128]{1,0:T(8,128)(2,1)} %constant.28.clone.spread_ref) | copy-start | bytes 6148
  54.1 16.0 %collective-permute-start.5 = (bf16[32,4,16,128]{3,2,1,0:T(8,128)(2,1)}, bf16[32,4,16,128]{3,2,1,0:T(8,128)(2,1)}, u32[]{:S(2)}, u32[]{:S(2)}) collective-permute-start(bf16[32,4,16,128]{3,2,1,0:T(8,128)(2,1)} %grid_sum.1.refs_0_), channel_id=1, source_target_pairs={{0,3},{1,0},{2,1},{3,2},{4,7},{5,4},{6,5},{7,6},{8,11},{9,8},{10,9... | collective-permute-start | bytes 1572872 | tf_op jit(solution)/shard_map/ppermute | solution.py:825
  56.4 14.7 %collective-permute-start.4 = (bf16[32,4,16,128]{3,2,1,0:T(8,128)(2,1)}, bf16[32,4,16,128]{3,2,1,0:T(8,128)(2,1)}, u32[]{:S(2)}, u32[]{:S(2)}) collective-permute-start(bf16[32,4,16,128]{3,2,1,0:T(8,128)(2,1)} %grid_sum.1.refs_0_), channel_id=1, source_target_pairs={{0,2},{1,3},{2,0},{3,1},{4,6},{5,7},{6,4},{7,5},{8,10},{9,11},{10,... | collective-permute-start | bytes 1572872 | tf_op jit(solution)/shard_map/ppermute | solution.py:825
  56.9 26.4 %collective-permute-start.3 = (bf16[32,4,16,128]{3,2,1,0:T(8,128)(2,1)}, bf16[32,4,16,128]{3,2,1,0:T(8,128)(2,1)}, u32[]{:S(2)}, u32[]{:S(2)}) collective-permute-start(bf16[32,4,16,128]{3,2,1,0:T(8,128)(2,1)} %grid_sum.1.refs_0_), channel_id=1, source_target_pairs={{0,1},{1,2},{2,3},{3,0},{4,5},{5,6},{6,7},{7,4},{8,9},{9,10},{10,1... | collective-permute-start | bytes 1572872 | tf_op jit(solution)/shard_map/ppermute | solution.py:825
  59.3 5.0 %copy-start.3 = (s32[16]{0:T(128)S(1)}, s32[16]{0:T(128)}, u32[]{:S(2)}) copy-start(s32[16]{0:T(128)} %counts_ref.13) | copy-start | bytes 196
  64.3 19.0 %copy-start = (bf16[2,512,512]{2,1,0:T(8,128)(2,1)S(1)}, bf16[2,512,512]{2,1,0:T(8,128)(2,1)}, u32[]{:S(2)}) copy-start(bf16[2,512,512]{2,1,0:T(8,128)(2,1)} %constant.26.clone.table_ref.refs_4_.refs_2_.refs_1_) | copy-start | bytes 3145732
  96.7 36.0 %all-to-all-start.4 = ((bf16[32,16,16,128]{3,2,1,0:T(8,128)(2,1)}), bf16[32,16,16,128]{3,2,1,0:T(8,128)(2,1)S(1)}, u32[]{:S(2)}, u32[]{:S(2)}) async-start(bf16[32,16,16,128]{3,2,1,0:T(8,128)(2,1)} %get-tuple-element.15), calls=%async_computation.4 | async-start | bytes 4194304 | tf_op jit(solution)/shard_map/all_to_all | solution.py:819
  109.5 28.3 %copy-start.7 = (f32[16]{0:T(128)S(1)}, f32[16]{0:T(128)}, u32[]{:S(2)}) copy-start(f32[16]{0:T(128)} %visc_ref.3) | copy-start | bytes 196
  132.6 33.6 %all-to-all-start.2 = ((bf16[32,16,16,128]{3,2,1,0:T(8,128)(2,1)}), bf16[32,16,16,128]{3,2,1,0:T(8,128)(2,1)}, u32[]{:S(2)}, u32[]{:S(2)}) async-start(bf16[32,16,16,128]{3,2,1,0:T(8,128)(2,1)} %grid_odd.2), calls=%async_computation.2 | async-start | bytes 4194304 | tf_op jit(solution)/shard_map/all_to_all | solution.py:819
  166.3 32.9 %all-to-all-start.5 = ((bf16[32,16,16,128]{3,2,1,0:T(8,128)(2,1)}), bf16[32,16,16,128]{3,2,1,0:T(8,128)(2,1)S(1)}, u32[]{:S(2)}, u32[]{:S(2)}) async-start(bf16[32,16,16,128]{3,2,1,0:T(8,128)(2,1)} %middle_stage.3), calls=%async_computation.5 | async-start | bytes 4194304 | tf_op jit(solution)/shard_map/all_to_all | solution.py:819
  199.2 1.4 copy-start.9
  200.6 32.9 %all-to-all-start.3 = ((bf16[32,16,16,128]{3,2,1,0:T(8,128)(2,1)}), bf16[32,16,16,128]{3,2,1,0:T(8,128)(2,1)S(1)}, u32[]{:S(2)}, u32[]{:S(2)}) async-start(bf16[32,16,16,128]{3,2,1,0:T(8,128)(2,1)} %middle_stage.2), calls=%async_computation.3 | async-start | bytes 4194304 | tf_op jit(solution)/shard_map/all_to_all | solution.py:819
  242.9 32.9 %all-to-all-start.6 = ((bf16[32,16,16,128]{3,2,1,0:T(8,128)(2,1)}), bf16[32,16,16,128]{3,2,1,0:T(8,128)(2,1)S(1)}, u32[]{:S(2)}, u32[]{:S(2)}) async-start(bf16[32,16,16,128]{3,2,1,0:T(8,128)(2,1)} %get-tuple-element.16), calls=%async_computation.6 | async-start | bytes 4194304 | tf_op jit(solution)/shard_map/all_to_all | solution.py:819
  275.8 1.3 copy-start.10
  277.1 32.9 %all-to-all-start.7 = ((bf16[32,16,16,128]{3,2,1,0:T(8,128)(2,1)}), bf16[32,16,16,128]{3,2,1,0:T(8,128)(2,1)S(1)}, u32[]{:S(2)}, u32[]{:S(2)}) async-start(bf16[32,16,16,128]{3,2,1,0:T(8,128)(2,1)} %grid_odd.3), calls=%async_computation.7 | async-start | bytes 4194304 | tf_op jit(solution)/shard_map/all_to_all | solution.py:819
  291.0 28.5 %collective-permute-start.8 = (bf16[16,64,128]{2,1,0:T(8,128)(2,1)S(1)}, bf16[16,64,128]{2,1,0:T(8,128)(2,1)S(1)}, u32[]{:S(2)}, u32[]{:S(2)}) collective-permute-start(bf16[16,64,128]{2,1,0:T(8,128)(2,1)S(1)} %get-tuple-element.22.refs_4_), channel_id=1, source_target_pairs={{0,3},{1,0},{2,1},{3,2},{4,7},{5,4},{6,5},{7,6},{8,11},{9,8},{10,9... | collective-permute-start | bytes 786440 | tf_op jit(solution)/shard_map/ppermute | solution.py:825
  291.3 35.0 %collective-permute-start.7 = (bf16[16,64,128]{2,1,0:T(8,128)(2,1)S(1)}, bf16[16,64,128]{2,1,0:T(8,128)(2,1)S(1)}, u32[]{:S(2)}, u32[]{:S(2)}) collective-permute-start(bf16[16,64,128]{2,1,0:T(8,128)(2,1)S(1)} %get-tuple-element.22.refs_4_), channel_id=1, source_target_pairs={{0,2},{1,3},{2,0},{3,1},{4,6},{5,7},{6,4},{7,5},{8,10},{9,11},{10,... | collective-permute-start | bytes 786440 | tf_op jit(solution)/shard_map/ppermute | solution.py:825
  291.8 34.5 %collective-permute-start.6 = (bf16[16,64,128]{2,1,0:T(8,128)(2,1)S(1)}, bf16[16,64,128]{2,1,0:T(8,128)(2,1)S(1)}, u32[]{:S(2)}, u32[]{:S(2)}) collective-permute-start(bf16[16,64,128]{2,1,0:T(8,128)(2,1)S(1)} %get-tuple-element.22.refs_4_), channel_id=1, source_target_pairs={{0,1},{1,2},{2,3},{3,0},{4,5},{5,6},{6,7},{7,4},{8,9},{9,10},{10,1... | collective-permute-start | bytes 786440 | tf_op jit(solution)/shard_map/ppermute | solution.py:825
  318.7 7.6 %collective-permute-start.11 = (bf16[16,64,128]{2,1,0:T(8,128)(2,1)S(1)}, bf16[16,64,128]{2,1,0:T(8,128)(2,1)S(1)}, u32[]{:S(2)}, u32[]{:S(2)}) collective-permute-start(bf16[16,64,128]{2,1,0:T(8,128)(2,1)S(1)} %get-tuple-element.23.refs_8_), channel_id=1, source_target_pairs={{0,3},{1,0},{2,1},{3,2},{4,7},{5,4},{6,5},{7,6},{8,11},{9,8},{10,9... | collective-permute-start | bytes 786440 | tf_op jit(solution)/shard_map/ppermute | solution.py:825
  319.0 8.3 %collective-permute-start.10 = (bf16[16,64,128]{2,1,0:T(8,128)(2,1)S(1)}, bf16[16,64,128]{2,1,0:T(8,128)(2,1)S(1)}, u32[]{:S(2)}, u32[]{:S(2)}) collective-permute-start(bf16[16,64,128]{2,1,0:T(8,128)(2,1)S(1)} %get-tuple-element.23.refs_8_), channel_id=1, source_target_pairs={{0,2},{1,3},{2,0},{3,1},{4,6},{5,7},{6,4},{7,5},{8,10},{9,11},{10,... | collective-permute-start | bytes 786440 | tf_op jit(solution)/shard_map/ppermute | solution.py:825
  319.5 14.8 %collective-permute-start.9 = (bf16[16,64,128]{2,1,0:T(8,128)(2,1)S(1)}, bf16[16,64,128]{2,1,0:T(8,128)(2,1)S(1)}, u32[]{:S(2)}, u32[]{:S(2)}) collective-permute-start(bf16[16,64,128]{2,1,0:T(8,128)(2,1)S(1)} %get-tuple-element.23.refs_8_), channel_id=1, source_target_pairs={{0,1},{1,2},{2,3},{3,0},{4,5},{5,6},{6,7},{7,4},{8,9},{9,10},{10,1... | collective-permute-start | bytes 786440 | tf_op jit(solution)/shard_map/ppermute | solution.py:825
  320.2 14.2 %copy-start.1 = (bf16[16,64,256]{2,1,0:T(8,128)(2,1)S(1)}, bf16[16,64,256]{2,1,0:T(8,128)(2,1)}, u32[]{:S(2)}) copy-start(bf16[16,64,256]{2,1,0:T(8,128)(2,1)} %get-tuple-element.20.refs_2_) | copy-start | bytes 1572868
  320.2 14.2 %copy-start.2 = (bf16[16,64,256]{2,1,0:T(8,128)(2,1)S(1)}, bf16[16,64,256]{2,1,0:T(8,128)(2,1)}, u32[]{:S(2)}) copy-start(bf16[16,64,256]{2,1,0:T(8,128)(2,1)} %get-tuple-element.21.refs_3_) | copy-start | bytes 1572868
  348.2 7.0 %collective-permute-start.14 = (f32[8,128]{1,0:T(8,128)S(1)}, f32[8,128]{1,0:T(8,128)S(1)}, u32[]{:S(2)}, u32[]{:S(2)}) collective-permute-start(f32[8,128]{1,0:T(8,128)S(1)} %reduce_sum.9.own_ref), channel_id=1, source_target_pairs={{0,3},{1,0},{2,1},{3,2},{4,7},{5,4},{6,5},{7,6},{8,11},{9,8},{10,9... | collective-permute-start | bytes 12296 | tf_op jit(solution)/shard_map/ppermute | solution.py:825
  348.8 6.4 %collective-permute-start.13 = (f32[8,128]{1,0:T(8,128)S(1)}, f32[8,128]{1,0:T(8,128)S(1)}, u32[]{:S(2)}, u32[]{:S(2)}) collective-permute-start(f32[8,128]{1,0:T(8,128)S(1)} %reduce_sum.9.own_ref), channel_id=1, source_target_pairs={{0,2},{1,3},{2,0},{3,1},{4,6},{5,7},{6,4},{7,5},{8,10},{9,11},{10,... | collective-permute-start | bytes 12296 | tf_op jit(solution)/shard_map/ppermute | solution.py:825
  349.1 6.1 %collective-permute-start.12 = (f32[8,128]{1,0:T(8,128)S(1)}, f32[8,128]{1,0:T(8,128)S(1)}, u32[]{:S(2)}, u32[]{:S(2)}) collective-permute-start(f32[8,128]{1,0:T(8,128)S(1)} %reduce_sum.9.own_ref), channel_id=1, source_target_pairs={{0,1},{1,2},{2,3},{3,0},{4,5},{5,6},{6,7},{7,4},{8,9},{9,10},{10,1... | collective-permute-start | bytes 12296 | tf_op jit(solution)/shard_map/ppermute | solution.py:825

commit v4 on v3

--- a/solution.py
+++ b/solution.py
@@ -165,7 +165,7 @@
     )(in_hbm(probes), in_hbm(legendre))
 
 
-def grid_sum_kernel(coef_ref, lev_ref, x_ref, out_ref):
+def grid_sum_kernel(coef_ref, lev_ref, x_ref, first_ref, second_ref):
     blocks, lats, waves, _ = x_ref.shape
     flat = x_ref[...].reshape(blocks * lats * waves, LANES)
     summed = jnp.dot(twice(flat), sum_matrix(coef_ref, lev_ref), preferred_element_type=F32)
@@ -173,7 +173,9 @@
     group = lax.broadcasted_iota(jnp.int32, (blocks, 4, waves, LANES), 3) // 32
     low = jnp.where(group == 0, summed[:, 0:4], summed[:, 4:8])
     high = jnp.where(group == 2, summed[:, 8:12], summed[:, 12:16])
-    out_ref[...] = jnp.where(group < 2, low, high).astype(BF16)
+    packed = jnp.where(group < 2, low, high).astype(BF16)
+    first_ref[...] = packed[:, :2]
+    second_ref[...] = packed[:, 2:]
 
 
 def grid_sum(x, coef, lev):
@@ -187,8 +189,8 @@
             smem_spec(),
             pl.BlockSpec((blocks // steps, lats, waves, LANES), lambda g: (g, 0, 0, 0)),
         ],
-        out_specs=pl.BlockSpec((blocks // steps, 4, waves, LANES), lambda g: (g, 0, 0, 0)),
-        out_shape=jax.ShapeDtypeStruct((blocks, 4, waves, LANES), BF16),
+        out_specs=[pl.BlockSpec((blocks // steps, 2, waves, LANES), lambda g: (g, 0, 0, 0))] * 2,
+        out_shape=[jax.ShapeDtypeStruct((blocks, 2, waves, LANES), BF16)] * 2,
         compiler_params=params(12),
         name="grid_sum",
     )(coef, lev, in_hbm(x))
@@ -203,8 +205,8 @@
     for pair in range(2):
         both = []
         for k in range(2):
-            parts = [ref[:, 2 * pair + k].astype(F32) for ref in totals]
-            both.append((parts[0] + parts[1]) + (parts[2] + parts[3]))
+            parts = [ref[:, k].astype(F32) for ref in totals[2 * pair : 2 * pair + 2]]
+            both.append(parts[0] + parts[1])
         lanes = slice(pair * LANES, (pair + 1) * LANES)
         for parity in range(2):
             masked = []
@@ -578,19 +580,28 @@
     def _():
         spread_rows(x_ref, taken)
 
-    up_matrix = sum_matrix(up_ref, lev_ref)
     down_matrix = sum_matrix(down_ref, lev_ref)
+    matrix = jnp.concatenate([sum_matrix(up_ref, lev_ref), down_matrix], axis=1)
+    highs, lows = [], []
     for k in range(count):
         fields = taken[pl.ds(slot(step * count + k), lats, stride=waves), :].astype(BF16)
-        image = transform_of(table_ref[k, 0], fields)
-        high, low = halves(image)
+        high, low = halves(transform_of(table_ref[k, 0], fields))
         out_ref[k] = jnp.concatenate([high, low], axis=1)
-        up_sum = jnp.dot(twice(high), up_matrix, preferred_element_type=F32)
-        part_ref[k] = pack_levels(up_sum).astype(BF16)
-        down_sum = jnp.dot(twice(high), down_matrix, preferred_element_type=F32) + jnp.dot(
-            low, down_matrix[:LANES], preferred_element_type=F32
+        highs.append(high)
+        lows.append(low)
+    sums = jnp.dot(
+        twice(jnp.concatenate(highs, axis=0)), matrix, preferred_element_type=F32
+    )
+    rest = jnp.dot(
+        jnp.concatenate(lows, axis=0), down_matrix[:LANES], preferred_element_type=F32
+    )
+    degrees = table_ref.shape[3]
+    for k in range(count):
+        rows = slice(k * degrees, (k + 1) * degrees)
+        part_ref[k] = pack_levels(sums[rows, :LANES]).astype(BF16)
+        low_ref[k] = jnp.concatenate(
+            halves(pack_levels(sums[rows, LANES:] + rest[rows])), axis=1
         )
-        low_ref[k] = jnp.concatenate(halves(pack_levels(down_sum)), axis=1)
 
 
 def image_stage(x, legendre, up, down, lev, parity):
@@ -827,6 +838,10 @@
     ]
 
 
+def add_partner(values, pairs):
+    return (values.astype(F32) + lax.ppermute(values, "lev", pairs).astype(F32)).astype(BF16)
+
+
 def shards(
     probes, legendre, quad_weight, trunc_counts, background, level_up, level_down, viscosity
 ):
@@ -860,8 +875,18 @@
         folded[p] = exchange(values)
 
     def couple_first(x):
-        partial = grid_sum(x, level_down, lev)
-        total = grid_total(trunc_counts, [partial] + from_levels(partial), tables[0])
+        near = [(i, i ^ 1) for i in range(lev_count)]
+        far = [(i, lev_count - 1 - i) for i in range(lev_count)]
+        first, second = grid_sum(x, level_down, lev)
+        first = add_partner(first, near)
+        second = add_partner(second, far)
+        parts = [
+            first,
+            lax.ppermute(first, "lev", far),
+            second,
+            lax.ppermute(second, "lev", near),
+        ]
+        total = grid_total(trunc_counts, parts, tables[0])
         return True, level_up, lev, [total]
 
     def couple_none(x):

time: 364 us -> 358 us (0.984)
  waiting for transfers between devices: 157 us -> 147 us
  starting transfers between devices: 56.7 us -> 64.6 us
  Pallas kernels: 130 us -> 125 us
    ppermute x15 -> x12, waiting for transfers between devices: 35.6 us -> 21.1 us  [from_levels(): lax.ppermute(part, 'lev', [(i, (i + k) % count) for i in range(count)])]
    ppermute x0 -> x4, starting transfers between devices: none -> 5.31 us  [the longest x2 2.98 us: add_partner(): lax.ppermute(values, 'lev', pairs).astype(F32)]
    ppermute x0 -> x4, waiting for transfers between devices: none -> 4.73 us  [the longest x2 4.73 us: add_partner(): lax.ppermute(values, 'lev', pairs).astype(F32)]
    ppermute x15 -> x12, starting transfers between devices: 11.6 us -> 13.1 us  [from_levels(): lax.ppermute(part, 'lev', [(i, (i + k) % count) for i in range(count)])]
  transfers between devices with their start and end apart: 23 -> 24, of which waited for: 13 -> 11; matrix products, arithmetic and copies ran while one was open for 0% -> 1% of each run, Pallas kernels for 27% -> 26%
where the time goes in v4:
time: 358 us; the launch traced here: 356 us
  waiting for transfers between devices  147 us (41%)
  Pallas kernels  125 us (35%)
  starting transfers between devices  64.6 us (18%)
  blocking collectives  11.8 us (3%)
  local copies, waits for them, and re-layouts  4.51 us (1%)
    all_to_all x8, waiting for transfers between devices, exchange(): lax.all_to_all(blocks, 'lat', split_axis=0, concat_axis=0, tiled=True)  121 us
    all_to_all x8, starting transfers between devices, exchange(): lax.all_to_all(blocks, 'lat', split_axis=0, concat_axis=0, tiled=True)  46.2 us
    pallas_call x2, Pallas kernels, middle_stage(): pl.pallas_call(functools.partial(middle_kernel, parity=parity), grid=(1,)...  25.3 us
    ppermute x12, waiting for transfers between devices, from_levels(): lax.ppermute(part, 'lev', [(i, (i + k) % count) for i in range(count)])  21.1 us
    pallas_call x2, Pallas kernels, grid_pass(): pl.pallas_call(functools.partial(grid_middle_kernel, coupled=coupled, mas...  19.5 us
    pallas_call x2, Pallas kernels, image_stage(): pl.pallas_call(images_kernel, grid=(steps,), in_specs=[smem_spec(), smem_...  14.4 us
    ppermute x12, starting transfers between devices, from_levels(): lax.ppermute(part, 'lev', [(i, (i + k) % count) for i in range(count)])  13.1 us
    all_to_all x1, blocking collectives, exchange(): lax.all_to_all(blocks, 'lat', split_axis=0, concat_axis=0, tiled=True)  11.8 us
  transfers between devices with their start and end apart: 24, of which 11 were waited for; matrix products, arithmetic and copies ran while one was open for 1% of the time, Pallas kernels for 26%

profile of v4, /device:TPU:1, one launch (start us, length us, event | category | flops | bytes accessed | tf_op | source)
XLA Modules:
  0.0 356.2 jit_solution(550429679146413477)
XLA Ops:
  0.6 5.1 %legendre_raw.1 = bf16[32,16,16,128]{3,2,1,0:T(8,128)(2,1)} custom-call(bf16[16,2,256,128]{3,2,1,0:T(8,128)(2,1)} %probes_ref.5, bf16[16,2,512,256]{3,2,1,0:T(8,128)(2,1)} %table_ref.13), custom_call_target="tpu_custom_call" | custom-call | tf_op jit(solution)/shard_map/legendre_raw/pallas_call | solution.py:153
  5.7 9.7 %all-to-all-start.1 = ((bf16[32,16,16,128]{3,2,1,0:T(8,128)(2,1)}), bf16[32,16,16,128]{3,2,1,0:T(8,128)(2,1)S(1)}, u32[]{:S(2)}, u32[]{:S(2)}) async-start(bf16[32,16,16,128]{3,2,1,0:T(8,128)(2,1)} %legendre_raw.1), calls=%async_computation.1 | async-start | bytes 4194304 | tf_op jit(solution)/shard_map/all_to_all | solution.py:830
  15.5 2.0 level_partial.1.refs_0_
  17.5 2.5 collective-permute-start.2
  20.0 0.5 collective-permute-start.1
  20.5 0.6 collective-permute-start
  21.1 9.8 %collective-permute-done.2.refs_3_ = bf16[16,64,128]{2,1,0:T(8,128)(2,1)S(1)} collective-permute-done((bf16[16,64,128]{2,1,0:T(8,128)(2,1)S(1)}, bf16[16,64,128]{2,1,0:T(8,128)(2,1)S(1)}, u32[]{:S(2)}, u32[]{:S(2)}) %collective-permute-start.2) | collective-permute-done | bytes 262176 | tf_op jit(solution)/shard_map/ppermute | solution.py:836
  30.9 4.4 %collective-permute-done.refs_1_ = bf16[16,64,128]{2,1,0:T(8,128)(2,1)S(1)} collective-permute-done((bf16[16,64,128]{2,1,0:T(8,128)(2,1)S(1)}, bf16[16,64,128]{2,1,0:T(8,128)(2,1)S(1)}, u32[]{:S(2)}, u32[]{:S(2)}) %collective-permute-start) | collective-permute-done | bytes 262176 | tf_op jit(solution)/shard_map/ppermute | solution.py:836
  35.4 5.5 %legendre_forward.1 = bf16[32,16,16,128]{3,2,1,0:T(8,128)(2,1)} custom-call(f32[16]{0:T(128)S(1)} %copy-done.5, s32[1]{0:T(128)} %bitcast.lev_ref, bf16[16,2,256,128]{3,2,1,0:T(8,128)(2,1)} %probes_ref.5, bf16[16,64,128]{2,1,0:T(8,128)(2,1)S(1)} %level_partial.1.refs_0_, bf16[16,64,128]{2,1,0:T(8,128)(2,1)S(1)} %collective-permute-done.refs_1_, ...), custom_call_target="tpu_custom_call" | custom-call | tf_op jit(solution)/shard_map/legendre_forward/pallas_call | solution.py:294
  40.9 2.9 all-to-all-done.1.x_ref
  43.8 1.4 copy-done.8
  45.2 4.6 %all-to-all-start = ((bf16[32,16,16,128]{3,2,1,0:T(8,128)(2,1)}), bf16[32,16,16,128]{3,2,1,0:T(8,128)(2,1)S(1)}, u32[]{:S(2)}, u32[]{:S(2)}) async-start(bf16[32,16,16,128]{3,2,1,0:T(8,128)(2,1)} %legendre_forward.1), calls=%async_computation | async-start | bytes 4194304 | tf_op jit(solution)/shard_map/all_to_all | solution.py:830
  49.8 3.5 grid_sum.1
  53.4 0.0 copy-start.6
  53.4 1.2 collective-permute-start.3
  54.5 1.8 collective-permute-start.5
  56.3 4.7 %collective-permute-done.3 = bf16[32,2,16,128]{3,2,1,0:T(8,128)(2,1)S(1)} collective-permute-done((bf16[32,2,16,128]{3,2,1,0:T(8,128)(2,1)S(1)}, bf16[32,2,16,128]{3,2,1,0:T(8,128)(2,1)S(1)}, u32[]{:S(2)}, u32[]{:S(2)}) %collective-permute-start.3) | collective-permute-done | bytes 262176 | tf_op jit(solution)/shard_map/ppermute | solution.py:842
  61.1 0.1 add_convert_fusion.1.refs_0_
  61.1 2.3 collective-permute-start.4
  63.5 0.8 add_convert_fusion.refs_2_
  64.3 1.4 multiply_convert_fusion
  65.7 0.2 copy.15
  65.9 0.1 convert_element_type.36.gain_ref
  66.1 5.0 %spread_gain.1.refs_1_.refs_0_ = bf16[2,8,1024,128]{3,2,1,0:T(8,128)(2,1)} custom-call(bf16[2,8,8,1024]{3,2,1,0:T(8,128)(2,1)S(1)} %convert_element_type.36.gain_ref, bf16[8,128]{1,0:T(8,128)(2,1)S(1)} %copy-done.6), custom_call_target="tpu_custom_call" | custom-call | tf_op jit(solution)/shard_map/spread_gain/pallas_call | solution.py:421
  71.1 5.7 %grid_even.2.even_ref = bf16[4,2,512,256]{3,2,1,0:T(8,128)(2,1)} custom-call(s32[16]{0:T(128)S(1)} %copy-done.3, bf16[32,16,16,128]{3,2,1,0:T(8,128)(2,1)} %copy-done.8, bf16[2,512,512]{2,1,0:T(8,128)(2,1)} %constant.26.clone.table_ref.refs_4_.refs_2_.refs_1_), custom_call_target="tpu_custom_call" | custom-call | tf_op jit(solution)/shard_map/grid_even/pallas_call | solution.py:446
  76.8 2.7 grid_total.1.refs_0_
  79.5 10.1 %grid_middle.2 = (bf16[32,16,16,128]{3,2,1,0:T(8,128)(2,1)}, bf16[4,2,512,256]{3,2,1,0:T(8,128)(2,1)}) custom-call(s32[16]{0:T(128)S(1)} %copy-done.3, f32[16]{0:T(128)S(1)} %copy-done.5, s32[1]{0:T(128)} %bitcast.lev_ref, bf16[32,16,16,128]{3,2,1,0:T(8,128)(2,1)S(1)} %all-to-all-done.x_ref, bf16[4,2,512,256]{3,2,1,0:T(8,128)(2,1)} %grid_even.2.even_ref, ...), custom_call_target="tpu_custom_call" | custom-call | tf_op jit(solution)/shard_map/grid_middle/pallas_call | solution.py:459
  89.6 8.8 %all-to-all-start.4 = ((bf16[32,16,16,128]{3,2,1,0:T(8,128)(2,1)}), bf16[32,16,16,128]{3,2,1,0:T(8,128)(2,1)S(1)}, u32[]{:S(2)}, u32[]{:S(2)}) async-start(bf16[32,16,16,128]{3,2,1,0:T(8,128)(2,1)} %get-tuple-element.19), calls=%async_computation.4 | async-start | bytes 4194304 | tf_op jit(solution)/shard_map/all_to_all | solution.py:830
  98.4 5.2 %grid_odd.2 = bf16[32,16,16,128]{3,2,1,0:T(8,128)(2,1)} custom-call(s32[16]{0:T(128)S(1)} %copy-done.3, bf16[4,2,512,256]{3,2,1,0:T(8,128)(2,1)} %get-tuple-element.18.odd_ref, bf16[2,512,512]{2,1,0:T(8,128)(2,1)} %constant.27.clone.refs_3_.table_ref.refs_2_), custom_call_target="tpu_custom_call" | custom-call | tf_op jit(solution)/shard_map/grid_odd/pallas_call | solution.py:491
  103.6 23.1 %all-to-all-done.4.x_ref = bf16[32,16,16,128]{3,2,1,0:T(8,128)(2,1)S(1)} async-done(((bf16[32,16,16,128]{3,2,1,0:T(8,128)(2,1)}), bf16[32,16,16,128]{3,2,1,0:T(8,128)(2,1)S(1)}, u32[]{:S(2)}, u32[]{:S(2)}) %all-to-all-start.4) | async-done | bytes 2097184 | tf_op jit(solution)/shard_map/all_to_all | solution.py:830
  126.7 5.2 %all-to-all-start.2 = ((bf16[32,16,16,128]{3,2,1,0:T(8,128)(2,1)}), bf16[32,16,16,128]{3,2,1,0:T(8,128)(2,1)}, u32[]{:S(2)}, u32[]{:S(2)}) async-start(bf16[32,16,16,128]{3,2,1,0:T(8,128)(2,1)} %grid_odd.2), calls=%async_computation.2 | async-start | bytes 4194304 | tf_op jit(solution)/shard_map/all_to_all | solution.py:830
  131.9 12.3 %middle_stage.3 = bf16[32,16,16,128]{3,2,1,0:T(8,128)(2,1)} custom-call(s32[1]{0:T(128)} %bitcast.1.first_ref, f32[16]{0:T(128)S(1)} %copy-done.7, s32[1]{0:T(128)} %bitcast.lev_ref, bf16[32,16,16,128]{3,2,1,0:T(8,128)(2,1)S(1)} %all-to-all-done.4.x_ref, bf16[16,2,512,256]{3,2,1,0:T(8,128)(2,1)} %table_ref.13), custom_call_target="tpu_custom_call" | custom-call | tf_op jit(solution)/shard_map/middle_stage/pallas_call | solution.py:555
  144.2 16.1 %all-to-all-done.2.x_ref = bf16[32,16,16,128]{3,2,1,0:T(8,128)(2,1)} async-done(((bf16[32,16,16,128]{3,2,1,0:T(8,128)(2,1)}), bf16[32,16,16,128]{3,2,1,0:T(8,128)(2,1)}, u32[]{:S(2)}, u32[]{:S(2)}) %all-to-all-start.2) | async-done | bytes 2097184 | tf_op jit(solution)/shard_map/all_to_all | solution.py:830
  160.4 4.5 %all-to-all-start.5 = ((bf16[32,16,16,128]{3,2,1,0:T(8,128)(2,1)}), bf16[32,16,16,128]{3,2,1,0:T(8,128)(2,1)S(1)}, u32[]{:S(2)}, u32[]{:S(2)}) async-start(bf16[32,16,16,128]{3,2,1,0:T(8,128)(2,1)} %middle_stage.3), calls=%async_computation.5 | async-start | bytes 4194304 | tf_op jit(solution)/shard_map/all_to_all | solution.py:830
  164.9 13.0 %middle_stage.2 = bf16[32,16,16,128]{3,2,1,0:T(8,128)(2,1)} custom-call(s32[1]{0:T(128)} %bitcast.1.first_ref, f32[16]{0:T(128)S(1)} %copy-done.7, s32[1]{0:T(128)} %bitcast.lev_ref, bf16[32,16,16,128]{3,2,1,0:T(8,128)(2,1)} %all-to-all-done.2.x_ref, bf16[16,2,512,256]{3,2,1,0:T(8,128)(2,1)} %table_ref.13), custom_call_target="tpu_custom_call" | custom-call | tf_op jit(solution)/shard_map/middle_stage/pallas_call | solution.py:555
  177.8 15.5 %all-to-all-done.5.x_ref = bf16[32,16,16,128]{3,2,1,0:T(8,128)(2,1)S(1)} async-done(((bf16[32,16,16,128]{3,2,1,0:T(8,128)(2,1)}), bf16[32,16,16,128]{3,2,1,0:T(8,128)(2,1)S(1)}, u32[]{:S(2)}, u32[]{:S(2)}) %all-to-all-start.5) | async-done | bytes 2097184 | tf_op jit(solution)/shard_map/all_to_all | solution.py:830
  193.3 1.4 copy-done.9
  194.7 4.5 %all-to-all-start.3 = ((bf16[32,16,16,128]{3,2,1,0:T(8,128)(2,1)}), bf16[32,16,16,128]{3,2,1,0:T(8,128)(2,1)S(1)}, u32[]{:S(2)}, u32[]{:S(2)}) async-start(bf16[32,16,16,128]{3,2,1,0:T(8,128)(2,1)} %middle_stage.2), calls=%async_computation.3 | async-start | bytes 4194304 | tf_op jit(solution)/shard_map/all_to_all | solution.py:830
  199.2 5.4 %grid_even.3.even_ref = bf16[4,2,512,256]{3,2,1,0:T(8,128)(2,1)} custom-call(s32[16]{0:T(128)S(1)} %copy-done.3, bf16[32,16,16,128]{3,2,1,0:T(8,128)(2,1)} %copy-done.9, bf16[2,512,512]{2,1,0:T(8,128)(2,1)} %constant.26.clone.table_ref.refs_4_.refs_2_.refs_1_), custom_call_target="tpu_custom_call" | custom-call | tf_op jit(solution)/shard_map/grid_even/pallas_call | solution.py:446
  204.6 23.0 %all-to-all-done.3.x_ref = bf16[32,16,16,128]{3,2,1,0:T(8,128)(2,1)S(1)} async-done(((bf16[32,16,16,128]{3,2,1,0:T(8,128)(2,1)}), bf16[32,16,16,128]{3,2,1,0:T(8,128)(2,1)S(1)}, u32[]{:S(2)}, u32[]{:S(2)}) %all-to-all-start.3) | async-done | bytes 2097184 | tf_op jit(solution)/shard_map/all_to_all | solution.py:830
  227.6 9.4 %grid_middle.3 = (bf16[32,16,16,128]{3,2,1,0:T(8,128)(2,1)}, bf16[4,2,512,256]{3,2,1,0:T(8,128)(2,1)}) custom-call(s32[16]{0:T(128)S(1)} %copy-done.3, f32[16]{0:T(128)S(1)} %copy-done.5, s32[1]{0:T(128)} %bitcast.lev_ref, bf16[32,16,16,128]{3,2,1,0:T(8,128)(2,1)S(1)} %all-to-all-done.3.x_ref, bf16[4,2,512,256]{3,2,1,0:T(8,128)(2,1)} %grid_even.3.even_ref, ...), custom_call_target="tpu_custom_call" | custom-call | tf_op jit(solution)/shard_map/grid_middle/pallas_call | solution.py:459
  237.0 4.5 %all-to-all-start.6 = ((bf16[32,16,16,128]{3,2,1,0:T(8,128)(2,1)}), bf16[32,16,16,128]{3,2,1,0:T(8,128)(2,1)S(1)}, u32[]{:S(2)}, u32[]{:S(2)}) async-start(bf16[32,16,16,128]{3,2,1,0:T(8,128)(2,1)} %get-tuple-element.20), calls=%async_computation.6 | async-start | bytes 4194304 | tf_op jit(solution)/shard_map/all_to_all | solution.py:830
  241.5 5.4 %grid_odd.3 = bf16[32,16,16,128]{3,2,1,0:T(8,128)(2,1)} custom-call(s32[16]{0:T(128)S(1)} %copy-done.3, bf16[4,2,512,256]{3,2,1,0:T(8,128)(2,1)} %get-tuple-element.22.odd_ref, bf16[2,512,512]{2,1,0:T(8,128)(2,1)} %constant.27.clone.refs_3_.table_ref.refs_2_), custom_call_target="tpu_custom_call" | custom-call | tf_op jit(solution)/shard_map/grid_odd/pallas_call | solution.py:491
  246.9 23.1 %all-to-all-done.6.x_ref = bf16[32,16,16,128]{3,2,1,0:T(8,128)(2,1)S(1)} async-done(((bf16[32,16,16,128]{3,2,1,0:T(8,128)(2,1)}), bf16[32,16,16,128]{3,2,1,0:T(8,128)(2,1)S(1)}, u32[]{:S(2)}, u32[]{:S(2)}) %all-to-all-start.6) | async-done | bytes 2097184 | tf_op jit(solution)/shard_map/all_to_all | solution.py:830
  269.9 1.3 copy-done.10
  271.3 4.5 %all-to-all-start.7 = ((bf16[32,16,16,128]{3,2,1,0:T(8,128)(2,1)}), bf16[32,16,16,128]{3,2,1,0:T(8,128)(2,1)S(1)}, u32[]{:S(2)}, u32[]{:S(2)}) async-start(bf16[32,16,16,128]{3,2,1,0:T(8,128)(2,1)} %grid_odd.3), calls=%async_computation.7 | async-start | bytes 4194304 | tf_op jit(solution)/shard_map/all_to_all | solution.py:830
  275.8 7.6 %image_stage.2 = (bf16[16,256,256]{2,1,0:T(8,128)(2,1)}, bf16[16,64,128]{2,1,0:T(8,128)(2,1)S(1)}, bf16[16,64,256]{2,1,0:T(8,128)(2,1)}) custom-call(f32[16]{0:T(128)S(1)} %copy-done.5, f32[16]{0:T(128)S(1)} %copy-done.4, s32[1]{0:T(128)} %bitcast.lev_ref, bf16[32,16,16,128]{3,2,1,0:T(8,128)(2,1)} %copy-done.10, bf16[16,2,512,256]{3,2,1,0:T(8,128)(2,1)} %table_ref.13), custom_call_target="tpu_custom_call" | custom-call | tf_op jit(solution)/shard_map/image_stage/pallas_call | solution.py:612
  283.3 1.1 collective-permute-start.9
  284.4 2.2 collective-permute-start.8
  286.6 0.1 collective-permute-start.7
  286.7 17.4 %all-to-all-done.7.x_ref = bf16[32,16,16,128]{3,2,1,0:T(8,128)(2,1)S(1)} async-done(((bf16[32,16,16,128]{3,2,1,0:T(8,128)(2,1)}), bf16[32,16,16,128]{3,2,1,0:T(8,128)(2,1)S(1)}, u32[]{:S(2)}, u32[]{:S(2)}) %all-to-all-start.7) | async-done | bytes 2097184 | tf_op jit(solution)/shard_map/all_to_all | solution.py:830
  304.2 6.8 %image_stage.3 = (bf16[16,256,256]{2,1,0:T(8,128)(2,1)}, bf16[16,64,128]{2,1,0:T(8,128)(2,1)S(1)}, bf16[16,64,256]{2,1,0:T(8,128)(2,1)}) custom-call(f32[16]{0:T(128)S(1)} %copy-done.5, f32[16]{0:T(128)S(1)} %copy-done.4, s32[1]{0:T(128)} %bitcast.lev_ref, bf16[32,16,16,128]{3,2,1,0:T(8,128)(2,1)S(1)} %all-to-all-done.7.x_ref, ...), custom_call_target="tpu_custom_call" | custom-call | tf_op jit(solution)/shard_map/image_stage/pallas_call | solution.py:612
  311.0 1.1 collective-permute-start.12
  312.1 2.2 collective-permute-start.11
  314.3 0.1 collective-permute-start.10
  314.4 3.1 gram_stage.2.refs_0_
  317.5 3.0 gram_stage.3.refs_1_
  320.6 6.9 %collective-permute-done.10.refs_9_ = bf16[16,64,128]{2,1,0:T(8,128)(2,1)S(1)} collective-permute-done((bf16[16,64,128]{2,1,0:T(8,128)(2,1)S(1)}, bf16[16,64,128]{2,1,0:T(8,128)(2,1)S(1)}, u32[]{:S(2)}, u32[]{:S(2)}) %collective-permute-start.10) | collective-permute-done | bytes 262176 | tf_op jit(solution)/shard_map/ppermute | solution.py:836
  327.5 2.0 finish_stage.1
  329.5 11.8 %all_to_all.45 = f32[32,8,128]{2,1,0:T(8,128)S(1)} all-to-all(f32[32,8,128]{2,1,0:T(8,128)} %get-tuple-element.28), channel_id=1, replica_groups=mesh['lat'=32,'lev'=4] {'lat'}, dimensions={0} | all-to-all | bytes 262144 | tf_op jit(solution)/shard_map/all_to_all | solution.py:830
  341.3 0.4 collective-permute-start.15
  341.7 2.2 collective-permute-start.14
  343.9 5.4 %full_stage.1.full_ref = bf16[16,2,256,256]{3,2,1,0:T(8,128)(2,1)} custom-call(f32[16]{0:T(128)S(1)} %copy-done.4, s32[1]{0:T(128)} %bitcast.lev_ref, bf16[16,256,256]{2,1,0:T(8,128)(2,1)} %get-tuple-element.21.image_ref.even_ref, bf16[16,256,256]{2,1,0:T(8,128)(2,1)} %get-tuple-element.23.image_ref.odd_ref, bf16[2,16,64,128]{3,2,1,0:T(8,128)(2,1)} %get-tuple-element.29.total_ref), custom_call_target="tpu_custom_call" | custom-call | tf_op jit(solution)/shard_map/full_stage/pallas_call | solution.py:789
  349.4 6.9 %basis_stage.1 = (bf16[16,2,256,128]{3,2,1,0:T(8,128)(2,1)}, f32[16,16]{1,0:T(8,128)}) custom-call(f32[8,128]{1,0:T(8,128)S(1)} %reduce_sum.9.own_ref, f32[8,128]{1,0:T(8,128)S(1)} %collective-permute-done.13.one_ref, f32[8,128]{1,0:T(8,128)S(1)} %collective-permute-done.14.two_ref, f32[8,128]{1,0:T(8,128)S(1)} %collective-permute-done.15.three_ref, ...), custom_call_target="tpu_custom_call" | custom-call | tf_op jit(solution)/shard_map/basis_stage/pallas_call | solution.py:810
  (37 shorter events, 0.1 us)
Async XLA Ops:
  5.7 9.8 %copy-start.4 = (f32[16]{0:T(128)S(1)}, f32[16]{0:T(128)}, u32[]{:S(2)}) copy-start(f32[16]{0:T(128)} %down_ref.7) | copy-start | bytes 196
  5.7 38.1 %all-to-all-start.1 = ((bf16[32,16,16,128]{3,2,1,0:T(8,128)(2,1)}), bf16[32,16,16,128]{3,2,1,0:T(8,128)(2,1)S(1)}, u32[]{:S(2)}, u32[]{:S(2)}) async-start(bf16[32,16,16,128]{3,2,1,0:T(8,128)(2,1)} %legendre_raw.1), calls=%async_computation.1 | async-start | bytes 4194304 | tf_op jit(solution)/shard_map/all_to_all | solution.py:830
  15.4 19.9 %copy-start.5 = (f32[16]{0:T(128)S(1)}, f32[16]{0:T(128)}, u32[]{:S(2)}) copy-start(f32[16]{0:T(128)} %up_ref.3) | copy-start | bytes 196
  17.5 13.4 %collective-permute-start.2 = (bf16[16,64,128]{2,1,0:T(8,128)(2,1)S(1)}, bf16[16,64,128]{2,1,0:T(8,128)(2,1)S(1)}, u32[]{:S(2)}, u32[]{:S(2)}) collective-permute-start(bf16[16,64,128]{2,1,0:T(8,128)(2,1)S(1)} %level_partial.1.refs_0_), channel_id=1, source_target_pairs={{0,3},{1,0},{2,1},{3,2},{4,7},{5,4},{6,5},{7,6},{8,11},{9,8},{10,9... | collective-permute-start | bytes 786440 | tf_op jit(solution)/shard_map/ppermute | solution.py:836
  20.0 10.9 %collective-permute-start.1 = (bf16[16,64,128]{2,1,0:T(8,128)(2,1)S(1)}, bf16[16,64,128]{2,1,0:T(8,128)(2,1)S(1)}, u32[]{:S(2)}, u32[]{:S(2)}) collective-permute-start(bf16[16,64,128]{2,1,0:T(8,128)(2,1)S(1)} %level_partial.1.refs_0_), channel_id=1, source_target_pairs={{0,2},{1,3},{2,0},{3,1},{4,6},{5,7},{6,4},{7,5},{8,10},{9,11},{10,... | collective-permute-start | bytes 786440 | tf_op jit(solution)/shard_map/ppermute | solution.py:836
  20.5 14.8 %collective-permute-start = (bf16[16,64,128]{2,1,0:T(8,128)(2,1)S(1)}, bf16[16,64,128]{2,1,0:T(8,128)(2,1)S(1)}, u32[]{:S(2)}, u32[]{:S(2)}) collective-permute-start(bf16[16,64,128]{2,1,0:T(8,128)(2,1)S(1)} %level_partial.1.refs_0_), channel_id=1, source_target_pairs={{0,1},{1,2},{2,3},{3,0},{4,5},{5,6},{6,7},{7,4},{8,9},{9,10},{10,1... | collective-permute-start | bytes 786440 | tf_op jit(solution)/shard_map/ppermute | solution.py:836
  43.8 1.4 copy-start.8
  45.2 34.4 %all-to-all-start = ((bf16[32,16,16,128]{3,2,1,0:T(8,128)(2,1)}), bf16[32,16,16,128]{3,2,1,0:T(8,128)(2,1)S(1)}, u32[]{:S(2)}, u32[]{:S(2)}) async-start(bf16[32,16,16,128]{3,2,1,0:T(8,128)(2,1)} %legendre_forward.1), calls=%async_computation | async-start | bytes 4194304 | tf_op jit(solution)/shard_map/all_to_all | solution.py:830
  49.8 14.5 %copy-start.11 = (f32[16]{0:T(128)S(1)}, f32[16]{0:T(128)}, u32[]{:S(2)}) copy-start(f32[16]{0:T(128)} %param.13) | copy-start | bytes 196
  53.4 12.7 %copy-start.6 = (bf16[8,128]{1,0:T(8,128)(2,1)S(1)}, bf16[8,128]{1,0:T(8,128)(2,1)}, u32[]{:S(2)}) copy-start(bf16[8,128]{1,0:T(8,128)(2,1)} %constant.28.clone.spread_ref) | copy-start | bytes 6148
  53.4 7.7 %collective-permute-start.3 = (bf16[32,2,16,128]{3,2,1,0:T(8,128)(2,1)S(1)}, bf16[32,2,16,128]{3,2,1,0:T(8,128)(2,1)S(1)}, u32[]{:S(2)}, u32[]{:S(2)}) collective-permute-start(bf16[32,2,16,128]{3,2,1,0:T(8,128)(2,1)S(1)} %get-tuple-element.16), channel_id=1, source_target_pairs={{0,1},{1,0},{2,3},{3,2},{4,5},{5,4},{6,7},{7,6},{8,9},{9,8},{10,11... | collective-permute-start | bytes 786440 | tf_op jit(solution)/shard_map/ppermute | solution.py:842
  54.5 9.0 %collective-permute-start.5 = (bf16[32,2,16,128]{3,2,1,0:T(8,128)(2,1)S(1)}, bf16[32,2,16,128]{3,2,1,0:T(8,128)(2,1)S(1)}, u32[]{:S(2)}, u32[]{:S(2)}) collective-permute-start(bf16[32,2,16,128]{3,2,1,0:T(8,128)(2,1)S(1)} %get-tuple-element.17), channel_id=1, source_target_pairs={{0,3},{1,2},{2,1},{3,0},{4,7},{5,6},{6,5},{7,4},{8,11},{9,10},{10,... | collective-permute-start | bytes 786440 | tf_op jit(solution)/shard_map/ppermute | solution.py:842
  61.1 15.7 %collective-permute-start.4 = (bf16[32,2,16,128]{3,2,1,0:T(8,128)(2,1)S(1)}, bf16[32,2,16,128]{3,2,1,0:T(8,128)(2,1)}, u32[]{:S(2)}, u32[]{:S(2)}) collective-permute-start(bf16[32,2,16,128]{3,2,1,0:T(8,128)(2,1)S(1)} %add_convert_fusion.1.refs_0_), channel_id=1, source_target_pairs={{0,3},{1,2},{2,1},{3,0},{4,7},{5,6},{6,5},{7,4},{8,11},{9,10},{10,... | collective-permute-start | bytes 786440 | tf_op jit(solution)/shard_map/ppermute | solution.py:885
  64.3 12.5 %collective-permute-start.6 = (bf16[32,2,16,128]{3,2,1,0:T(8,128)(2,1)}, bf16[32,2,16,128]{3,2,1,0:T(8,128)(2,1)}, u32[]{:S(2)}, u32[]{:S(2)}) collective-permute-start(bf16[32,2,16,128]{3,2,1,0:T(8,128)(2,1)} %add_convert_fusion.refs_2_), channel_id=1, source_target_pairs={{0,1},{1,0},{2,3},{3,2},{4,5},{5,4},{6,7},{7,6},{8,9},{9,8},{10,11... | collective-permute-start | bytes 786440 | tf_op jit(solution)/shard_map/ppermute | solution.py:887
  66.0 5.0 %copy-start.3 = (s32[16]{0:T(128)S(1)}, s32[16]{0:T(128)}, u32[]{:S(2)}) copy-start(s32[16]{0:T(128)} %counts_ref.13) | copy-start | bytes 196
  71.1 5.8 %copy-start = (bf16[2,512,512]{2,1,0:T(8,128)(2,1)S(1)}, bf16[2,512,512]{2,1,0:T(8,128)(2,1)}, u32[]{:S(2)}) copy-start(bf16[2,512,512]{2,1,0:T(8,128)(2,1)} %constant.26.clone.table_ref.refs_4_.refs_2_.refs_1_) | copy-start | bytes 3145732
  89.6 37.1 %all-to-all-start.4 = ((bf16[32,16,16,128]{3,2,1,0:T(8,128)(2,1)}), bf16[32,16,16,128]{3,2,1,0:T(8,128)(2,1)S(1)}, u32[]{:S(2)}, u32[]{:S(2)}) async-start(bf16[32,16,16,128]{3,2,1,0:T(8,128)(2,1)} %get-tuple-element.19), calls=%async_computation.4 | async-start | bytes 4194304 | tf_op jit(solution)/shard_map/all_to_all | solution.py:830
  103.6 28.3 %copy-start.7 = (f32[16]{0:T(128)S(1)}, f32[16]{0:T(128)}, u32[]{:S(2)}) copy-start(f32[16]{0:T(128)} %visc_ref.3) | copy-start | bytes 196
  126.7 33.6 %all-to-all-start.2 = ((bf16[32,16,16,128]{3,2,1,0:T(8,128)(2,1)}), bf16[32,16,16,128]{3,2,1,0:T(8,128)(2,1)}, u32[]{:S(2)}, u32[]{:S(2)}) async-start(bf16[32,16,16,128]{3,2,1,0:T(8,128)(2,1)} %grid_odd.2), calls=%async_computation.2 | async-start | bytes 4194304 | tf_op jit(solution)/shard_map/all_to_all | solution.py:830
  160.4 32.9 %all-to-all-start.5 = ((bf16[32,16,16,128]{3,2,1,0:T(8,128)(2,1)}), bf16[32,16,16,128]{3,2,1,0:T(8,128)(2,1)S(1)}, u32[]{:S(2)}, u32[]{:S(2)}) async-start(bf16[32,16,16,128]{3,2,1,0:T(8,128)(2,1)} %middle_stage.3), calls=%async_computation.5 | async-start | bytes 4194304 | tf_op jit(solution)/shard_map/all_to_all | solution.py:830
  193.3 1.4 copy-start.9
  194.7 32.9 %all-to-all-start.3 = ((bf16[32,16,16,128]{3,2,1,0:T(8,128)(2,1)}), bf16[32,16,16,128]{3,2,1,0:T(8,128)(2,1)S(1)}, u32[]{:S(2)}, u32[]{:S(2)}) async-start(bf16[32,16,16,128]{3,2,1,0:T(8,128)(2,1)} %middle_stage.2), calls=%async_computation.3 | async-start | bytes 4194304 | tf_op jit(solution)/shard_map/all_to_all | solution.py:830
  237.0 32.9 %all-to-all-start.6 = ((bf16[32,16,16,128]{3,2,1,0:T(8,128)(2,1)}), bf16[32,16,16,128]{3,2,1,0:T(8,128)(2,1)S(1)}, u32[]{:S(2)}, u32[]{:S(2)}) async-start(bf16[32,16,16,128]{3,2,1,0:T(8,128)(2,1)} %get-tuple-element.20), calls=%async_computation.6 | async-start | bytes 4194304 | tf_op jit(solution)/shard_map/all_to_all | solution.py:830
  269.9 1.3 copy-start.10
  271.3 32.9 %all-to-all-start.7 = ((bf16[32,16,16,128]{3,2,1,0:T(8,128)(2,1)}), bf16[32,16,16,128]{3,2,1,0:T(8,128)(2,1)S(1)}, u32[]{:S(2)}, u32[]{:S(2)}) async-start(bf16[32,16,16,128]{3,2,1,0:T(8,128)(2,1)} %grid_odd.3), calls=%async_computation.7 | async-start | bytes 4194304 | tf_op jit(solution)/shard_map/all_to_all | solution.py:830
  283.3 31.0 %collective-permute-start.9 = (bf16[16,64,128]{2,1,0:T(8,128)(2,1)S(1)}, bf16[16,64,128]{2,1,0:T(8,128)(2,1)S(1)}, u32[]{:S(2)}, u32[]{:S(2)}) collective-permute-start(bf16[16,64,128]{2,1,0:T(8,128)(2,1)S(1)} %get-tuple-element.26.refs_4_), channel_id=1, source_target_pairs={{0,3},{1,0},{2,1},{3,2},{4,7},{5,4},{6,5},{7,6},{8,11},{9,8},{10,9... | collective-permute-start | bytes 786440 | tf_op jit(solution)/shard_map/ppermute | solution.py:836
  284.4 36.1 %collective-permute-start.8 = (bf16[16,64,128]{2,1,0:T(8,128)(2,1)S(1)}, bf16[16,64,128]{2,1,0:T(8,128)(2,1)S(1)}, u32[]{:S(2)}, u32[]{:S(2)}) collective-permute-start(bf16[16,64,128]{2,1,0:T(8,128)(2,1)S(1)} %get-tuple-element.26.refs_4_), channel_id=1, source_target_pairs={{0,2},{1,3},{2,0},{3,1},{4,6},{5,7},{6,4},{7,5},{8,10},{9,11},{10,... | collective-permute-start | bytes 786440 | tf_op jit(solution)/shard_map/ppermute | solution.py:836
  286.6 33.9 %collective-permute-start.7 = (bf16[16,64,128]{2,1,0:T(8,128)(2,1)S(1)}, bf16[16,64,128]{2,1,0:T(8,128)(2,1)S(1)}, u32[]{:S(2)}, u32[]{:S(2)}) collective-permute-start(bf16[16,64,128]{2,1,0:T(8,128)(2,1)S(1)} %get-tuple-element.26.refs_4_), channel_id=1, source_target_pairs={{0,1},{1,2},{2,3},{3,0},{4,5},{5,6},{6,7},{7,4},{8,9},{9,10},{10,1... | collective-permute-start | bytes 786440 | tf_op jit(solution)/shard_map/ppermute | solution.py:836
  311.0 9.6 %collective-permute-start.12 = (bf16[16,64,128]{2,1,0:T(8,128)(2,1)S(1)}, bf16[16,64,128]{2,1,0:T(8,128)(2,1)S(1)}, u32[]{:S(2)}, u32[]{:S(2)}) collective-permute-start(bf16[16,64,128]{2,1,0:T(8,128)(2,1)S(1)} %get-tuple-element.27.refs_8_), channel_id=1, source_target_pairs={{0,3},{1,0},{2,1},{3,2},{4,7},{5,4},{6,5},{7,6},{8,11},{9,8},{10,9... | collective-permute-start | bytes 786440 | tf_op jit(solution)/shard_map/ppermute | solution.py:836
  312.1 8.5 %collective-permute-start.11 = (bf16[16,64,128]{2,1,0:T(8,128)(2,1)S(1)}, bf16[16,64,128]{2,1,0:T(8,128)(2,1)S(1)}, u32[]{:S(2)}, u32[]{:S(2)}) collective-permute-start(bf16[16,64,128]{2,1,0:T(8,128)(2,1)S(1)} %get-tuple-element.27.refs_8_), channel_id=1, source_target_pairs={{0,2},{1,3},{2,0},{3,1},{4,6},{5,7},{6,4},{7,5},{8,10},{9,11},{10,... | collective-permute-start | bytes 786440 | tf_op jit(solution)/shard_map/ppermute | solution.py:836
  314.3 13.1 %collective-permute-start.10 = (bf16[16,64,128]{2,1,0:T(8,128)(2,1)S(1)}, bf16[16,64,128]{2,1,0:T(8,128)(2,1)S(1)}, u32[]{:S(2)}, u32[]{:S(2)}) collective-permute-start(bf16[16,64,128]{2,1,0:T(8,128)(2,1)S(1)} %get-tuple-element.27.refs_8_), channel_id=1, source_target_pairs={{0,1},{1,2},{2,3},{3,0},{4,5},{5,6},{6,7},{7,4},{8,9},{9,10},{10,1... | collective-permute-start | bytes 786440 | tf_op jit(solution)/shard_map/ppermute | solution.py:836
  314.4 13.0 %copy-start.1 = (bf16[16,64,256]{2,1,0:T(8,128)(2,1)S(1)}, bf16[16,64,256]{2,1,0:T(8,128)(2,1)}, u32[]{:S(2)}) copy-start(bf16[16,64,256]{2,1,0:T(8,128)(2,1)} %get-tuple-element.24.refs_2_) | copy-start | bytes 1572868
  314.4 13.0 %copy-start.2 = (bf16[16,64,256]{2,1,0:T(8,128)(2,1)S(1)}, bf16[16,64,256]{2,1,0:T(8,128)(2,1)}, u32[]{:S(2)}) copy-start(bf16[16,64,256]{2,1,0:T(8,128)(2,1)} %get-tuple-element.25.refs_3_) | copy-start | bytes 1572868
  341.3 8.0 %collective-permute-start.15 = (f32[8,128]{1,0:T(8,128)S(1)}, f32[8,128]{1,0:T(8,128)S(1)}, u32[]{:S(2)}, u32[]{:S(2)}) collective-permute-start(f32[8,128]{1,0:T(8,128)S(1)} %reduce_sum.9.own_ref), channel_id=1, source_target_pairs={{0,3},{1,0},{2,1},{3,2},{4,7},{5,4},{6,5},{7,6},{8,11},{9,8},{10,9... | collective-permute-start | bytes 12296 | tf_op jit(solution)/shard_map/ppermute | solution.py:836
  341.7 7.7 %collective-permute-start.14 = (f32[8,128]{1,0:T(8,128)S(1)}, f32[8,128]{1,0:T(8,128)S(1)}, u32[]{:S(2)}, u32[]{:S(2)}) collective-permute-start(f32[8,128]{1,0:T(8,128)S(1)} %reduce_sum.9.own_ref), channel_id=1, source_target_pairs={{0,2},{1,3},{2,0},{3,1},{4,6},{5,7},{6,4},{7,5},{8,10},{9,11},{10,... | collective-permute-start | bytes 12296 | tf_op jit(solution)/shard_map/ppermute | solution.py:836
  343.9 5.5 %collective-permute-start.13 = (f32[8,128]{1,0:T(8,128)S(1)}, f32[8,128]{1,0:T(8,128)S(1)}, u32[]{:S(2)}, u32[]{:S(2)}) collective-permute-start(f32[8,128]{1,0:T(8,128)S(1)} %reduce_sum.9.own_ref), channel_id=1, source_target_pairs={{0,1},{1,2},{2,3},{3,0},{4,5},{5,6},{6,7},{7,4},{8,9},{9,10},{10,1... | collective-permute-start | bytes 12296 | tf_op jit(solution)/shard_map/ppermute | solution.py:836

commit v5 on v4

--- a/solution.py
+++ b/solution.py
@@ -729,11 +729,11 @@
 
 
 def basis_kernel(
-    own_ref, one_ref, two_ref, three_ref, full_ref, out_ref, factor_ref, mix, *, row_scale
+    own_ref, other_ref, full_ref, out_ref, factor_ref, mix, *, row_scale
 ):
     @pl.when(pl.program_id(0) == 0)
     def _():
-        packed = (own_ref[...] + two_ref[...]) + (one_ref[...] + three_ref[...])
+        packed = own_ref[...] + other_ref[...]
         top_lane = (lane_ids(8) & PROBES) == 0
         gram = jnp.concatenate(
             [
@@ -810,7 +810,7 @@
     return pl.pallas_call(
         functools.partial(basis_kernel, row_scale=row_scale),
         grid=(steps,),
-        in_specs=[whole_spec((8, LANES))] * 4
+        in_specs=[whole_spec((8, LANES))] * 2
         + [pl.BlockSpec((count, 2, degrees, 2 * LANES), lambda g: (g, 0, 0, 0))],
         out_specs=(
             pl.BlockSpec((count, 2, degrees, LANES), lambda g: (g, 0, 0, 0)),
@@ -915,7 +915,10 @@
     full = full_stage(images, total, level_down, lev)
     over_lat = jnp.sum(received, axis=0)
     row_scale = math.sqrt(M * K * 2 * level_local * lev_count)
-    return basis_stage([over_lat] + from_levels(over_lat), full, row_scale)
+    near = [(i, i ^ 1) for i in range(lev_count)]
+    far = [(i, lev_count - 1 - i) for i in range(lev_count)]
+    pair_sum = over_lat + lax.ppermute(over_lat, "lev", near)
+    return basis_stage([pair_sum, lax.ppermute(pair_sum, "lev", far)], full, row_scale)
 
 
 def solution(mesh):

time: 358 us -> 359 us (level)
    ppermute x12 -> x9, starting transfers between devices: 13.1 us -> 10.5 us  [from_levels(): lax.ppermute(part, 'lev', [(i, (i + k) % count) for i in range(count)])]
    ppermute x12 -> x9, waiting for transfers between devices: 21.1 us -> 21.1 us  [from_levels(): lax.ppermute(part, 'lev', [(i, (i + k) % count) for i in range(count)])]
  transfers between devices with their start and end apart: 24 -> 23, of which waited for: 11 -> 12; matrix products, arithmetic and copies ran while one was open for 1% -> 1% of each run, Pallas kernels for 26% -> 26%
where the time goes in v5:
time: 359 us; the launch traced here: 356 us
  waiting for transfers between devices  149 us (42%)
  Pallas kernels  125 us (35%)
  starting transfers between devices  63.2 us (18%)
  blocking collectives  11.8 us (3%)
  local copies, waits for them, and re-layouts  4.48 us (1%)
    all_to_all x8, waiting for transfers between devices, exchange(): lax.all_to_all(blocks, 'lat', split_axis=0, concat_axis=0, tiled=True)  121 us
    all_to_all x8, starting transfers between devices, exchange(): lax.all_to_all(blocks, 'lat', split_axis=0, concat_axis=0, tiled=True)  46.3 us
    pallas_call x2, Pallas kernels, middle_stage(): pl.pallas_call(functools.partial(middle_kernel, parity=parity), grid=(1,)...  25.3 us
    ppermute x9, waiting for transfers between devices, from_levels(): lax.ppermute(part, 'lev', [(i, (i + k) % count) for i in range(count)])  21.1 us
    pallas_call x2, Pallas kernels, grid_pass(): pl.pallas_call(functools.partial(grid_middle_kernel, coupled=coupled, mas...  19.4 us
    pallas_call x2, Pallas kernels, image_stage(): pl.pallas_call(images_kernel, grid=(steps,), in_specs=[smem_spec(), smem_...  14.4 us
    all_to_all x1, blocking collectives, exchange(): lax.all_to_all(blocks, 'lat', split_axis=0, concat_axis=0, tiled=True)  11.8 us
    pallas_call x2, Pallas kernels, grid_pass(): pl.pallas_call(functools.partial(grid_even_kernel, masked=masked_in), gri...  11.1 us
  transfers between devices with their start and end apart: 23, of which 12 were waited for; matrix products, arithmetic and copies ran while one was open for 1% of the time, Pallas kernels for 26%

profile of v5, /device:TPU:1, one launch (start us, length us, event | category | flops | bytes accessed | tf_op | source)
XLA Modules:
  0.0 356.4 jit_solution(16766058267903496285)
XLA Ops:
  0.6 5.1 %legendre_raw.1 = bf16[32,16,16,128]{3,2,1,0:T(8,128)(2,1)} custom-call(bf16[16,2,256,128]{3,2,1,0:T(8,128)(2,1)} %probes_ref.5, bf16[16,2,512,256]{3,2,1,0:T(8,128)(2,1)} %table_ref.13), custom_call_target="tpu_custom_call" | custom-call | tf_op jit(solution)/shard_map/legendre_raw/pallas_call | solution.py:153
  5.7 9.7 %all-to-all-start.1 = ((bf16[32,16,16,128]{3,2,1,0:T(8,128)(2,1)}), bf16[32,16,16,128]{3,2,1,0:T(8,128)(2,1)S(1)}, u32[]{:S(2)}, u32[]{:S(2)}) async-start(bf16[32,16,16,128]{3,2,1,0:T(8,128)(2,1)} %legendre_raw.1), calls=%async_computation.1 | async-start | bytes 4194304 | tf_op jit(solution)/shard_map/all_to_all | solution.py:830
  15.4 2.0 level_partial.1.refs_0_
  17.5 2.5 collective-permute-start.2
  20.0 0.5 collective-permute-start.1
  20.5 0.6 collective-permute-start
  21.1 9.8 %collective-permute-done.2.refs_3_ = bf16[16,64,128]{2,1,0:T(8,128)(2,1)S(1)} collective-permute-done((bf16[16,64,128]{2,1,0:T(8,128)(2,1)S(1)}, bf16[16,64,128]{2,1,0:T(8,128)(2,1)S(1)}, u32[]{:S(2)}, u32[]{:S(2)}) %collective-permute-start.2) | collective-permute-done | bytes 262176 | tf_op jit(solution)/shard_map/ppermute | solution.py:836
  30.9 4.4 %collective-permute-done.refs_1_ = bf16[16,64,128]{2,1,0:T(8,128)(2,1)S(1)} collective-permute-done((bf16[16,64,128]{2,1,0:T(8,128)(2,1)S(1)}, bf16[16,64,128]{2,1,0:T(8,128)(2,1)S(1)}, u32[]{:S(2)}, u32[]{:S(2)}) %collective-permute-start) | collective-permute-done | bytes 262176 | tf_op jit(solution)/shard_map/ppermute | solution.py:836
  35.4 5.5 %legendre_forward.1 = bf16[32,16,16,128]{3,2,1,0:T(8,128)(2,1)} custom-call(f32[16]{0:T(128)S(1)} %copy-done.5, s32[1]{0:T(128)} %bitcast.lev_ref, bf16[16,2,256,128]{3,2,1,0:T(8,128)(2,1)} %probes_ref.5, bf16[16,64,128]{2,1,0:T(8,128)(2,1)S(1)} %level_partial.1.refs_0_, bf16[16,64,128]{2,1,0:T(8,128)(2,1)S(1)} %collective-permute-done.refs_1_, ...), custom_call_target="tpu_custom_call" | custom-call | tf_op jit(solution)/shard_map/legendre_forward/pallas_call | solution.py:294
  40.9 2.9 all-to-all-done.1.x_ref
  43.8 1.4 copy-done.8
  45.2 4.6 %all-to-all-start = ((bf16[32,16,16,128]{3,2,1,0:T(8,128)(2,1)}), bf16[32,16,16,128]{3,2,1,0:T(8,128)(2,1)S(1)}, u32[]{:S(2)}, u32[]{:S(2)}) async-start(bf16[32,16,16,128]{3,2,1,0:T(8,128)(2,1)} %legendre_forward.1), calls=%async_computation | async-start | bytes 4194304 | tf_op jit(solution)/shard_map/all_to_all | solution.py:830
  49.8 3.5 grid_sum.1
  53.3 1.2 collective-permute-start.3
  54.5 1.8 collective-permute-start.5
  56.3 4.8 %collective-permute-done.3 = bf16[32,2,16,128]{3,2,1,0:T(8,128)(2,1)S(1)} collective-permute-done((bf16[32,2,16,128]{3,2,1,0:T(8,128)(2,1)S(1)}, bf16[32,2,16,128]{3,2,1,0:T(8,128)(2,1)S(1)}, u32[]{:S(2)}, u32[]{:S(2)}) %collective-permute-start.3) | collective-permute-done | bytes 262176 | tf_op jit(solution)/shard_map/ppermute | solution.py:842
  61.1 0.1 add_convert_fusion.1.refs_0_
  61.1 2.3 collective-permute-start.4
  63.4 0.8 add_convert_fusion.refs_2_
  64.2 1.4 multiply_convert_fusion
  65.6 0.2 copy.15
  65.9 0.1 convert_element_type.36.gain_ref
  66.0 5.0 %spread_gain.1.refs_1_.refs_0_ = bf16[2,8,1024,128]{3,2,1,0:T(8,128)(2,1)} custom-call(bf16[2,8,8,1024]{3,2,1,0:T(8,128)(2,1)S(1)} %convert_element_type.36.gain_ref, bf16[8,128]{1,0:T(8,128)(2,1)S(1)} %copy-done.6), custom_call_target="tpu_custom_call" | custom-call | tf_op jit(solution)/shard_map/spread_gain/pallas_call | solution.py:421
  71.0 5.7 %grid_even.2.even_ref = bf16[4,2,512,256]{3,2,1,0:T(8,128)(2,1)} custom-call(s32[16]{0:T(128)S(1)} %copy-done.3, bf16[32,16,16,128]{3,2,1,0:T(8,128)(2,1)} %copy-done.8, bf16[2,512,512]{2,1,0:T(8,128)(2,1)} %constant.26.clone.table_ref.refs_4_.refs_2_.refs_1_), custom_call_target="tpu_custom_call" | custom-call | tf_op jit(solution)/shard_map/grid_even/pallas_call | solution.py:446
  76.8 2.7 grid_total.1.refs_0_
  79.5 10.1 %grid_middle.2 = (bf16[32,16,16,128]{3,2,1,0:T(8,128)(2,1)}, bf16[4,2,512,256]{3,2,1,0:T(8,128)(2,1)}) custom-call(s32[16]{0:T(128)S(1)} %copy-done.3, f32[16]{0:T(128)S(1)} %copy-done.5, s32[1]{0:T(128)} %bitcast.lev_ref, bf16[32,16,16,128]{3,2,1,0:T(8,128)(2,1)S(1)} %all-to-all-done.x_ref, bf16[4,2,512,256]{3,2,1,0:T(8,128)(2,1)} %grid_even.2.even_ref, ...), custom_call_target="tpu_custom_call" | custom-call | tf_op jit(solution)/shard_map/grid_middle/pallas_call | solution.py:459
  89.5 8.8 %all-to-all-start.4 = ((bf16[32,16,16,128]{3,2,1,0:T(8,128)(2,1)}), bf16[32,16,16,128]{3,2,1,0:T(8,128)(2,1)S(1)}, u32[]{:S(2)}, u32[]{:S(2)}) async-start(bf16[32,16,16,128]{3,2,1,0:T(8,128)(2,1)} %get-tuple-element.19), calls=%async_computation.4 | async-start | bytes 4194304 | tf_op jit(solution)/shard_map/all_to_all | solution.py:830
  98.4 5.2 %grid_odd.2 = bf16[32,16,16,128]{3,2,1,0:T(8,128)(2,1)} custom-call(s32[16]{0:T(128)S(1)} %copy-done.3, bf16[4,2,512,256]{3,2,1,0:T(8,128)(2,1)} %get-tuple-element.18.odd_ref, bf16[2,512,512]{2,1,0:T(8,128)(2,1)} %constant.27.clone.refs_3_.table_ref.refs_2_), custom_call_target="tpu_custom_call" | custom-call | tf_op jit(solution)/shard_map/grid_odd/pallas_call | solution.py:491
  103.6 23.1 %all-to-all-done.4.x_ref = bf16[32,16,16,128]{3,2,1,0:T(8,128)(2,1)S(1)} async-done(((bf16[32,16,16,128]{3,2,1,0:T(8,128)(2,1)}), bf16[32,16,16,128]{3,2,1,0:T(8,128)(2,1)S(1)}, u32[]{:S(2)}, u32[]{:S(2)}) %all-to-all-start.4) | async-done | bytes 2097184 | tf_op jit(solution)/shard_map/all_to_all | solution.py:830
  126.7 5.2 %all-to-all-start.2 = ((bf16[32,16,16,128]{3,2,1,0:T(8,128)(2,1)}), bf16[32,16,16,128]{3,2,1,0:T(8,128)(2,1)}, u32[]{:S(2)}, u32[]{:S(2)}) async-start(bf16[32,16,16,128]{3,2,1,0:T(8,128)(2,1)} %grid_odd.2), calls=%async_computation.2 | async-start | bytes 4194304 | tf_op jit(solution)/shard_map/all_to_all | solution.py:830
  131.9 12.3 %middle_stage.3 = bf16[32,16,16,128]{3,2,1,0:T(8,128)(2,1)} custom-call(s32[1]{0:T(128)} %bitcast.1.first_ref, f32[16]{0:T(128)S(1)} %copy-done.7, s32[1]{0:T(128)} %bitcast.lev_ref, bf16[32,16,16,128]{3,2,1,0:T(8,128)(2,1)S(1)} %all-to-all-done.4.x_ref, bf16[16,2,512,256]{3,2,1,0:T(8,128)(2,1)} %table_ref.13), custom_call_target="tpu_custom_call" | custom-call | tf_op jit(solution)/shard_map/middle_stage/pallas_call | solution.py:555
  144.2 16.1 %all-to-all-done.2.x_ref = bf16[32,16,16,128]{3,2,1,0:T(8,128)(2,1)} async-done(((bf16[32,16,16,128]{3,2,1,0:T(8,128)(2,1)}), bf16[32,16,16,128]{3,2,1,0:T(8,128)(2,1)}, u32[]{:S(2)}, u32[]{:S(2)}) %all-to-all-start.2) | async-done | bytes 2097184 | tf_op jit(solution)/shard_map/all_to_all | solution.py:830
  160.3 4.5 %all-to-all-start.5 = ((bf16[32,16,16,128]{3,2,1,0:T(8,128)(2,1)}), bf16[32,16,16,128]{3,2,1,0:T(8,128)(2,1)S(1)}, u32[]{:S(2)}, u32[]{:S(2)}) async-start(bf16[32,16,16,128]{3,2,1,0:T(8,128)(2,1)} %middle_stage.3), calls=%async_computation.5 | async-start | bytes 4194304 | tf_op jit(solution)/shard_map/all_to_all | solution.py:830
  164.8 13.0 %middle_stage.2 = bf16[32,16,16,128]{3,2,1,0:T(8,128)(2,1)} custom-call(s32[1]{0:T(128)} %bitcast.1.first_ref, f32[16]{0:T(128)S(1)} %copy-done.7, s32[1]{0:T(128)} %bitcast.lev_ref, bf16[32,16,16,128]{3,2,1,0:T(8,128)(2,1)} %all-to-all-done.2.x_ref, bf16[16,2,512,256]{3,2,1,0:T(8,128)(2,1)} %table_ref.13), custom_call_target="tpu_custom_call" | custom-call | tf_op jit(solution)/shard_map/middle_stage/pallas_call | solution.py:555
  177.8 15.5 %all-to-all-done.5.x_ref = bf16[32,16,16,128]{3,2,1,0:T(8,128)(2,1)S(1)} async-done(((bf16[32,16,16,128]{3,2,1,0:T(8,128)(2,1)}), bf16[32,16,16,128]{3,2,1,0:T(8,128)(2,1)S(1)}, u32[]{:S(2)}, u32[]{:S(2)}) %all-to-all-start.5) | async-done | bytes 2097184 | tf_op jit(solution)/shard_map/all_to_all | solution.py:830
  193.3 1.4 copy-done.9
  194.7 4.5 %all-to-all-start.3 = ((bf16[32,16,16,128]{3,2,1,0:T(8,128)(2,1)}), bf16[32,16,16,128]{3,2,1,0:T(8,128)(2,1)S(1)}, u32[]{:S(2)}, u32[]{:S(2)}) async-start(bf16[32,16,16,128]{3,2,1,0:T(8,128)(2,1)} %middle_stage.2), calls=%async_computation.3 | async-start | bytes 4194304 | tf_op jit(solution)/shard_map/all_to_all | solution.py:830
  199.2 5.4 %grid_even.3.even_ref = bf16[4,2,512,256]{3,2,1,0:T(8,128)(2,1)} custom-call(s32[16]{0:T(128)S(1)} %copy-done.3, bf16[32,16,16,128]{3,2,1,0:T(8,128)(2,1)} %copy-done.9, bf16[2,512,512]{2,1,0:T(8,128)(2,1)} %constant.26.clone.table_ref.refs_4_.refs_2_.refs_1_), custom_call_target="tpu_custom_call" | custom-call | tf_op jit(solution)/shard_map/grid_even/pallas_call | solution.py:446
  204.5 23.1 %all-to-all-done.3.x_ref = bf16[32,16,16,128]{3,2,1,0:T(8,128)(2,1)S(1)} async-done(((bf16[32,16,16,128]{3,2,1,0:T(8,128)(2,1)}), bf16[32,16,16,128]{3,2,1,0:T(8,128)(2,1)S(1)}, u32[]{:S(2)}, u32[]{:S(2)}) %all-to-all-start.3) | async-done | bytes 2097184 | tf_op jit(solution)/shard_map/all_to_all | solution.py:830
  227.6 9.4 %grid_middle.3 = (bf16[32,16,16,128]{3,2,1,0:T(8,128)(2,1)}, bf16[4,2,512,256]{3,2,1,0:T(8,128)(2,1)}) custom-call(s32[16]{0:T(128)S(1)} %copy-done.3, f32[16]{0:T(128)S(1)} %copy-done.5, s32[1]{0:T(128)} %bitcast.lev_ref, bf16[32,16,16,128]{3,2,1,0:T(8,128)(2,1)S(1)} %all-to-all-done.3.x_ref, bf16[4,2,512,256]{3,2,1,0:T(8,128)(2,1)} %grid_even.3.even_ref, ...), custom_call_target="tpu_custom_call" | custom-call | tf_op jit(solution)/shard_map/grid_middle/pallas_call | solution.py:459
  237.0 4.5 %all-to-all-start.6 = ((bf16[32,16,16,128]{3,2,1,0:T(8,128)(2,1)}), bf16[32,16,16,128]{3,2,1,0:T(8,128)(2,1)S(1)}, u32[]{:S(2)}, u32[]{:S(2)}) async-start(bf16[32,16,16,128]{3,2,1,0:T(8,128)(2,1)} %get-tuple-element.20), calls=%async_computation.6 | async-start | bytes 4194304 | tf_op jit(solution)/shard_map/all_to_all | solution.py:830
  241.5 5.4 %grid_odd.3 = bf16[32,16,16,128]{3,2,1,0:T(8,128)(2,1)} custom-call(s32[16]{0:T(128)S(1)} %copy-done.3, bf16[4,2,512,256]{3,2,1,0:T(8,128)(2,1)} %get-tuple-element.22.odd_ref, bf16[2,512,512]{2,1,0:T(8,128)(2,1)} %constant.27.clone.refs_3_.table_ref.refs_2_), custom_call_target="tpu_custom_call" | custom-call | tf_op jit(solution)/shard_map/grid_odd/pallas_call | solution.py:491
  246.9 23.0 %all-to-all-done.6.x_ref = bf16[32,16,16,128]{3,2,1,0:T(8,128)(2,1)S(1)} async-done(((bf16[32,16,16,128]{3,2,1,0:T(8,128)(2,1)}), bf16[32,16,16,128]{3,2,1,0:T(8,128)(2,1)S(1)}, u32[]{:S(2)}, u32[]{:S(2)}) %all-to-all-start.6) | async-done | bytes 2097184 | tf_op jit(solution)/shard_map/all_to_all | solution.py:830
  269.9 1.3 copy-done.10
  271.2 4.5 %all-to-all-start.7 = ((bf16[32,16,16,128]{3,2,1,0:T(8,128)(2,1)}), bf16[32,16,16,128]{3,2,1,0:T(8,128)(2,1)S(1)}, u32[]{:S(2)}, u32[]{:S(2)}) async-start(bf16[32,16,16,128]{3,2,1,0:T(8,128)(2,1)} %grid_odd.3), calls=%async_computation.7 | async-start | bytes 4194304 | tf_op jit(solution)/shard_map/all_to_all | solution.py:830
  275.7 7.6 %image_stage.2 = (bf16[16,256,256]{2,1,0:T(8,128)(2,1)}, bf16[16,64,128]{2,1,0:T(8,128)(2,1)S(1)}, bf16[16,64,256]{2,1,0:T(8,128)(2,1)}) custom-call(f32[16]{0:T(128)S(1)} %copy-done.5, f32[16]{0:T(128)S(1)} %copy-done.4, s32[1]{0:T(128)} %bitcast.lev_ref, bf16[32,16,16,128]{3,2,1,0:T(8,128)(2,1)} %copy-done.10, bf16[16,2,512,256]{3,2,1,0:T(8,128)(2,1)} %table_ref.13), custom_call_target="tpu_custom_call" | custom-call | tf_op jit(solution)/shard_map/image_stage/pallas_call | solution.py:612
  283.3 1.1 collective-permute-start.9
  284.4 2.2 collective-permute-start.8
  286.6 0.1 collective-permute-start.7
  286.7 17.4 %all-to-all-done.7.x_ref = bf16[32,16,16,128]{3,2,1,0:T(8,128)(2,1)S(1)} async-done(((bf16[32,16,16,128]{3,2,1,0:T(8,128)(2,1)}), bf16[32,16,16,128]{3,2,1,0:T(8,128)(2,1)S(1)}, u32[]{:S(2)}, u32[]{:S(2)}) %all-to-all-start.7) | async-done | bytes 2097184 | tf_op jit(solution)/shard_map/all_to_all | solution.py:830
  304.1 6.8 %image_stage.3 = (bf16[16,256,256]{2,1,0:T(8,128)(2,1)}, bf16[16,64,128]{2,1,0:T(8,128)(2,1)S(1)}, bf16[16,64,256]{2,1,0:T(8,128)(2,1)}) custom-call(f32[16]{0:T(128)S(1)} %copy-done.5, f32[16]{0:T(128)S(1)} %copy-done.4, s32[1]{0:T(128)} %bitcast.lev_ref, bf16[32,16,16,128]{3,2,1,0:T(8,128)(2,1)S(1)} %all-to-all-done.7.x_ref, ...), custom_call_target="tpu_custom_call" | custom-call | tf_op jit(solution)/shard_map/image_stage/pallas_call | solution.py:612
  311.0 1.1 collective-permute-start.12
  312.1 2.2 collective-permute-start.11
  314.3 0.1 collective-permute-start.10
  314.4 3.1 gram_stage.2.refs_0_
  317.5 3.0 gram_stage.3.refs_1_
  320.6 6.9 %collective-permute-done.10.refs_9_ = bf16[16,64,128]{2,1,0:T(8,128)(2,1)S(1)} collective-permute-done((bf16[16,64,128]{2,1,0:T(8,128)(2,1)S(1)}, bf16[16,64,128]{2,1,0:T(8,128)(2,1)S(1)}, u32[]{:S(2)}, u32[]{:S(2)}) %collective-permute-start.10) | collective-permute-done | bytes 262176 | tf_op jit(solution)/shard_map/ppermute | solution.py:836
  327.4 2.0 finish_stage.1
  329.4 11.8 %all_to_all.45 = f32[32,8,128]{2,1,0:T(8,128)S(1)} all-to-all(f32[32,8,128]{2,1,0:T(8,128)} %get-tuple-element.28), channel_id=1, replica_groups=mesh['lat'=32,'lev'=4] {'lat'}, dimensions={0} | all-to-all | bytes 262144 | tf_op jit(solution)/shard_map/all_to_all | solution.py:830
  341.3 0.8 collective-permute-start.13
  342.1 1.7 collective-permute-done.13
  343.8 0.3 collective-permute-start.14
  344.1 5.4 %full_stage.1.full_ref = bf16[16,2,256,256]{3,2,1,0:T(8,128)(2,1)} custom-call(f32[16]{0:T(128)S(1)} %copy-done.4, s32[1]{0:T(128)} %bitcast.lev_ref, bf16[16,256,256]{2,1,0:T(8,128)(2,1)} %get-tuple-element.21.image_ref.even_ref, bf16[16,256,256]{2,1,0:T(8,128)(2,1)} %get-tuple-element.23.image_ref.odd_ref, bf16[2,16,64,128]{3,2,1,0:T(8,128)(2,1)} %get-tuple-element.29.total_ref), custom_call_target="tpu_custom_call" | custom-call | tf_op jit(solution)/shard_map/full_stage/pallas_call | solution.py:789
  349.6 6.8 %basis_stage.1 = (bf16[16,2,256,128]{3,2,1,0:T(8,128)(2,1)}, f32[16,16]{1,0:T(8,128)}) custom-call(f32[8,128]{1,0:T(8,128)S(1)} %add.15.own_ref, f32[8,128]{1,0:T(8,128)S(1)} %collective-permute-done.14.other_ref, bf16[16,2,256,256]{3,2,1,0:T(8,128)(2,1)} %full_stage.1.full_ref), custom_call_target="tpu_custom_call" | custom-call | tf_op jit(solution)/shard_map/basis_stage/pallas_call | solution.py:810
  (36 shorter events, 0.1 us)
Async XLA Ops:
  5.7 9.8 %copy-start.4 = (f32[16]{0:T(128)S(1)}, f32[16]{0:T(128)}, u32[]{:S(2)}) copy-start(f32[16]{0:T(128)} %down_ref.7) | copy-start | bytes 196
  5.7 38.1 %all-to-all-start.1 = ((bf16[32,16,16,128]{3,2,1,0:T(8,128)(2,1)}), bf16[32,16,16,128]{3,2,1,0:T(8,128)(2,1)S(1)}, u32[]{:S(2)}, u32[]{:S(2)}) async-start(bf16[32,16,16,128]{3,2,1,0:T(8,128)(2,1)} %legendre_raw.1), calls=%async_computation.1 | async-start | bytes 4194304 | tf_op jit(solution)/shard_map/all_to_all | solution.py:830
  15.4 19.9 %copy-start.5 = (f32[16]{0:T(128)S(1)}, f32[16]{0:T(128)}, u32[]{:S(2)}) copy-start(f32[16]{0:T(128)} %up_ref.3) | copy-start | bytes 196
  17.5 13.5 %collective-permute-start.2 = (bf16[16,64,128]{2,1,0:T(8,128)(2,1)S(1)}, bf16[16,64,128]{2,1,0:T(8,128)(2,1)S(1)}, u32[]{:S(2)}, u32[]{:S(2)}) collective-permute-start(bf16[16,64,128]{2,1,0:T(8,128)(2,1)S(1)} %level_partial.1.refs_0_), channel_id=1, source_target_pairs={{0,3},{1,0},{2,1},{3,2},{4,7},{5,4},{6,5},{7,6},{8,11},{9,8},{10,9... | collective-permute-start | bytes 786440 | tf_op jit(solution)/shard_map/ppermute | solution.py:836
  20.0 10.9 %collective-permute-start.1 = (bf16[16,64,128]{2,1,0:T(8,128)(2,1)S(1)}, bf16[16,64,128]{2,1,0:T(8,128)(2,1)S(1)}, u32[]{:S(2)}, u32[]{:S(2)}) collective-permute-start(bf16[16,64,128]{2,1,0:T(8,128)(2,1)S(1)} %level_partial.1.refs_0_), channel_id=1, source_target_pairs={{0,2},{1,3},{2,0},{3,1},{4,6},{5,7},{6,4},{7,5},{8,10},{9,11},{10,... | collective-permute-start | bytes 786440 | tf_op jit(solution)/shard_map/ppermute | solution.py:836
  20.5 14.8 %collective-permute-start = (bf16[16,64,128]{2,1,0:T(8,128)(2,1)S(1)}, bf16[16,64,128]{2,1,0:T(8,128)(2,1)S(1)}, u32[]{:S(2)}, u32[]{:S(2)}) collective-permute-start(bf16[16,64,128]{2,1,0:T(8,128)(2,1)S(1)} %level_partial.1.refs_0_), channel_id=1, source_target_pairs={{0,1},{1,2},{2,3},{3,0},{4,5},{5,6},{6,7},{7,4},{8,9},{9,10},{10,1... | collective-permute-start | bytes 786440 | tf_op jit(solution)/shard_map/ppermute | solution.py:836
  43.8 1.4 copy-start.8
  45.2 34.3 %all-to-all-start = ((bf16[32,16,16,128]{3,2,1,0:T(8,128)(2,1)}), bf16[32,16,16,128]{3,2,1,0:T(8,128)(2,1)S(1)}, u32[]{:S(2)}, u32[]{:S(2)}) async-start(bf16[32,16,16,128]{3,2,1,0:T(8,128)(2,1)} %legendre_forward.1), calls=%async_computation | async-start | bytes 4194304 | tf_op jit(solution)/shard_map/all_to_all | solution.py:830
  49.8 14.4 %copy-start.11 = (f32[16]{0:T(128)S(1)}, f32[16]{0:T(128)}, u32[]{:S(2)}) copy-start(f32[16]{0:T(128)} %param.13) | copy-start | bytes 196
  53.3 12.6 %copy-start.6 = (bf16[8,128]{1,0:T(8,128)(2,1)S(1)}, bf16[8,128]{1,0:T(8,128)(2,1)}, u32[]{:S(2)}) copy-start(bf16[8,128]{1,0:T(8,128)(2,1)} %constant.28.clone.spread_ref) | copy-start | bytes 6148
  53.3 7.7 %collective-permute-start.3 = (bf16[32,2,16,128]{3,2,1,0:T(8,128)(2,1)S(1)}, bf16[32,2,16,128]{3,2,1,0:T(8,128)(2,1)S(1)}, u32[]{:S(2)}, u32[]{:S(2)}) collective-permute-start(bf16[32,2,16,128]{3,2,1,0:T(8,128)(2,1)S(1)} %get-tuple-element.16), channel_id=1, source_target_pairs={{0,1},{1,0},{2,3},{3,2},{4,5},{5,4},{6,7},{7,6},{8,9},{9,8},{10,11... | collective-permute-start | bytes 786440 | tf_op jit(solution)/shard_map/ppermute | solution.py:842
  54.5 8.9 %collective-permute-start.5 = (bf16[32,2,16,128]{3,2,1,0:T(8,128)(2,1)S(1)}, bf16[32,2,16,128]{3,2,1,0:T(8,128)(2,1)S(1)}, u32[]{:S(2)}, u32[]{:S(2)}) collective-permute-start(bf16[32,2,16,128]{3,2,1,0:T(8,128)(2,1)S(1)} %get-tuple-element.17), channel_id=1, source_target_pairs={{0,3},{1,2},{2,1},{3,0},{4,7},{5,6},{6,5},{7,4},{8,11},{9,10},{10,... | collective-permute-start | bytes 786440 | tf_op jit(solution)/shard_map/ppermute | solution.py:842
  61.1 15.6 %collective-permute-start.4 = (bf16[32,2,16,128]{3,2,1,0:T(8,128)(2,1)S(1)}, bf16[32,2,16,128]{3,2,1,0:T(8,128)(2,1)}, u32[]{:S(2)}, u32[]{:S(2)}) collective-permute-start(bf16[32,2,16,128]{3,2,1,0:T(8,128)(2,1)S(1)} %add_convert_fusion.1.refs_0_), channel_id=1, source_target_pairs={{0,3},{1,2},{2,1},{3,0},{4,7},{5,6},{6,5},{7,4},{8,11},{9,10},{10,... | collective-permute-start | bytes 786440 | tf_op jit(solution)/shard_map/ppermute | solution.py:885
  64.2 12.5 %collective-permute-start.6 = (bf16[32,2,16,128]{3,2,1,0:T(8,128)(2,1)}, bf16[32,2,16,128]{3,2,1,0:T(8,128)(2,1)}, u32[]{:S(2)}, u32[]{:S(2)}) collective-permute-start(bf16[32,2,16,128]{3,2,1,0:T(8,128)(2,1)} %add_convert_fusion.refs_2_), channel_id=1, source_target_pairs={{0,1},{1,0},{2,3},{3,2},{4,5},{5,4},{6,7},{7,6},{8,9},{9,8},{10,11... | collective-permute-start | bytes 786440 | tf_op jit(solution)/shard_map/ppermute | solution.py:887
  66.0 5.0 %copy-start.3 = (s32[16]{0:T(128)S(1)}, s32[16]{0:T(128)}, u32[]{:S(2)}) copy-start(s32[16]{0:T(128)} %counts_ref.13) | copy-start | bytes 196
  71.0 5.8 %copy-start = (bf16[2,512,512]{2,1,0:T(8,128)(2,1)S(1)}, bf16[2,512,512]{2,1,0:T(8,128)(2,1)}, u32[]{:S(2)}) copy-start(bf16[2,512,512]{2,1,0:T(8,128)(2,1)} %constant.26.clone.table_ref.refs_4_.refs_2_.refs_1_) | copy-start | bytes 3145732
  89.5 37.1 %all-to-all-start.4 = ((bf16[32,16,16,128]{3,2,1,0:T(8,128)(2,1)}), bf16[32,16,16,128]{3,2,1,0:T(8,128)(2,1)S(1)}, u32[]{:S(2)}, u32[]{:S(2)}) async-start(bf16[32,16,16,128]{3,2,1,0:T(8,128)(2,1)} %get-tuple-element.19), calls=%async_computation.4 | async-start | bytes 4194304 | tf_op jit(solution)/shard_map/all_to_all | solution.py:830
  103.6 28.3 %copy-start.7 = (f32[16]{0:T(128)S(1)}, f32[16]{0:T(128)}, u32[]{:S(2)}) copy-start(f32[16]{0:T(128)} %visc_ref.3) | copy-start | bytes 196
  126.7 33.6 %all-to-all-start.2 = ((bf16[32,16,16,128]{3,2,1,0:T(8,128)(2,1)}), bf16[32,16,16,128]{3,2,1,0:T(8,128)(2,1)}, u32[]{:S(2)}, u32[]{:S(2)}) async-start(bf16[32,16,16,128]{3,2,1,0:T(8,128)(2,1)} %grid_odd.2), calls=%async_computation.2 | async-start | bytes 4194304 | tf_op jit(solution)/shard_map/all_to_all | solution.py:830
  160.3 32.9 %all-to-all-start.5 = ((bf16[32,16,16,128]{3,2,1,0:T(8,128)(2,1)}), bf16[32,16,16,128]{3,2,1,0:T(8,128)(2,1)S(1)}, u32[]{:S(2)}, u32[]{:S(2)}) async-start(bf16[32,16,16,128]{3,2,1,0:T(8,128)(2,1)} %middle_stage.3), calls=%async_computation.5 | async-start | bytes 4194304 | tf_op jit(solution)/shard_map/all_to_all | solution.py:830
  193.3 1.4 copy-start.9
  194.7 32.9 %all-to-all-start.3 = ((bf16[32,16,16,128]{3,2,1,0:T(8,128)(2,1)}), bf16[32,16,16,128]{3,2,1,0:T(8,128)(2,1)S(1)}, u32[]{:S(2)}, u32[]{:S(2)}) async-start(bf16[32,16,16,128]{3,2,1,0:T(8,128)(2,1)} %middle_stage.2), calls=%async_computation.3 | async-start | bytes 4194304 | tf_op jit(solution)/shard_map/all_to_all | solution.py:830
  237.0 32.9 %all-to-all-start.6 = ((bf16[32,16,16,128]{3,2,1,0:T(8,128)(2,1)}), bf16[32,16,16,128]{3,2,1,0:T(8,128)(2,1)S(1)}, u32[]{:S(2)}, u32[]{:S(2)}) async-start(bf16[32,16,16,128]{3,2,1,0:T(8,128)(2,1)} %get-tuple-element.20), calls=%async_computation.6 | async-start | bytes 4194304 | tf_op jit(solution)/shard_map/all_to_all | solution.py:830
  269.9 1.3 copy-start.10
  271.2 32.9 %all-to-all-start.7 = ((bf16[32,16,16,128]{3,2,1,0:T(8,128)(2,1)}), bf16[32,16,16,128]{3,2,1,0:T(8,128)(2,1)S(1)}, u32[]{:S(2)}, u32[]{:S(2)}) async-start(bf16[32,16,16,128]{3,2,1,0:T(8,128)(2,1)} %grid_odd.3), calls=%async_computation.7 | async-start | bytes 4194304 | tf_op jit(solution)/shard_map/all_to_all | solution.py:830
  283.3 31.0 %collective-permute-start.9 = (bf16[16,64,128]{2,1,0:T(8,128)(2,1)S(1)}, bf16[16,64,128]{2,1,0:T(8,128)(2,1)S(1)}, u32[]{:S(2)}, u32[]{:S(2)}) collective-permute-start(bf16[16,64,128]{2,1,0:T(8,128)(2,1)S(1)} %get-tuple-element.26.refs_4_), channel_id=1, source_target_pairs={{0,3},{1,0},{2,1},{3,2},{4,7},{5,4},{6,5},{7,6},{8,11},{9,8},{10,9... | collective-permute-start | bytes 786440 | tf_op jit(solution)/shard_map/ppermute | solution.py:836
  284.4 36.1 %collective-permute-start.8 = (bf16[16,64,128]{2,1,0:T(8,128)(2,1)S(1)}, bf16[16,64,128]{2,1,0:T(8,128)(2,1)S(1)}, u32[]{:S(2)}, u32[]{:S(2)}) collective-permute-start(bf16[16,64,128]{2,1,0:T(8,128)(2,1)S(1)} %get-tuple-element.26.refs_4_), channel_id=1, source_target_pairs={{0,2},{1,3},{2,0},{3,1},{4,6},{5,7},{6,4},{7,5},{8,10},{9,11},{10,... | collective-permute-start | bytes 786440 | tf_op jit(solution)/shard_map/ppermute | solution.py:836
  286.6 33.9 %collective-permute-start.7 = (bf16[16,64,128]{2,1,0:T(8,128)(2,1)S(1)}, bf16[16,64,128]{2,1,0:T(8,128)(2,1)S(1)}, u32[]{:S(2)}, u32[]{:S(2)}) collective-permute-start(bf16[16,64,128]{2,1,0:T(8,128)(2,1)S(1)} %get-tuple-element.26.refs_4_), channel_id=1, source_target_pairs={{0,1},{1,2},{2,3},{3,0},{4,5},{5,6},{6,7},{7,4},{8,9},{9,10},{10,1... | collective-permute-start | bytes 786440 | tf_op jit(solution)/shard_map/ppermute | solution.py:836
  311.0 9.6 %collective-permute-start.12 = (bf16[16,64,128]{2,1,0:T(8,128)(2,1)S(1)}, bf16[16,64,128]{2,1,0:T(8,128)(2,1)S(1)}, u32[]{:S(2)}, u32[]{:S(2)}) collective-permute-start(bf16[16,64,128]{2,1,0:T(8,128)(2,1)S(1)} %get-tuple-element.27.refs_8_), channel_id=1, source_target_pairs={{0,3},{1,0},{2,1},{3,2},{4,7},{5,4},{6,5},{7,6},{8,11},{9,8},{10,9... | collective-permute-start | bytes 786440 | tf_op jit(solution)/shard_map/ppermute | solution.py:836
  312.1 8.5 %collective-permute-start.11 = (bf16[16,64,128]{2,1,0:T(8,128)(2,1)S(1)}, bf16[16,64,128]{2,1,0:T(8,128)(2,1)S(1)}, u32[]{:S(2)}, u32[]{:S(2)}) collective-permute-start(bf16[16,64,128]{2,1,0:T(8,128)(2,1)S(1)} %get-tuple-element.27.refs_8_), channel_id=1, source_target_pairs={{0,2},{1,3},{2,0},{3,1},{4,6},{5,7},{6,4},{7,5},{8,10},{9,11},{10,... | collective-permute-start | bytes 786440 | tf_op jit(solution)/shard_map/ppermute | solution.py:836
  314.3 13.1 %collective-permute-start.10 = (bf16[16,64,128]{2,1,0:T(8,128)(2,1)S(1)}, bf16[16,64,128]{2,1,0:T(8,128)(2,1)S(1)}, u32[]{:S(2)}, u32[]{:S(2)}) collective-permute-start(bf16[16,64,128]{2,1,0:T(8,128)(2,1)S(1)} %get-tuple-element.27.refs_8_), channel_id=1, source_target_pairs={{0,1},{1,2},{2,3},{3,0},{4,5},{5,6},{6,7},{7,4},{8,9},{9,10},{10,1... | collective-permute-start | bytes 786440 | tf_op jit(solution)/shard_map/ppermute | solution.py:836
  314.4 13.0 %copy-start.1 = (bf16[16,64,256]{2,1,0:T(8,128)(2,1)S(1)}, bf16[16,64,256]{2,1,0:T(8,128)(2,1)}, u32[]{:S(2)}) copy-start(bf16[16,64,256]{2,1,0:T(8,128)(2,1)} %get-tuple-element.24.refs_2_) | copy-start | bytes 1572868
  314.4 13.0 %copy-start.2 = (bf16[16,64,256]{2,1,0:T(8,128)(2,1)S(1)}, bf16[16,64,256]{2,1,0:T(8,128)(2,1)}, u32[]{:S(2)}) copy-start(bf16[16,64,256]{2,1,0:T(8,128)(2,1)} %get-tuple-element.25.refs_3_) | copy-start | bytes 1572868
  341.3 2.5 collective-permute-start.13
  343.8 5.8 %collective-permute-start.14 = (f32[8,128]{1,0:T(8,128)S(1)}, f32[8,128]{1,0:T(8,128)S(1)}, u32[]{:S(2)}, u32[]{:S(2)}) collective-permute-start(f32[8,128]{1,0:T(8,128)S(1)} %add.15.own_ref), channel_id=1, source_target_pairs={{0,3},{1,2},{2,1},{3,0},{4,7},{5,6},{6,5},{7,4},{8,11},{9,10},{10,... | collective-permute-start | bytes 12296 | tf_op jit(solution)/shard_map/ppermute | solution.py:921
